TPU v7x, 32 devices: a whole 2x2x4 slice. The times are simulated.
32 devices in a mesh: trades: 8 (over y, x, core), paths: 4 (over z).
Axes of the slice: x: 2, y: 2, z: 4, core: 2. Of those that a mesh axis runs over, the one named last changes fastest.
Arguments:
- path_states: bfloat16 [2, 1024, 512], P(None, 'paths'), may hold values from -6 to 6
- trade_loads: bfloat16 [4096, 512], P('trades'), may hold values from -0.25 to 0.25
- trade_amounts: float32 [2, 4096], P(None, 'trades'), may hold values from -6 to 6
- trade_legs: int32 [2, 4096], P(None, 'trades'), may hold values from 0 to 39
- trade_set: int32 [4096], P('trades'), may hold values from 0 to 255, as said below
- set_slot: int32 [256], replicated, may hold values from 0 to 255, as said below
- risk_weights: float32 [40], replicated, may hold values from 0.5 to 4
Outputs:
- fitted_margin: float32 [2, 256, 1024], P(None, 'trades', 'paths')
- exposure: float32 [2, 256], P(None, 'trades')
Inputs may be any that keep to these rules, and one draw needn't show every extreme that they name: `trade_set`: each row of one trade shard (aligned blocks of 512 trades) names a set; at most 160 trades of one block belong to the sets of one owner (owner = set_slot // 32), and one owner receives exactly 160 from every block. `set_slot`: A permutation of the netting sets.
All inputs are finite; a program needn't handle non-finite values.
Results may differ from a plain program's by a relative error of at most 0.0075.
Values may be sent and summed in bfloat16 or wider, within the bound.
No kernel may reach another device: no remote copies, remote signals or barrier semaphores. Data moves between devices by JAX's collectives and lax.ppermute only.
A program may use at most 64 MiB of HBM per device.

v0:
```python
import jax
import jax.numpy as jnp
from jax import lax
from jax.sharding import PartitionSpec as P

B = 40
NB = 16
DATES = 2


CORR_LEN = 8.0
IM_SCALE = 0.2
RIDGE = 0.05
VALUE_SCALE = 4.0


def price_trades(states, loadings, first_amount, second_amount):
    factor_sum = jnp.einsum("rk,dpk->rdp", loadings, states, preferred_element_type=jnp.float32)
    first_leg = first_amount[:, None, None]
    second_leg = second_amount[:, None, None]
    trade_value = first_leg * jax.nn.softplus(factor_sum) + second_leg * jax.nn.softplus(
        -factor_sum
    )
    rise_delta = first_leg * jax.nn.sigmoid(factor_sum)
    fall_delta = -second_leg * jax.nn.sigmoid(-factor_sum)
    return jnp.stack([trade_value, rise_delta, fall_delta], axis=2)


def bucket_margin(bucket_delta, weights):
    positions = jnp.arange(B).astype(jnp.float32)
    correlation = jnp.exp(-jnp.abs(positions[:, None] - positions[None, :]) / CORR_LEN)
    weighted = bucket_delta * weights[None, :, None]
    mixed = jnp.einsum("bc,scp->sbp", correlation, weighted, precision=lax.Precision.HIGHEST)
    return IM_SCALE * jnp.sqrt(1.0 + jnp.sum(weighted * mixed, axis=1))


def design(set_value, features):
    constant = jnp.ones_like(set_value)
    spread = jnp.broadcast_to(features.T[:, None, :], (NB - 2,) + set_value.shape)
    return jnp.concatenate(
        [constant[None], jnp.tanh(set_value / VALUE_SCALE)[None], spread], axis=0
    )


def solve_small(gram_matrix, moments):
    factor_lower = jnp.linalg.cholesky(gram_matrix)
    halfway = lax.linalg.triangular_solve(
        factor_lower, moments[..., None], left_side=True, lower=True
    )
    solved = lax.linalg.triangular_solve(
        factor_lower, halfway, left_side=True, lower=True, transpose_a=True
    )
    return solved[..., 0]


def reduce_slots(got_terms, got_tags, set_count):
    slot_count = got_terms.shape[0]
    date_count = got_terms.shape[1]
    path_count = got_terms.shape[3]
    value_cols = got_terms[:, :, 0, :].reshape(slot_count, date_count * path_count)
    rise_cols = got_terms[:, :, 1, :].reshape(slot_count, date_count * path_count)
    fall_cols = got_terms[:, :, 2, :].reshape(slot_count, date_count * path_count)
    set_tag = got_tags[:, 0]
    set_value = jax.ops.segment_sum(value_cols, set_tag, num_segments=set_count + 1)[:set_count]
    set_value = set_value.reshape(set_count, date_count, path_count)
    bucket_count = (set_count + 1) * B
    rise_sum = jax.ops.segment_sum(
        rise_cols, set_tag * B + got_tags[:, 1], num_segments=bucket_count
    )
    fall_sum = jax.ops.segment_sum(
        fall_cols, set_tag * B + got_tags[:, 2], num_segments=bucket_count
    )
    bucket_delta = (rise_sum + fall_sum)[: set_count * B]
    bucket_delta = bucket_delta.reshape(set_count, B, date_count, path_count)
    return (set_value, bucket_delta)


def on_device(
    path_states, trade_loads, trade_amounts, trade_legs, trade_set, set_slot, risk_weights
):
    owners = lax.axis_size("trades")
    row_count = trade_set.shape[0]
    set_count = set_slot.shape[0] // owners
    capacity = 5 * row_count // (2 * owners)
    paths_all = path_states.shape[1] * lax.axis_size("paths")
    set_position = set_slot[trade_set]
    owner_index = set_position // set_count
    local_index = set_position % set_count
    owner_marks = (owner_index[:, None] == jnp.arange(owners, dtype=jnp.int32)[None, :]).astype(
        jnp.int32
    )
    owner_rank = jnp.sum((jnp.cumsum(owner_marks, axis=0) - 1) * owner_marks, axis=1)
    target = owner_index * capacity + owner_rank
    trade_tags = jnp.stack([local_index, trade_legs[0], trade_legs[1]], axis=1)
    blank_tags = jnp.zeros((owners * capacity, 3), jnp.int32).at[:, 0].set(set_count)
    send_tags = blank_tags.at[target].set(trade_tags).reshape(owners, capacity, 3)
    trade_terms = price_trades(path_states, trade_loads, trade_amounts[0], trade_amounts[1])
    inner_shape = trade_terms.shape[1:]
    send_terms = (
        jnp.zeros((owners * capacity,) + inner_shape, jnp.float32).at[target].set(trade_terms)
    )
    send_terms = send_terms.reshape((owners, capacity) + inner_shape)
    got_terms, got_tags = (
        lax.all_to_all(send_terms, "trades", split_axis=0, concat_axis=0, tiled=True),
        lax.all_to_all(send_tags, "trades", split_axis=0, concat_axis=0, tiled=True),
    )
    got_terms = got_terms.reshape((owners * capacity,) + inner_shape)
    got_tags = got_tags.reshape(owners * capacity, 3)
    set_value, bucket_delta = reduce_slots(got_terms, got_tags, set_count)
    basis_list = []
    gram_list = []
    moment_list = []
    for date_index in range(DATES):
        margin = bucket_margin(bucket_delta[:, :, date_index], risk_weights)
        features = path_states[date_index][:, : NB - 2].astype(jnp.float32)
        basis_terms = design(set_value[:, date_index], features)
        basis_list.append(basis_terms)
        gram_list.append(
            jnp.einsum("isp,jsp->sij", basis_terms, basis_terms, precision=lax.Precision.HIGHEST)
        )
        moment_list.append(
            jnp.einsum("isp,sp->si", basis_terms, margin, precision=lax.Precision.HIGHEST)
        )
    gram_matrix = jnp.stack(gram_list, axis=1)
    moments = jnp.stack(moment_list, axis=1)
    ridge_term = RIDGE * paths_all * jnp.eye(NB, dtype=jnp.float32)
    gram_total, moment_total = lax.psum((gram_matrix, moments), "paths")
    coefficients = solve_small(gram_total + ridge_term, moment_total)
    fitted_list = []
    positive_list = []
    for date_index in range(DATES):
        fitted = jnp.einsum(
            "isp,si->sp",
            basis_list[date_index],
            coefficients[:, date_index],
            precision=lax.Precision.HIGHEST,
        )
        fitted_list.append(fitted)
        positive_list.append(jnp.sum(jnp.maximum(set_value[:, date_index] - fitted, 0.0), axis=1))
    positive_sum = lax.psum(jnp.stack(positive_list), "paths")
    fitted_margin = jnp.stack(fitted_list)
    exposure = positive_sum / paths_all
    return (fitted_margin, exposure)


def solution(mesh):
    in_specs = (
        P(None, "paths", None),
        P("trades", None),
        P(None, "trades"),
        P(None, "trades"),
        P("trades"),
        P(),
        P(),
    )
    out_specs = (P(None, "trades", "paths"), P(None, "trades"))
    return jax.shard_map(
        on_device, mesh=mesh, in_specs=in_specs, out_specs=out_specs, check_vma=False
    )
```

profile of v0, /device:TPU:0, one launch (start us, length us, event | category | flops | bytes accessed | tf_op | source)
XLA Modules:
  0.0 421.1 jit_solution(97807923092345413)
XLA Ops:
  7.9 3.6 gather_fusion
  12.2 1.1 reduce-window.6
  15.4 2.0 scatter_fusion
  18.5 5.2 %all-to-all-start = ((s32[8,1,480]{2,1,0:T(1,128)}), s32[8,1,480]{2,1,0:T(1,128)S(1)}, u32[]{:S(2)}, u32[]{:S(2)}) async-start(s32[8,1,480]{2,1,0:T(1,128)} %reshape.320), calls=%async_computation | async-start | bytes 32768 | tf_op jit(solution)/shard_map/all_to_all | solution.py:105
  23.7 1.9 fusion.18
  25.8 4.1 copy.87
  29.9 5.3 %broadcast_in_dim.14 = f32[1280,2,3,256]{3,1,2,0:T(2,128)} broadcast(f32[]{:T(128)} %constant.130.clone.1), dimensions={} | broadcast | bytes 7864324 | tf_op jit(solution)/shard_map/broadcast_in_dim | solution.py:100
  35.2 63.9 %scatter_fusion.1 = f32[1280,2,3,256]{3,1,2,0:T(2,128)} fusion(f32[1280,2,3,256]{3,1,2,0:T(2,128)} %broadcast_in_dim.14, s32[512]{0:T(512)S(1)} %bitcast.209, f32[512,2,3,256]{3,1,2,0:T(2,128)} %copy.87), kind=kCustom, calls=%fused_computation.2 | custom fusion | bytes 9439232 | tf_op jit(solution)/shard_map/scatter | solution.py:100
  99.2 4.9 %all-to-all-start.1 = ((f32[8,160,2,3,256]{4,2,3,1,0:T(2,128)}), f32[8,160,2,3,256]{4,2,3,1,0:T(2,128)}, u32[]{:S(2)}, u32[]{:S(2)}) async-start(f32[8,160,2,3,256]{4,2,3,1,0:T(2,128)} %bitcast.191), calls=%async_computation.1 | async-start | bytes 15728640 | tf_op jit(solution)/shard_map/all_to_all | solution.py:104
  106.4 86.1 %all-to-all-done.1 = f32[8,160,2,3,256]{4,2,3,1,0:T(2,128)} async-done(((f32[8,160,2,3,256]{4,2,3,1,0:T(2,128)}), f32[8,160,2,3,256]{4,2,3,1,0:T(2,128)}, u32[]{:S(2)}, u32[]{:S(2)}) %all-to-all-start.1) | async-done | bytes 7864352 | tf_op jit(solution)/shard_map/all_to_all | solution.py:104
  192.5 6.8 %fusion.70 = (f32[1280,2,1,256]{3,1,2,0:T(2,128)S(1)}, f32[1280,2,1,256]{3,1,2,0:T(2,128)}, f32[1280,2,1,256]{3,1,2,0:T(2,128)S(1)}) fusion(f32[1280,2,3,256]{3,1,2,0:T(2,128)} %bitcast.17), kind=kLoop, calls=%fused_computation.146 | loop fusion | bytes 15728640 | tf_op jit(solution)/shard_map/slice | solution.py:61
  199.3 1.7 copy.127
  201.0 1.7 copy.128
  202.8 11.7 %scatter_custom_fusion.3 = f32[1320,512]{1,0:T(8,128)S(1)} fusion(s32[1280]{0:T(1024)S(1)} %get-tuple-element.14, f32[1280,512]{1,0:T(8,128)} %bitcast.197, f32[]{:T(128)} %constant.130.clone.1), kind=kCustom, calls=%fused_computation.16 | custom fusion | flops 655360 | bytes 2703872 | tf_op jit(solution)/shard_map/scatter-add | solution.py:67
  214.5 12.9 %scatter_custom_fusion.4 = f32[1320,512]{1,0:T(8,128)} fusion(s32[1280]{0:T(1024)S(1)} %get-tuple-element.15, f32[1280,512]{1,0:T(8,128)} %bitcast.196, f32[]{:T(128)} %constant.130.clone.1), kind=kCustom, calls=%fused_computation.14 | custom fusion | flops 655360 | bytes 2703872 | tf_op jit(solution)/shard_map/scatter-add | solution.py:70
  227.4 3.9 slice_add_fusion
  231.3 3.3 reshape.245
  234.6 3.1 fusion.71
  237.7 1.5 fusion.10
  239.5 10.7 %scatter_custom_fusion.2 = f32[33,512]{1,0:T(8,128)S(1)} fusion(s32[1280]{0:T(1024)S(1)} %get-tuple-element.16, f32[1280,512]{1,0:T(8,128)S(1)} %bitcast.198, f32[]{:T(128)} %constant.130.clone.1), kind=kCustom, calls=%fused_computation.61 | custom fusion | flops 655360 | bytes 67588 | tf_op jit(solution)/shard_map/scatter-add | solution.py:64
  250.4 0.9 convolution_bitcast_fusion.3
  252.0 3.2 fusion.13
  255.3 0.9 convolution_bitcast_fusion.2
  256.9 0.9 pad_maximum_fusion.9
  257.8 19.5 %psum.22 = f32[32,2,16]{2,0,1:T(8,128)S(1)} all-reduce(f32[32,2,16]{2,0,1:T(8,128)S(1)} %pad_maximum_fusion.11), channel_id=1, replica_groups=mesh['trades'=8,'paths'=4] {'paths'}, use_global_device_ids=true, to_apply=%region_14.15 | all-reduce | flops 1024 | bytes 8192 | tf_op jit(solution)/shard_map/psum | solution.py:127
  277.3 19.0 %all-reduce.3.cloned.1.call-done = f32[32,2,16,16]{2,3,1,0:T(8,128)} async-done(((f32[32,2,16,16]{2,3,1,0:T(8,128)}), f32[32,2,16,16]{2,3,1,0:T(8,128)}) %all-reduce.3.cloned.1.call-update) | async-done | bytes 65552 | tf_op jit(solution)/shard_map/psum | solution.py:127
  296.3 1.1 broadcast_add_fusion
  297.6 1.1 fusion.26
  298.7 93.8 %custom-call.9 = f32[32,2,16,16]{3,2,1,0:T(8,128)S(1)} custom-call(f32[32,2,16,16]{3,2,1,0:T(8,128)S(1)} %fusion.26), custom_call_target="Cholesky" | custom-call | tf_op jit(solution)/shard_map/jit(cholesky)/cholesky | solution.py:46
  393.1 5.4 %custom-call.10 = f32[32,2,1,16,16]{0,3,4,2,1:T(8,128)S(1)} custom-call(f32[32,2,1,16,16]{0,4,3,2,1:T(8,128)S(1)} %select_bitcast_fusion), custom_call_target="InvertDiagBlocksLowerTriangular" | custom-call | tf_op jit(solution)/shard_map/triangular_solve | solution.py:50
  399.7 0.9 fusion.76
  402.0 10.8 %psum.23 = f32[2,32]{1,0:T(2,128)S(1)} all-reduce(f32[2,32]{1,0:T(2,128)S(1)} %pad_maximum_fusion.12), channel_id=1, replica_groups=mesh['trades'=8,'paths'=4] {'paths'}, use_global_device_ids=true, to_apply=%region_17.18 | all-reduce | flops 64 | bytes 512 | tf_op jit(solution)/shard_map/psum | solution.py:140
  (77 shorter events, 12.8 us)
Async XLA Ops:
  7.2 16.5 %copy-start = (bf16[512,512]{1,0:T(8,128)(2,1)S(1)}, bf16[512,512]{1,0:T(8,128)(2,1)}, u32[]{:S(2)}) copy-start(bf16[512,512]{1,0:T(8,128)(2,1)} %param.10) | copy-start | bytes 1572868
  15.4 8.3 %copy-start.3 = (f32[2,512]{1,0:T(2,128)S(1)}, f32[2,512]{1,0:T(2,128)}, u32[]{:S(2)}) copy-start(f32[2,512]{1,0:T(2,128)} %param.11) | copy-start | bytes 12292
  15.4 8.3 %copy-start.2 = (bf16[2,256,512]{2,1,0:T(8,128)(2,1)S(1)}, bf16[2,256,512]{2,1,0:T(8,128)(2,1)}, u32[]{:S(2)}) copy-start(bf16[2,256,512]{2,1,0:T(8,128)(2,1)} %param.9) | copy-start | bytes 1572868
  18.5 80.7 %all-to-all-start = ((s32[8,1,480]{2,1,0:T(1,128)}), s32[8,1,480]{2,1,0:T(1,128)S(1)}, u32[]{:S(2)}, u32[]{:S(2)}) async-start(s32[8,1,480]{2,1,0:T(1,128)} %reshape.320), calls=%async_computation | async-start | bytes 32768 | tf_op jit(solution)/shard_map/all_to_all | solution.py:105
  99.2 93.4 %all-to-all-start.1 = ((f32[8,160,2,3,256]{4,2,3,1,0:T(2,128)}), f32[8,160,2,3,256]{4,2,3,1,0:T(2,128)}, u32[]{:S(2)}, u32[]{:S(2)}) async-start(f32[8,160,2,3,256]{4,2,3,1,0:T(2,128)} %bitcast.191), calls=%async_computation.1 | async-start | bytes 15728640 | tf_op jit(solution)/shard_map/all_to_all | solution.py:104
  104.1 192.2 %all-reduce.3.cloned.1.call-start = ((), (), s32[]{:S(2)}) async-start(), calls=%async_computation.2 | async-start | bytes 1048576 | tf_op jit(solution)/shard_map/psum | solution.py:127
  234.5 3.1 copy-start.4
  234.6 4.7 %copy-start.1 = (f32[1280,2,1,256]{3,1,2,0:T(2,128)S(1)}, f32[1280,2,1,256]{3,1,2,0:T(2,128)}, u32[]{:S(2)}) copy-start(f32[1280,2,1,256]{3,1,2,0:T(2,128)} %get-tuple-element.18) | copy-start | bytes 7864324
Sparse Core Ops, SparseCore 0:
  257.9 38.3 all-reduce.2
where the time goes:
time: 429 us; the launch traced here: 421 us
  other arithmetic  147 us (34%)
  waiting for transfers between devices  105 us (24%)
  local copies, waits for them, and re-layouts  100 us (23%)
  blocking collectives  30.3 us (7%)
  between operations  15.4 us (4%)
  matrix products  12.5 us (3%)
  starting transfers between devices  10.6 us (2%)
    another operation x4, other arithmetic, solve_small(): factor_lower = jnp.linalg.cholesky(gram_matrix)  94 us
    all_to_all x1, waiting for transfers between devices, on_device(): lax.all_to_all(send_terms, 'trades', split_axis=0, concat_axis=0, tiled=T...  86.1 us
    scatter x1, local copies, waits for them, and re-layouts, on_device(): jnp.zeros((owners * capacity,) + inner_shape, jnp.float32).at[target]  63.9 us
    psum x1, blocking collectives, on_device(): gram_total, moment_total = lax.psum((gram_matrix, moments), 'paths')  19.5 us
    psum x1, waiting for transfers between devices, on_device(): gram_total, moment_total = lax.psum((gram_matrix, moments), 'paths')  19 us
    scatter-add x1, other arithmetic, reduce_slots(): jax.ops.segment_sum(fall_cols, set_tag * B + got_tags[:, 2], num_segments...  12.9 us
    scatter-add x1, other arithmetic, reduce_slots(): jax.ops.segment_sum(rise_cols, set_tag * B + got_tags[:, 1], num_segments...  11.7 us
    psum x1, blocking collectives, on_device(): positive_sum = lax.psum(jnp.stack(positive_list), 'paths')  10.8 us
  transfers between devices with their start and end apart: 3, of which 2 were waited for; matrix products, arithmetic and copies ran while one was open for 18% of the time, Pallas kernels for 0%

commit v1 on v0

v1 whole, which is shorter than its diff:
```python
import math

import jax
import jax.numpy as jnp
from jax import lax
from jax.experimental import pallas as pl
from jax.experimental.pallas import tpu as pltpu
from jax.sharding import PartitionSpec as P

B = 40
NB = 16
DATES = 2
NF = NB - 2
META = 8
HALF = 256

CORR_LEN = 8.0
IM_SCALE = 0.2
RIDGE = 0.05
VALUE_SCALE = 4.0

F32 = jnp.float32
BF16 = jnp.bfloat16
VMEM_LIMIT = 56 << 20
NT = (((1,), (1,)), ((), ()))


def iota(shape, axis):
    return lax.broadcasted_iota(jnp.int32, shape, axis)


def dot(a, b):
    return jnp.dot(a, b, preferred_element_type=F32)


def dot_nt(a, b):
    return lax.dot_general(a, b, NT, preferred_element_type=F32)


def pieces(x, count):
    out = []
    for _ in range(count):
        piece = x.astype(BF16)
        out.append(piece)
        x = x - piece.astype(F32)
    return out


def pick_rows(rows, height):
    width = rows[0].shape[1]
    at = iota((height, width), 0)
    out = jnp.zeros((height, width), F32)
    for i, row in enumerate(rows):
        out = jnp.where(at == i, row, out)
    return out


def pack_kernel(owners, cap, set_count, me_ref, set_ref, slot_ref, amount_ref, leg_ref, load_ref, *outs):
    trades = set_ref.shape[1]
    sets = slot_ref.shape[1]
    slot = slot_ref[...].astype(F32)
    slot_owner = jnp.floor((slot + 0.5) * (1.0 / set_count))
    slot_local = slot - slot_owner * set_count
    digits = pick_rows([slot_owner, slot_local], 16).astype(BF16)
    member = jnp.where(iota((sets, trades), 0) == set_ref[...], 1.0, 0.0).astype(BF16)
    found = dot(digits, member)
    owner, local = found[0:1], found[1:2]
    height = -(-owners // 16) * 16
    marks = jnp.where(iota((height, trades), 0).astype(F32) == owner, 1.0, 0.0)
    ahead = jnp.where(iota((trades, trades), 0) < iota((trades, trades), 1), 1.0, 0.0).astype(BF16)
    rank = jnp.sum(dot(marks.astype(BF16), ahead) * marks, axis=0, keepdims=True)
    target = (owner * cap + rank).astype(jnp.int32) - me_ref[0] * cap
    target = jnp.where(target < 0, target + owners * cap, target)
    amounts = amount_ref[...]
    legs = leg_ref[...].astype(F32)
    meta = [p.astype(F32) for p in pieces(amounts[0:1], 3) + pieces(amounts[1:2], 3)]
    meta = pick_rows(meta + [legs[0:1], legs[1:2], local], 16).astype(BF16)
    loads = load_ref[...]
    for k in range(owners):
        place = jnp.where(iota((HALF, trades), 0) + k * cap == target, 1.0, 0.0).astype(BF16)
        moved = dot(place[:cap], loads)
        tags = dot_nt(meta, place)
        out = outs[k] if len(outs) > 1 else outs[0].at[k]
        out[0:cap, :] = moved.astype(BF16)
        out[cap : cap + META, 0:HALF] = tags[0:META].astype(BF16)
        out[cap : cap + META, HALF : 2 * HALF] = tags[META : 2 * META].astype(BF16)


def owner_kernel(owners, cap, set_count, weight_ref, state_ref, *refs):
    blocks = refs[: -7]
    out_ref, level_ref, delta_ref, terms_ref, high_ref, low_ref, place_ref = refs[-7:]
    if len(blocks) == 1:
        blocks = [blocks[0].at[k] for k in range(owners)]
    count = owners * cap
    cols = state_ref.shape[0]
    paths = cols // DATES
    states = state_ref[...]
    meta = jnp.zeros((2 * META, count), F32)
    for k in range(owners):
        tags = jnp.concatenate(
            [blocks[k][cap : cap + META, 0:HALF], blocks[k][cap : cap + META, HALF : 2 * HALF]], axis=0
        ).astype(F32)
        tags = jnp.where(iota(tags.shape, 1) < cap, tags, 0.0)
        tags = jnp.concatenate([tags, jnp.zeros((2 * META, count - HALF), F32)], axis=1)
        meta = meta + (pltpu.roll(tags, k * cap, 1) if k else tags)
    first = meta[0:1] + meta[1:2] + meta[2:3]
    second = meta[3:4] + meta[4:5] + meta[5:6]
    columns = pick_rows([first, second], 128).T
    loads = jnp.concatenate([block[0:cap, :] for block in blocks], axis=0)
    level_ref[...] = dot_nt(loads, states)
    step = 128
    for r in range(0, count, step):
        x = level_ref[r : r + step, :]
        a = columns[r : r + step, 0:1]
        c = columns[r : r + step, 1:2]
        e = jnp.exp(-jnp.abs(x))
        more = 1.0 + e
        tail = jnp.log(more)
        near = 1.0 / more
        far = e * near
        up = x >= 0.0
        value = a * (jnp.maximum(x, 0.0) + tail) + c * (jnp.maximum(-x, 0.0) + tail)
        terms_ref[r : r + step, :] = (a * jnp.where(up, near, far)).astype(BF16)
        terms_ref[count + r : count + r + step, :] = (-c * jnp.where(up, far, near)).astype(BF16)
        high = value.astype(BF16)
        high_ref[r : r + step, :] = high
        low_ref[r : r + step, :] = (value - high.astype(F32)).astype(BF16)
    in_set = jnp.where(iota((set_count, count), 0).astype(F32) == meta[8:9], 1.0, 0.0)
    for leg in range(2):
        at_leg = meta[6 + leg : 7 + leg]
        for b in range(B):
            place_ref[b * set_count : (b + 1) * set_count, leg * count : (leg + 1) * count] = (
                jnp.where(at_leg == float(b), in_set, 0.0).astype(BF16)
            )
    delta_ref[...] = dot(place_ref[...], terms_ref[...])
    in_set = in_set.astype(BF16)
    set_value = dot(in_set, high_ref[...]) + dot(in_set, low_ref[...])
    rho = math.exp(-1.0 / CORR_LEN)
    carry = jnp.zeros((set_count, cols), F32)
    quad = jnp.zeros((set_count, cols), F32)
    for b in range(B - 1, -1, -1):
        carry = rho * carry + weight_ref[b] * delta_ref[b * set_count : (b + 1) * set_count, :]
        quad = quad + (1.0 if b == 0 else 1.0 - rho * rho) * (carry * carry)
    margin = IM_SCALE * jnp.sqrt(1.0 + quad)
    spread = jnp.tanh(set_value / VALUE_SCALE)
    eye = jnp.where(iota((NB, 128), 0) == iota((NB, 128), 1), 1.0, 0.0).astype(BF16)
    basis = dot_nt(eye, states[:, 0:128])
    at = iota(basis.shape, 0)
    basis = jnp.where(at < NF, basis, jnp.where(at == NF, 1.0, 0.0))
    for d in range(DATES):
        own = slice(d * paths, (d + 1) * paths)
        t, m = spread[:, own], margin[:, own]
        rows = jnp.concatenate([t, m, t * t, t * m], axis=0)
        some = basis[:, own].astype(BF16)
        sums = sum(dot_nt(some, piece) for piece in pieces(rows, 3))
        out_ref[d * set_count : (d + 1) * set_count, :] = set_value[:, own]
        base = DATES * set_count
        out_ref[base + d * NB : base + (d + 1) * NB, :] = basis[:, own]
        base = base + DATES * NB
        width = 4 * set_count
        out_ref[base : base + NB, d * width : (d + 1) * width] = sums


def fit_kernel(groups, set_count, *refs):
    parts, (fit_ref, pos_ref) = refs[:groups], refs[groups:]
    paths = parts[0].shape[1]
    paths_all = groups * paths
    ridge = RIDGE * paths_all
    width = 4 * set_count
    base = DATES * (set_count + NB)
    rows = []
    for d in range(DATES):
        sums = sum(p[base : base + NB, d * width : (d + 1) * width] for p in parts)
        first = DATES * set_count + d * NB
        basis = jnp.concatenate([p[first : first + NB, :] for p in parts], axis=1).astype(BF16)
        values = jnp.concatenate([p[d * set_count : (d + 1) * set_count, :] for p in parts], axis=1)
        gram = dot_nt(basis, basis)
        diag = iota((NB, NB), 0) == iota((NB, NB), 1)
        gram = jnp.where(diag, gram + ridge, gram)
        right = sums
        at_g, at_r = iota(gram.shape, 0), iota(right.shape, 0)
        for j in range(NB - 1):
            inv = 1.0 / gram[j : j + 1, j : j + 1]
            col = gram[:, j : j + 1]
            row_g = gram[j : j + 1, :] * inv
            row_r = right[j : j + 1, :] * inv
            gram = jnp.where(at_g == j, row_g, gram - col * row_g)
            right = jnp.where(at_r == j, row_r, right - col * row_r)
        right = jnp.where(at_r < NB - 1, right, 0.0)
        solved = pltpu.roll(right, width - set_count, 1)
        last = sums[NF : NF + 1]
        square = pltpu.roll(last, width - 2 * set_count, 1) + ridge
        cross = pltpu.roll(last, width - 3 * set_count, 1)
        here = iota((1, width), 1) < set_count
        below = jnp.where(here, square - jnp.sum(sums * right, axis=0, keepdims=True), 1.0)
        above = cross - jnp.sum(sums * solved, axis=0, keepdims=True)
        slope = jnp.where(here, above / below, 0.0)
        coef = jnp.where(at_r < NB - 1, solved - right * slope, slope)
        coef = jnp.concatenate([coef, jnp.zeros((width - NB, width), F32)], axis=0).T
        coef = coef[0:set_count]
        linear = sum(dot(piece[:, 0:NB], basis) for piece in pieces(coef, 3))
        fitted = linear + coef[:, NB - 1 : NB] * jnp.tanh(values / VALUE_SCALE)
        fit_ref[d] = fitted[:, 0:paths]
        positive = jnp.sum(jnp.maximum(values - fitted, 0.0), axis=1, keepdims=True)
        rows.append(jnp.broadcast_to(positive * (1.0 / paths_all), (set_count, 128)))
    rows.append(jnp.zeros((128 - DATES * set_count, 128), F32))
    flat = jnp.concatenate(rows, axis=0).T
    for d in range(DATES):
        moved = pltpu.roll(flat, 128 - d * set_count, 1) if d else flat
        pos_ref[d : d + 1, :] = moved[0:1, 0:set_count]


def smem():
    return pl.BlockSpec(memory_space=pltpu.SMEM)


def vmem(count):
    return [pl.BlockSpec(memory_space=pltpu.VMEM)] * count


def params():
    return pltpu.CompilerParams(vmem_limit_bytes=VMEM_LIMIT)


def turn(x, axis, k):
    n = lax.axis_size(axis)
    return lax.ppermute(x, axis, [(i, (i + k) % n) for i in range(n)])


def on_device(
    path_states, trade_loads, trade_amounts, trade_legs, trade_set, set_slot, risk_weights
):
    owners = lax.axis_size("trades")
    groups = lax.axis_size("paths")
    trades, factors = trade_loads.shape
    sets = set_slot.shape[0]
    set_count = sets // owners
    cap = 5 * trades // (2 * owners)
    paths = path_states.shape[1]
    cols = DATES * paths
    count = owners * cap
    block = (cap + META, factors)
    few = owners <= 8
    me = lax.axis_index("trades").astype(jnp.int32)
    if few:
        shape = [jax.ShapeDtypeStruct(block, BF16)] * owners
    else:
        me = jnp.zeros_like(me)
        shape = [jax.ShapeDtypeStruct((owners,) + block, BF16)]
    packed = pl.pallas_call(
        lambda *refs: pack_kernel(owners, cap, set_count, *refs),
        out_shape=shape,
        in_specs=[smem()] + vmem(5),
        out_specs=vmem(len(shape)),
        compiler_params=params(),
        name="pack",
    )(
        me.reshape(1),
        trade_set.reshape(1, trades),
        set_slot.reshape(1, sets),
        trade_amounts,
        trade_legs,
        trade_loads,
    )
    if few:
        got = [packed[0]] + [turn(packed[k], "trades", k) for k in range(1, owners)]
    else:
        got = [lax.all_to_all(packed[0], "trades", split_axis=0, concat_axis=0, tiled=True)]
    packet = (DATES * (set_count + NB) + NB, paths)
    mine = pl.pallas_call(
        lambda *refs: owner_kernel(owners, cap, set_count, *refs),
        out_shape=jax.ShapeDtypeStruct(packet, F32),
        in_specs=[smem()] + vmem(1 + len(got)),
        out_specs=vmem(1)[0],
        scratch_shapes=[
            pltpu.VMEM((count, cols), F32),
            pltpu.VMEM((B * set_count, cols), F32),
            pltpu.VMEM((2 * count, cols), BF16),
            pltpu.VMEM((count, cols), BF16),
            pltpu.VMEM((count, cols), BF16),
            pltpu.VMEM((B * set_count, 2 * count), BF16),
        ],
        compiler_params=params(),
        name="owner",
    )(risk_weights, path_states.reshape(cols, factors), *got)
    parts = [mine] + [turn(mine, "paths", k) for k in range(1, groups)]
    fitted_margin, exposure = pl.pallas_call(
        lambda *refs: fit_kernel(groups, set_count, *refs),
        out_shape=[
            jax.ShapeDtypeStruct((DATES, set_count, paths), F32),
            jax.ShapeDtypeStruct((DATES, set_count), F32),
        ],
        in_specs=vmem(groups),
        out_specs=vmem(2),
        compiler_params=params(),
        name="fit",
    )(*parts)
    return (fitted_margin, exposure)


def solution(mesh):
    in_specs = (
        P(None, "paths", None),
        P("trades", None),
        P(None, "trades"),
        P(None, "trades"),
        P("trades"),
        P(),
        P(),
    )
    out_specs = (P(None, "trades", "paths"), P(None, "trades"))
    return jax.shard_map(
        on_device, mesh=mesh, in_specs=in_specs, out_specs=out_specs, check_vma=False
    )
```

time: 429 us -> 55.3 us (0.13); the launches traced: 421 us -> 55.1 us
  other arithmetic: 147 us -> 0 us
  local copies, waits for them, and re-layouts: 100 us -> 2.03 us
  waiting for transfers between devices: 105 us -> 18 us
  blocking collectives: 30.3 us -> 0 us
  Pallas kernels: 0 us -> 17.9 us
  between operations: 15.4 us -> 0.7 us
  matrix products: 12.5 us -> 0 us
  starting transfers between devices: 10.6 us -> 16.5 us
    another operation x16 -> x0, other arithmetic: 103 us -> none  [the longest x4 94 us: solve_small(): factor_lower = jnp.linalg.cholesky(gram_matrix)]
    all_to_all x2 -> x0, waiting for transfers between devices: 86.1 us -> none  [the longest x1 86.1 us: on_device(): lax.all_to_all(send_terms, 'trades', split_axis=0, concat_axis=0, tiled=T...]
    scatter x4 -> x0, local copies, waits for them, and re-layouts: 66 us -> none  [the longest x1 63.9 us: on_device(): jnp.zeros((owners * capacity,) + inner_shape, jnp.float32).at[target]]
    scatter-add x3 -> x0, other arithmetic: 35.3 us -> none  [the longest x1 12.9 us: reduce_slots(): jax.ops.segment_sum(fall_cols, set_tag * B + got_tags[:, 2], num_segments...]
    psum x2 -> x0, blocking collectives: 30.3 us -> none  [the longest x1 19.5 us: on_device(): gram_total, moment_total = lax.psum((gram_matrix, moments), 'paths')]
    psum x1 -> x0, waiting for transfers between devices: 19 us -> none  [on_device(): gram_total, moment_total = lax.psum((gram_matrix, moments), 'paths')]
    ppermute x0 -> x10, waiting for transfers between devices: none -> 18 us  [turn(): return lax.ppermute(x, axis, [(i, (i + k) % n) for i in range(n)])]
    pallas_call x0 -> x3, Pallas kernels: none -> 17.9 us  [the longest x1 9.36 us: on_device(): pl.pallas_call(lambda *refs: owner_kernel(owners, cap, set_count, *refs),...]
  transfers between devices with their start and end apart: 3 -> 10, of which waited for: 2 -> 6; matrix products, arithmetic and copies ran while one was open for 18% -> 0% of each run, Pallas kernels for 0% -> 0%
where the time goes in v1:
time: 55.3 us; the launch traced here: 55.1 us
  waiting for transfers between devices  18 us (33%)
  Pallas kernels  17.9 us (32%)
  starting transfers between devices  16.5 us (30%)
  local copies, waits for them, and re-layouts  2.03 us (4%)
  between operations  0.7 us (1%)
    ppermute x10, waiting for transfers between devices, turn(): return lax.ppermute(x, axis, [(i, (i + k) % n) for i in range(n)])  18 us
    ppermute x10, starting transfers between devices, turn(): return lax.ppermute(x, axis, [(i, (i + k) % n) for i in range(n)])  16.5 us
    pallas_call x1, Pallas kernels, on_device(): pl.pallas_call(lambda *refs: owner_kernel(owners, cap, set_count, *refs),...  9.36 us
    pallas_call x1, Pallas kernels, on_device(): pl.pallas_call(lambda *refs: fit_kernel(groups, set_count, *refs), out_sh...  5.08 us
    pallas_call x1, Pallas kernels, on_device(): pl.pallas_call(lambda *refs: pack_kernel(owners, cap, set_count, *refs),...  3.46 us
    unnamed x20, local copies, waits for them, and re-layouts  2.03 us
  transfers between devices with their start and end apart: 10, of which 6 were waited for; matrix products, arithmetic and copies ran while one was open for 0% of the time, Pallas kernels for 0%

profile of v1, /device:TPU:0, one launch (start us, length us, event | category | flops | bytes accessed | tf_op | source)
XLA Modules:
  0.0 55.1 jit_solution(13224764021729806546)
XLA Ops:
  0.6 3.5 %pack.1 = (bf16[168,512]{1,0:T(8,128)(2,1)}, bf16[168,512]{1,0:T(8,128)(2,1)}, bf16[168,512]{1,0:T(8,128)(2,1)}, bf16[168,512]{1,0:T(8,128)(2,1)}, bf16[168,512]...) custom-call(s32[1]{0:T(128)} %bitcast.1.refs_0_, ...), custom_call_target="tpu_custom_call" | custom-call | tf_op jit(solution)/shard_map/pack/pallas_call | solution.py:250
  4.1 0.5 collective-permute-start
  4.5 2.5 %collective-permute-start.1 = (bf16[168,512]{1,0:T(8,128)(2,1)}, bf16[168,512]{1,0:T(8,128)(2,1)S(1)}, u32[]{:S(2)}, u32[]{:S(2)}) collective-permute-start(bf16[168,512]{1,0:T(8,128)(2,1)} %get-tuple-element.12), channel_id=1, source_target_pairs={{0,8},{4,12},{8,16},{12,20},{16,24},{20,28},{24,0},{28,4},{1,9},{5... | collective-permute-start | bytes 516104 | tf_op jit(solution)/shard_map/ppermute | solution.py:227
  7.1 2.4 %collective-permute-start.2 = (bf16[168,512]{1,0:T(8,128)(2,1)}, bf16[168,512]{1,0:T(8,128)(2,1)S(1)}, u32[]{:S(2)}, u32[]{:S(2)}) collective-permute-start(bf16[168,512]{1,0:T(8,128)(2,1)} %get-tuple-element.13), channel_id=1, source_target_pairs={{0,12},{4,16},{8,20},{12,24},{16,28},{20,0},{24,4},{28,8},{1,13},{... | collective-permute-start | bytes 516104 | tf_op jit(solution)/shard_map/ppermute | solution.py:227
  9.5 0.5 collective-permute-start.3
  10.0 0.1 collective-permute-start.4
  10.1 1.8 %collective-permute-done.refs_3_ = bf16[168,512]{1,0:T(8,128)(2,1)S(1)} collective-permute-done((bf16[168,512]{1,0:T(8,128)(2,1)}, bf16[168,512]{1,0:T(8,128)(2,1)S(1)}, u32[]{:S(2)}, u32[]{:S(2)}) %collective-permute-start) | collective-permute-done | bytes 172064 | tf_op jit(solution)/shard_map/ppermute | solution.py:227
  11.8 2.5 %collective-permute-start.5 = (bf16[168,512]{1,0:T(8,128)(2,1)}, bf16[168,512]{1,0:T(8,128)(2,1)S(1)}, u32[]{:S(2)}, u32[]{:S(2)}) collective-permute-start(bf16[168,512]{1,0:T(8,128)(2,1)} %get-tuple-element.16), channel_id=1, source_target_pairs={{0,24},{4,28},{8,0},{12,4},{16,8},{20,12},{24,16},{28,20},{1,25},{... | collective-permute-start | bytes 516104 | tf_op jit(solution)/shard_map/ppermute | solution.py:227
  14.3 0.0 collective-permute-done.1.refs_4_
  14.3 3.4 %collective-permute-start.6 = (bf16[168,512]{1,0:T(8,128)(2,1)}, bf16[168,512]{1,0:T(8,128)(2,1)S(1)}, u32[]{:S(2)}, u32[]{:S(2)}) collective-permute-start(bf16[168,512]{1,0:T(8,128)(2,1)} %get-tuple-element.17), channel_id=1, source_target_pairs={{0,28},{4,0},{8,4},{12,8},{16,12},{20,16},{24,20},{28,24},{1,29},{... | collective-permute-start | bytes 516104 | tf_op jit(solution)/shard_map/ppermute | solution.py:227
  17.7 2.1 %collective-permute-done.2.refs_5_ = bf16[168,512]{1,0:T(8,128)(2,1)S(1)} collective-permute-done((bf16[168,512]{1,0:T(8,128)(2,1)}, bf16[168,512]{1,0:T(8,128)(2,1)S(1)}, u32[]{:S(2)}, u32[]{:S(2)}) %collective-permute-start.2) | collective-permute-done | bytes 172064 | tf_op jit(solution)/shard_map/ppermute | solution.py:227
  19.8 0.2 collective-permute-done.3.refs_6_
  20.0 3.5 %collective-permute-done.4.refs_7_ = bf16[168,512]{1,0:T(8,128)(2,1)S(1)} collective-permute-done((bf16[168,512]{1,0:T(8,128)(2,1)}, bf16[168,512]{1,0:T(8,128)(2,1)S(1)}, u32[]{:S(2)}, u32[]{:S(2)}) %collective-permute-start.4) | collective-permute-done | bytes 172064 | tf_op jit(solution)/shard_map/ppermute | solution.py:227
  23.5 0.0 collective-permute-done.5.refs_8_
  23.5 0.0 collective-permute-done.6.refs_9_
  23.5 0.0 copy-start.6
  23.6 0.0 copy-done
  23.6 0.0 copy-done.1
  23.6 0.0 copy-done.2
  23.6 0.6 %copy-done.4 = bf16[168,512]{1,0:T(8,128)(2,1)} copy-done((bf16[168,512]{1,0:T(8,128)(2,1)}, bf16[168,512]{1,0:T(8,128)(2,1)S(1)}, u32[]{:S(2)}) %copy-start.4) | copy-done | bytes 172056
  24.2 0.0 copy-done.5
  24.3 0.1 copy-done.6
  24.3 9.4 %owner.1.refs_0_ = f32[112,256]{1,0:T(8,128)} custom-call(f32[40]{0:T(128)} %refs_0_.1, bf16[512,512]{1,0:T(8,128)(2,1)} %bitcast.4, bf16[168,512]{1,0:T(8,128)(2,1)} %get-tuple-element.10.refs_2_, bf16[168,512]{1,0:T(8,128)(2,1)} %copy-done, bf16[168,512]{1,0:T(8,128)(2,1)} %copy-done.1, bf16[168,512]{1,0:T(8,128)(2,1)} %copy-done.2, ...), custom_call_target="tpu_custom_call" | custom-call | tf_op jit(solution)/shard_map/owner/pallas_call | solution.py:270
  33.7 3.6 %collective-permute-start.9 = (f32[112,256]{1,0:T(8,128)}, f32[112,256]{1,0:T(8,128)S(1)}, u32[]{:S(2)}, u32[]{:S(2)}) collective-permute-start(f32[112,256]{1,0:T(8,128)} %owner.1.refs_0_), channel_id=1, source_target_pairs={{0,3},{1,0},{2,1},{3,2},{4,7},{5,4},{6,5},{7,6},{8,11},{9,8},{10,9... | collective-permute-start | bytes 344072 | tf_op jit(solution)/shard_map/ppermute | solution.py:227
  37.3 0.0 collective-permute-start.8
  37.3 1.0 %collective-permute-start.7 = (f32[112,256]{1,0:T(8,128)}, f32[112,256]{1,0:T(8,128)S(1)}, u32[]{:S(2)}, u32[]{:S(2)}) collective-permute-start(f32[112,256]{1,0:T(8,128)} %owner.1.refs_0_), channel_id=1, source_target_pairs={{0,1},{1,2},{2,3},{3,0},{4,5},{5,6},{6,7},{7,4},{8,9},{9,10},{10,1... | collective-permute-start | bytes 344072 | tf_op jit(solution)/shard_map/ppermute | solution.py:227
  38.3 2.9 %collective-permute-done.9.refs_3_ = f32[112,256]{1,0:T(8,128)S(1)} collective-permute-done((f32[112,256]{1,0:T(8,128)}, f32[112,256]{1,0:T(8,128)S(1)}, u32[]{:S(2)}, u32[]{:S(2)}) %collective-permute-start.9) | collective-permute-done | bytes 114720 | tf_op jit(solution)/shard_map/ppermute | solution.py:227
  41.2 7.6 %collective-permute-done.8.refs_2_ = f32[112,256]{1,0:T(8,128)S(1)} collective-permute-done((f32[112,256]{1,0:T(8,128)}, f32[112,256]{1,0:T(8,128)S(1)}, u32[]{:S(2)}, u32[]{:S(2)}) %collective-permute-start.8) | collective-permute-done | bytes 114720 | tf_op jit(solution)/shard_map/ppermute | solution.py:227
  48.8 0.0 collective-permute-done.7.refs_1_
  48.8 0.6 %copy-done.8 = f32[112,256]{1,0:T(8,128)} copy-done((f32[112,256]{1,0:T(8,128)}, f32[112,256]{1,0:T(8,128)S(1)}, u32[]{:S(2)}) %copy-start.8) | copy-done | bytes 114712
  49.4 0.6 %copy-done.9 = f32[112,256]{1,0:T(8,128)} copy-done((f32[112,256]{1,0:T(8,128)}, f32[112,256]{1,0:T(8,128)S(1)}, u32[]{:S(2)}) %copy-start.9) | copy-done | bytes 114712
  50.1 5.1 %fit.1 = (f32[2,32,256]{2,1,0:T(8,128)}, f32[2,32]{1,0:T(2,128)}) custom-call(f32[112,256]{1,0:T(8,128)} %owner.1.refs_0_, f32[112,256]{1,0:T(8,128)} %copy-done.9, f32[112,256]{1,0:T(8,128)} %copy-done.8, f32[112,256]{1,0:T(8,128)} %copy-done.7), custom_call_target="tpu_custom_call" | custom-call | tf_op jit(solution)/shard_map/fit/pallas_call | solution.py:287
  (11 shorter events, 0.0 us)
Async XLA Ops:
  4.1 7.7 %collective-permute-start = (bf16[168,512]{1,0:T(8,128)(2,1)}, bf16[168,512]{1,0:T(8,128)(2,1)S(1)}, u32[]{:S(2)}, u32[]{:S(2)}) collective-permute-start(bf16[168,512]{1,0:T(8,128)(2,1)} %get-tuple-element.11), channel_id=1, source_target_pairs={{0,4},{4,8},{8,12},{12,16},{16,20},{20,24},{24,28},{28,0},{1,5},{5... | collective-permute-start | bytes 516104 | tf_op jit(solution)/shard_map/ppermute | solution.py:227
  4.5 9.8 %collective-permute-start.1 = (bf16[168,512]{1,0:T(8,128)(2,1)}, bf16[168,512]{1,0:T(8,128)(2,1)S(1)}, u32[]{:S(2)}, u32[]{:S(2)}) collective-permute-start(bf16[168,512]{1,0:T(8,128)(2,1)} %get-tuple-element.12), channel_id=1, source_target_pairs={{0,8},{4,12},{8,16},{12,20},{16,24},{20,28},{24,0},{28,4},{1,9},{5... | collective-permute-start | bytes 516104 | tf_op jit(solution)/shard_map/ppermute | solution.py:227
  7.1 12.8 %collective-permute-start.2 = (bf16[168,512]{1,0:T(8,128)(2,1)}, bf16[168,512]{1,0:T(8,128)(2,1)S(1)}, u32[]{:S(2)}, u32[]{:S(2)}) collective-permute-start(bf16[168,512]{1,0:T(8,128)(2,1)} %get-tuple-element.13), channel_id=1, source_target_pairs={{0,12},{4,16},{8,20},{12,24},{16,28},{20,0},{24,4},{28,8},{1,13},{... | collective-permute-start | bytes 516104 | tf_op jit(solution)/shard_map/ppermute | solution.py:227
  9.5 10.6 %collective-permute-start.3 = (bf16[168,512]{1,0:T(8,128)(2,1)}, bf16[168,512]{1,0:T(8,128)(2,1)S(1)}, u32[]{:S(2)}, u32[]{:S(2)}) collective-permute-start(bf16[168,512]{1,0:T(8,128)(2,1)} %get-tuple-element.14), channel_id=1, source_target_pairs={{0,16},{4,20},{8,24},{12,28},{16,0},{20,4},{24,8},{28,12},{1,17},{... | collective-permute-start | bytes 516104 | tf_op jit(solution)/shard_map/ppermute | solution.py:227
  10.0 13.6 %collective-permute-start.4 = (bf16[168,512]{1,0:T(8,128)(2,1)}, bf16[168,512]{1,0:T(8,128)(2,1)S(1)}, u32[]{:S(2)}, u32[]{:S(2)}) collective-permute-start(bf16[168,512]{1,0:T(8,128)(2,1)} %get-tuple-element.15), channel_id=1, source_target_pairs={{0,20},{4,24},{8,28},{12,0},{16,4},{20,8},{24,12},{28,16},{1,21},{... | collective-permute-start | bytes 516104 | tf_op jit(solution)/shard_map/ppermute | solution.py:227
  11.8 11.7 %copy-start = (bf16[168,512]{1,0:T(8,128)(2,1)}, bf16[168,512]{1,0:T(8,128)(2,1)S(1)}, u32[]{:S(2)}) copy-start(bf16[168,512]{1,0:T(8,128)(2,1)S(1)} %collective-permute-done.refs_3_) | copy-start | bytes 516100
  11.8 11.7 %collective-permute-start.5 = (bf16[168,512]{1,0:T(8,128)(2,1)}, bf16[168,512]{1,0:T(8,128)(2,1)S(1)}, u32[]{:S(2)}, u32[]{:S(2)}) collective-permute-start(bf16[168,512]{1,0:T(8,128)(2,1)} %get-tuple-element.16), channel_id=1, source_target_pairs={{0,24},{4,28},{8,0},{12,4},{16,8},{20,12},{24,16},{28,20},{1,25},{... | collective-permute-start | bytes 516104 | tf_op jit(solution)/shard_map/ppermute | solution.py:227
  14.3 9.2 %copy-start.1 = (bf16[168,512]{1,0:T(8,128)(2,1)}, bf16[168,512]{1,0:T(8,128)(2,1)S(1)}, u32[]{:S(2)}) copy-start(bf16[168,512]{1,0:T(8,128)(2,1)S(1)} %collective-permute-done.1.refs_4_) | copy-start | bytes 516100
  14.3 9.2 %collective-permute-start.6 = (bf16[168,512]{1,0:T(8,128)(2,1)}, bf16[168,512]{1,0:T(8,128)(2,1)S(1)}, u32[]{:S(2)}, u32[]{:S(2)}) collective-permute-start(bf16[168,512]{1,0:T(8,128)(2,1)} %get-tuple-element.17), channel_id=1, source_target_pairs={{0,28},{4,0},{8,4},{12,8},{16,12},{20,16},{24,20},{28,24},{1,29},{... | collective-permute-start | bytes 516104 | tf_op jit(solution)/shard_map/ppermute | solution.py:227
  19.8 3.7 %copy-start.2 = (bf16[168,512]{1,0:T(8,128)(2,1)}, bf16[168,512]{1,0:T(8,128)(2,1)S(1)}, u32[]{:S(2)}) copy-start(bf16[168,512]{1,0:T(8,128)(2,1)S(1)} %collective-permute-done.2.refs_5_) | copy-start | bytes 516100
  20.0 3.5 %copy-start.3 = (bf16[168,512]{1,0:T(8,128)(2,1)}, bf16[168,512]{1,0:T(8,128)(2,1)S(1)}, u32[]{:S(2)}) copy-start(bf16[168,512]{1,0:T(8,128)(2,1)S(1)} %collective-permute-done.3.refs_6_) | copy-start | bytes 516100
  23.5 0.7 %copy-start.4 = (bf16[168,512]{1,0:T(8,128)(2,1)}, bf16[168,512]{1,0:T(8,128)(2,1)S(1)}, u32[]{:S(2)}) copy-start(bf16[168,512]{1,0:T(8,128)(2,1)S(1)} %collective-permute-done.4.refs_7_) | copy-start | bytes 516100
  23.5 0.7 %copy-start.5 = (bf16[168,512]{1,0:T(8,128)(2,1)}, bf16[168,512]{1,0:T(8,128)(2,1)S(1)}, u32[]{:S(2)}) copy-start(bf16[168,512]{1,0:T(8,128)(2,1)S(1)} %collective-permute-done.5.refs_8_) | copy-start | bytes 516100
  23.5 0.8 %copy-start.6 = (bf16[168,512]{1,0:T(8,128)(2,1)}, bf16[168,512]{1,0:T(8,128)(2,1)S(1)}, u32[]{:S(2)}) copy-start(bf16[168,512]{1,0:T(8,128)(2,1)S(1)} %collective-permute-done.6.refs_9_) | copy-start | bytes 516100
  33.7 7.5 %collective-permute-start.9 = (f32[112,256]{1,0:T(8,128)}, f32[112,256]{1,0:T(8,128)S(1)}, u32[]{:S(2)}, u32[]{:S(2)}) collective-permute-start(f32[112,256]{1,0:T(8,128)} %owner.1.refs_0_), channel_id=1, source_target_pairs={{0,3},{1,0},{2,1},{3,2},{4,7},{5,4},{6,5},{7,6},{8,11},{9,8},{10,9... | collective-permute-start | bytes 344072 | tf_op jit(solution)/shard_map/ppermute | solution.py:227
  37.3 11.5 %collective-permute-start.8 = (f32[112,256]{1,0:T(8,128)}, f32[112,256]{1,0:T(8,128)S(1)}, u32[]{:S(2)}, u32[]{:S(2)}) collective-permute-start(f32[112,256]{1,0:T(8,128)} %owner.1.refs_0_), channel_id=1, source_target_pairs={{0,2},{1,3},{2,0},{3,1},{4,6},{5,7},{6,4},{7,5},{8,10},{9,11},{10,... | collective-permute-start | bytes 344072 | tf_op jit(solution)/shard_map/ppermute | solution.py:227
  37.3 11.5 %collective-permute-start.7 = (f32[112,256]{1,0:T(8,128)}, f32[112,256]{1,0:T(8,128)S(1)}, u32[]{:S(2)}, u32[]{:S(2)}) collective-permute-start(f32[112,256]{1,0:T(8,128)} %owner.1.refs_0_), channel_id=1, source_target_pairs={{0,1},{1,2},{2,3},{3,0},{4,5},{5,6},{6,7},{7,4},{8,9},{9,10},{10,1... | collective-permute-start | bytes 344072 | tf_op jit(solution)/shard_map/ppermute | solution.py:227
  41.2 7.6 %copy-start.7 = (f32[112,256]{1,0:T(8,128)}, f32[112,256]{1,0:T(8,128)S(1)}, u32[]{:S(2)}) copy-start(f32[112,256]{1,0:T(8,128)S(1)} %collective-permute-done.9.refs_3_) | copy-start | bytes 344068
  48.8 0.6 %copy-start.8 = (f32[112,256]{1,0:T(8,128)}, f32[112,256]{1,0:T(8,128)S(1)}, u32[]{:S(2)}) copy-start(f32[112,256]{1,0:T(8,128)S(1)} %collective-permute-done.8.refs_2_) | copy-start | bytes 344068
  49.4 0.6 %copy-start.9 = (f32[112,256]{1,0:T(8,128)}, f32[112,256]{1,0:T(8,128)S(1)}, u32[]{:S(2)}) copy-start(f32[112,256]{1,0:T(8,128)S(1)} %collective-permute-done.7.refs_1_) | copy-start | bytes 344068

commit v2 on v1

--- a/solution.py
+++ b/solution.py
@@ -87,8 +87,8 @@
 
 
 def owner_kernel(owners, cap, set_count, weight_ref, state_ref, *refs):
-    blocks = refs[: -7]
-    out_ref, level_ref, delta_ref, terms_ref, high_ref, low_ref, place_ref = refs[-7:]
+    blocks = refs[:-8]
+    out_ref, value_ref, level_ref, delta_ref, terms_ref, high_ref, low_ref, place_ref = refs[-8:]
     if len(blocks) == 1:
         blocks = [blocks[0].at[k] for k in range(owners)]
     count = owners * cap
@@ -147,64 +147,76 @@
     basis = dot_nt(eye, states[:, 0:128])
     at = iota(basis.shape, 0)
     basis = jnp.where(at < NF, basis, jnp.where(at == NF, 1.0, 0.0))
+    sums = []
     for d in range(DATES):
         own = slice(d * paths, (d + 1) * paths)
         t, m = spread[:, own], margin[:, own]
         rows = jnp.concatenate([t, m, t * t, t * m], axis=0)
         some = basis[:, own].astype(BF16)
-        sums = sum(dot_nt(some, piece) for piece in pieces(rows, 3))
-        out_ref[d * set_count : (d + 1) * set_count, :] = set_value[:, own]
+        sums.append(sum(dot_nt(some, piece) for piece in pieces(rows, 3)))
+        value_ref[d] = set_value[:, own]
+        out_ref[d * set_count : (d + 1) * set_count, :] = set_value[:, own].astype(BF16)
         base = DATES * set_count
-        out_ref[base + d * NB : base + (d + 1) * NB, :] = basis[:, own]
-        base = base + DATES * NB
-        width = 4 * set_count
-        out_ref[base : base + NB, d * width : (d + 1) * width] = sums
-
-
-def fit_kernel(groups, set_count, *refs):
+        out_ref[base + d * NB : base + (d + 1) * NB, :] = some
+    base = DATES * (set_count + NB)
+    for i, piece in enumerate(pieces(jnp.concatenate(sums, axis=1), 3)):
+        out_ref[base + i * NB : base + (i + 1) * NB, :] = piece
+
+
+def fit_kernel(groups, set_count, value_ref, *refs):
     parts, (fit_ref, pos_ref) = refs[:groups], refs[groups:]
     paths = parts[0].shape[1]
     paths_all = groups * paths
     ridge = RIDGE * paths_all
     width = 4 * set_count
     base = DATES * (set_count + NB)
-    rows = []
+    total = sum(p[base + i * NB : base + (i + 1) * NB, :].astype(F32) for i in range(3) for p in parts)
+    shape = (NB, width)
+    row, lane = iota(shape, 0), iota(shape, 1)
+    shift = 2 * set_count
+    bases, sums, works = [], [], []
     for d in range(DATES):
-        sums = sum(p[base : base + NB, d * width : (d + 1) * width] for p in parts)
         first = DATES * set_count + d * NB
-        basis = jnp.concatenate([p[first : first + NB, :] for p in parts], axis=1).astype(BF16)
-        values = jnp.concatenate([p[d * set_count : (d + 1) * set_count, :] for p in parts], axis=1)
-        gram = dot_nt(basis, basis)
-        diag = iota((NB, NB), 0) == iota((NB, NB), 1)
-        gram = jnp.where(diag, gram + ridge, gram)
-        right = sums
-        at_g, at_r = iota(gram.shape, 0), iota(right.shape, 0)
-        for j in range(NB - 1):
-            inv = 1.0 / gram[j : j + 1, j : j + 1]
-            col = gram[:, j : j + 1]
-            row_g = gram[j : j + 1, :] * inv
-            row_r = right[j : j + 1, :] * inv
-            gram = jnp.where(at_g == j, row_g, gram - col * row_g)
-            right = jnp.where(at_r == j, row_r, right - col * row_r)
-        right = jnp.where(at_r < NB - 1, right, 0.0)
+        basis = jnp.concatenate([p[first : first + NB, :] for p in parts], axis=1)
+        blank = jnp.zeros((shift, basis.shape[1]), BF16)
+        placed = jnp.concatenate([blank, basis, blank[: width - shift - NB]], axis=0)
+        gram = dot_nt(basis, placed)
+        gram = jnp.where(lane - shift == row, gram + ridge, gram)
+        part = total[:, d * width : (d + 1) * width]
+        bases.append(basis)
+        sums.append(part)
+        works.append(jnp.where(lane < shift, part, gram))
+    for j in range(NB - 1):
+        for d in range(DATES):
+            work = works[d]
+            col = jnp.broadcast_to(work[:, shift + j : shift + j + 1], shape)
+            inv = 1.0 / jnp.broadcast_to(col[j : j + 1, :], shape)
+            pivot = jnp.broadcast_to(work[j : j + 1, :], shape) * inv
+            works[d] = jnp.where(row == j, pivot, work - col * pivot)
+    flats = []
+    for d in range(DATES):
+        part, basis = sums[d], bases[d]
+        right = jnp.where(row < NB - 1, works[d], 0.0)
         solved = pltpu.roll(right, width - set_count, 1)
-        last = sums[NF : NF + 1]
+        last = part[NF : NF + 1]
         square = pltpu.roll(last, width - 2 * set_count, 1) + ridge
         cross = pltpu.roll(last, width - 3 * set_count, 1)
         here = iota((1, width), 1) < set_count
-        below = jnp.where(here, square - jnp.sum(sums * right, axis=0, keepdims=True), 1.0)
-        above = cross - jnp.sum(sums * solved, axis=0, keepdims=True)
+        below = jnp.where(here, square - jnp.sum(part * right, axis=0, keepdims=True), 1.0)
+        above = cross - jnp.sum(part * solved, axis=0, keepdims=True)
         slope = jnp.where(here, above / below, 0.0)
-        coef = jnp.where(at_r < NB - 1, solved - right * slope, slope)
+        coef = jnp.where(row < NB - 1, solved - right * slope, slope)
         coef = jnp.concatenate([coef, jnp.zeros((width - NB, width), F32)], axis=0).T
         coef = coef[0:set_count]
+        values = [value_ref[d]] + [p[d * set_count : (d + 1) * set_count, :].astype(F32) for p in parts[1:]]
+        values = jnp.concatenate(values, axis=1)
         linear = sum(dot(piece[:, 0:NB], basis) for piece in pieces(coef, 3))
-        fitted = linear + coef[:, NB - 1 : NB] * jnp.tanh(values / VALUE_SCALE)
+        fitted = linear + coef[:, NB - 1 : NB] * jnp.tanh(values * (1.0 / VALUE_SCALE))
         fit_ref[d] = fitted[:, 0:paths]
         positive = jnp.sum(jnp.maximum(values - fitted, 0.0), axis=1, keepdims=True)
-        rows.append(jnp.broadcast_to(positive * (1.0 / paths_all), (set_count, 128)))
-    rows.append(jnp.zeros((128 - DATES * set_count, 128), F32))
-    flat = jnp.concatenate(rows, axis=0).T
+        flats.append(jnp.broadcast_to(positive * (1.0 / paths_all), (set_count, 128)))
+    flats.append(jnp.zeros((128 - DATES * set_count, 128), F32))
+    flat = jnp.concatenate(flats, axis=0).T
     for d in range(DATES):
         moved = pltpu.roll(flat, 128 - d * set_count, 1) if d else flat
         pos_ref[d : d + 1, :] = moved[0:1, 0:set_count]
@@ -266,12 +278,15 @@
         got = [packed[0]] + [turn(packed[k], "trades", k) for k in range(1, owners)]
     else:
         got = [lax.all_to_all(packed[0], "trades", split_axis=0, concat_axis=0, tiled=True)]
-    packet = (DATES * (set_count + NB) + NB, paths)
-    mine = pl.pallas_call(
+    packet = (DATES * (set_count + NB) + 3 * NB, paths)
+    mine, value = pl.pallas_call(
         lambda *refs: owner_kernel(owners, cap, set_count, *refs),
-        out_shape=jax.ShapeDtypeStruct(packet, F32),
+        out_shape=[
+            jax.ShapeDtypeStruct(packet, BF16),
+            jax.ShapeDtypeStruct((DATES, set_count, paths), F32),
+        ],
         in_specs=[smem()] + vmem(1 + len(got)),
-        out_specs=vmem(1)[0],
+        out_specs=vmem(2),
         scratch_shapes=[
             pltpu.VMEM((count, cols), F32),
             pltpu.VMEM((B * set_count, cols), F32),
@@ -290,11 +305,11 @@
             jax.ShapeDtypeStruct((DATES, set_count, paths), F32),
             jax.ShapeDtypeStruct((DATES, set_count), F32),
         ],
-        in_specs=vmem(groups),
+        in_specs=vmem(1 + groups),
         out_specs=vmem(2),
         compiler_params=params(),
         name="fit",
-    )(*parts)
+    )(value, *parts)
     return (fitted_margin, exposure)
 
 

time: 55.3 us -> 50.6 us (0.915)
  waiting for transfers between devices: 18 us -> 14.8 us
  Pallas kernels: 17.9 us -> 17 us
  local copies, waits for them, and re-layouts: 2.03 us -> 1.4 us
    ppermute x10, waiting for transfers between devices: 18 us -> 14.8 us  [turn(): return lax.ppermute(x, axis, [(i, (i + k) % n) for i in range(n)])]
    pallas_call x1, Pallas kernels: 5.08 us -> 4.18 us  [on_device(): pl.pallas_call(lambda *refs: fit_kernel(groups, set_count, *refs), out_sh...]
    unnamed x20, local copies, waits for them, and re-layouts: 2.03 us -> 1.4 us
where the time goes in v2:
time: 50.6 us; the launch traced here: 50.4 us
  Pallas kernels  17 us (34%)
  starting transfers between devices  16.5 us (33%)
  waiting for transfers between devices  14.8 us (29%)
  local copies, waits for them, and re-layouts  1.4 us (3%)
  between operations  0.7 us (1%)
    ppermute x10, starting transfers between devices, turn(): return lax.ppermute(x, axis, [(i, (i + k) % n) for i in range(n)])  16.5 us
    ppermute x10, waiting for transfers between devices, turn(): return lax.ppermute(x, axis, [(i, (i + k) % n) for i in range(n)])  14.8 us
    pallas_call x1, Pallas kernels, on_device(): pl.pallas_call(lambda *refs: owner_kernel(owners, cap, set_count, *refs),...  9.37 us
    pallas_call x1, Pallas kernels, on_device(): pl.pallas_call(lambda *refs: fit_kernel(groups, set_count, *refs), out_sh...  4.18 us
    pallas_call x1, Pallas kernels, on_device(): pl.pallas_call(lambda *refs: pack_kernel(owners, cap, set_count, *refs),...  3.47 us
    unnamed x20, local copies, waits for them, and re-layouts  1.4 us
  transfers between devices with their start and end apart: 10, of which 6 were waited for; matrix products, arithmetic and copies ran while one was open for 0% of the time, Pallas kernels for 0%

profile of v2, /device:TPU:0, one launch (start us, length us, event | category | flops | bytes accessed | tf_op | source)
XLA Modules:
  0.0 50.4 jit_solution(3212432470341621269)
XLA Ops:
  0.6 3.5 %pack.1 = (bf16[168,512]{1,0:T(8,128)(2,1)}, bf16[168,512]{1,0:T(8,128)(2,1)}, bf16[168,512]{1,0:T(8,128)(2,1)}, bf16[168,512]{1,0:T(8,128)(2,1)}, bf16[168,512]...) custom-call(s32[1]{0:T(128)} %bitcast.1.refs_0_, ...), custom_call_target="tpu_custom_call" | custom-call | tf_op jit(solution)/shard_map/pack/pallas_call | solution.py:262
  4.1 0.5 collective-permute-start
  4.6 2.5 %collective-permute-start.1 = (bf16[168,512]{1,0:T(8,128)(2,1)}, bf16[168,512]{1,0:T(8,128)(2,1)S(1)}, u32[]{:S(2)}, u32[]{:S(2)}) collective-permute-start(bf16[168,512]{1,0:T(8,128)(2,1)} %get-tuple-element.14), channel_id=1, source_target_pairs={{0,8},{4,12},{8,16},{12,20},{16,24},{20,28},{24,0},{28,4},{1,9},{5... | collective-permute-start | bytes 516104 | tf_op jit(solution)/shard_map/ppermute | solution.py:239
  7.1 2.4 %collective-permute-start.2 = (bf16[168,512]{1,0:T(8,128)(2,1)}, bf16[168,512]{1,0:T(8,128)(2,1)S(1)}, u32[]{:S(2)}, u32[]{:S(2)}) collective-permute-start(bf16[168,512]{1,0:T(8,128)(2,1)} %get-tuple-element.15), channel_id=1, source_target_pairs={{0,12},{4,16},{8,20},{12,24},{16,28},{20,0},{24,4},{28,8},{1,13},{... | collective-permute-start | bytes 516104 | tf_op jit(solution)/shard_map/ppermute | solution.py:239
  9.5 0.5 %collective-permute-start.3 = (bf16[168,512]{1,0:T(8,128)(2,1)}, bf16[168,512]{1,0:T(8,128)(2,1)S(1)}, u32[]{:S(2)}, u32[]{:S(2)}) collective-permute-start(bf16[168,512]{1,0:T(8,128)(2,1)} %get-tuple-element.16), channel_id=1, source_target_pairs={{0,16},{4,20},{8,24},{12,28},{16,0},{20,4},{24,8},{28,12},{1,17},{... | collective-permute-start | bytes 516104 | tf_op jit(solution)/shard_map/ppermute | solution.py:239
  10.0 0.1 collective-permute-start.4
  10.1 1.8 %collective-permute-done.refs_3_ = bf16[168,512]{1,0:T(8,128)(2,1)S(1)} collective-permute-done((bf16[168,512]{1,0:T(8,128)(2,1)}, bf16[168,512]{1,0:T(8,128)(2,1)S(1)}, u32[]{:S(2)}, u32[]{:S(2)}) %collective-permute-start) | collective-permute-done | bytes 172064 | tf_op jit(solution)/shard_map/ppermute | solution.py:239
  11.8 2.5 %collective-permute-start.5 = (bf16[168,512]{1,0:T(8,128)(2,1)}, bf16[168,512]{1,0:T(8,128)(2,1)S(1)}, u32[]{:S(2)}, u32[]{:S(2)}) collective-permute-start(bf16[168,512]{1,0:T(8,128)(2,1)} %get-tuple-element.18), channel_id=1, source_target_pairs={{0,24},{4,28},{8,0},{12,4},{16,8},{20,12},{24,16},{28,20},{1,25},{... | collective-permute-start | bytes 516104 | tf_op jit(solution)/shard_map/ppermute | solution.py:239
  14.3 0.0 collective-permute-done.1.refs_4_
  14.3 3.4 %collective-permute-start.6 = (bf16[168,512]{1,0:T(8,128)(2,1)}, bf16[168,512]{1,0:T(8,128)(2,1)S(1)}, u32[]{:S(2)}, u32[]{:S(2)}) collective-permute-start(bf16[168,512]{1,0:T(8,128)(2,1)} %get-tuple-element.19), channel_id=1, source_target_pairs={{0,28},{4,0},{8,4},{12,8},{16,12},{20,16},{24,20},{28,24},{1,29},{... | collective-permute-start | bytes 516104 | tf_op jit(solution)/shard_map/ppermute | solution.py:239
  17.7 2.1 %collective-permute-done.2.refs_5_ = bf16[168,512]{1,0:T(8,128)(2,1)S(1)} collective-permute-done((bf16[168,512]{1,0:T(8,128)(2,1)}, bf16[168,512]{1,0:T(8,128)(2,1)S(1)}, u32[]{:S(2)}, u32[]{:S(2)}) %collective-permute-start.2) | collective-permute-done | bytes 172064 | tf_op jit(solution)/shard_map/ppermute | solution.py:239
  19.9 0.2 collective-permute-done.3.refs_6_
  20.0 3.5 %collective-permute-done.4.refs_7_ = bf16[168,512]{1,0:T(8,128)(2,1)S(1)} collective-permute-done((bf16[168,512]{1,0:T(8,128)(2,1)}, bf16[168,512]{1,0:T(8,128)(2,1)S(1)}, u32[]{:S(2)}, u32[]{:S(2)}) %collective-permute-start.4) | collective-permute-done | bytes 172064 | tf_op jit(solution)/shard_map/ppermute | solution.py:239
  23.5 0.0 collective-permute-done.5.refs_8_
  23.5 0.0 collective-permute-done.6.refs_9_
  23.6 0.0 copy-start.6
  23.6 0.0 copy-done
  23.6 0.0 copy-done.1
  23.6 0.0 copy-done.2
  23.6 0.6 %copy-done.4 = bf16[168,512]{1,0:T(8,128)(2,1)} copy-done((bf16[168,512]{1,0:T(8,128)(2,1)}, bf16[168,512]{1,0:T(8,128)(2,1)S(1)}, u32[]{:S(2)}) %copy-start.4) | copy-done | bytes 172056
  24.2 0.1 copy-done.5
  24.3 0.1 copy-done.6
  24.3 9.4 %owner.1 = (bf16[144,256]{1,0:T(8,128)(2,1)}, f32[2,32,256]{2,1,0:T(8,128)}) custom-call(f32[40]{0:T(128)} %refs_0_.1, bf16[512,512]{1,0:T(8,128)(2,1)} %bitcast.4, bf16[168,512]{1,0:T(8,128)(2,1)} %get-tuple-element.12.refs_2_, bf16[168,512]{1,0:T(8,128)(2,1)} %copy-done, bf16[168,512]{1,0:T(8,128)(2,1)} %copy-done.1, bf16[168,512]{1,0:T(8,128)(2,1)} %copy-done.2, ...), custom_call_target="tpu_custom_call" | custom-call | tf_op jit(solution)/shard_map/owner/pallas_call | solution.py:282
  33.7 3.6 %collective-permute-start.9 = (bf16[144,256]{1,0:T(8,128)(2,1)}, bf16[144,256]{1,0:T(8,128)(2,1)S(1)}, u32[]{:S(2)}, u32[]{:S(2)}) collective-permute-start(bf16[144,256]{1,0:T(8,128)(2,1)} %get-tuple-element.21.refs_1_), channel_id=1, source_target_pairs={{0,3},{1,0},{2,1},{3,2},{4,7},{5,4},{6,5},{7,6},{8,11},{9,8},{10,9... | collective-permute-start | bytes 221192 | tf_op jit(solution)/shard_map/ppermute | solution.py:239
  37.3 0.0 collective-permute-start.8
  37.3 1.0 %collective-permute-start.7 = (bf16[144,256]{1,0:T(8,128)(2,1)}, bf16[144,256]{1,0:T(8,128)(2,1)S(1)}, u32[]{:S(2)}, u32[]{:S(2)}) collective-permute-start(bf16[144,256]{1,0:T(8,128)(2,1)} %get-tuple-element.21.refs_1_), channel_id=1, source_target_pairs={{0,1},{1,2},{2,3},{3,0},{4,5},{5,6},{6,7},{7,4},{8,9},{9,10},{10,1... | collective-permute-start | bytes 221192 | tf_op jit(solution)/shard_map/ppermute | solution.py:239
  38.3 2.0 %collective-permute-done.9.refs_4_ = bf16[144,256]{1,0:T(8,128)(2,1)S(1)} collective-permute-done((bf16[144,256]{1,0:T(8,128)(2,1)}, bf16[144,256]{1,0:T(8,128)(2,1)S(1)}, u32[]{:S(2)}, u32[]{:S(2)}) %collective-permute-start.9) | collective-permute-done | bytes 73760 | tf_op jit(solution)/shard_map/ppermute | solution.py:239
  40.3 5.2 %collective-permute-done.8.refs_3_ = bf16[144,256]{1,0:T(8,128)(2,1)S(1)} collective-permute-done((bf16[144,256]{1,0:T(8,128)(2,1)}, bf16[144,256]{1,0:T(8,128)(2,1)S(1)}, u32[]{:S(2)}, u32[]{:S(2)}) %collective-permute-start.8) | collective-permute-done | bytes 73760 | tf_op jit(solution)/shard_map/ppermute | solution.py:239
  45.5 0.0 collective-permute-done.7.refs_2_
  45.5 0.6 %copy-done.8 = bf16[144,256]{1,0:T(8,128)(2,1)} copy-done((bf16[144,256]{1,0:T(8,128)(2,1)}, bf16[144,256]{1,0:T(8,128)(2,1)S(1)}, u32[]{:S(2)}) %copy-start.8) | copy-done | bytes 73752
  46.2 0.0 copy-done.9
  46.2 4.2 %fit.1 = (f32[2,32,256]{2,1,0:T(8,128)}, f32[2,32]{1,0:T(2,128)}) custom-call(f32[2,32,256]{2,1,0:T(8,128)} %get-tuple-element.20.refs_0_, bf16[144,256]{1,0:T(8,128)(2,1)} %get-tuple-element.21.refs_1_, bf16[144,256]{1,0:T(8,128)(2,1)} %copy-done.9, bf16[144,256]{1,0:T(8,128)(2,1)} %copy-done.8, bf16[144,256]{1,0:T(8,128)(2,1)} %copy-done.7), custom_call_target="tpu_custom_call" | custom-call | tf_op jit(solution)/shard_map/fit/pallas_call | solution.py:302
  (11 shorter events, 0.0 us)
Async XLA Ops:
  4.1 7.7 %collective-permute-start = (bf16[168,512]{1,0:T(8,128)(2,1)}, bf16[168,512]{1,0:T(8,128)(2,1)S(1)}, u32[]{:S(2)}, u32[]{:S(2)}) collective-permute-start(bf16[168,512]{1,0:T(8,128)(2,1)} %get-tuple-element.13), channel_id=1, source_target_pairs={{0,4},{4,8},{8,12},{12,16},{16,20},{20,24},{24,28},{28,0},{1,5},{5... | collective-permute-start | bytes 516104 | tf_op jit(solution)/shard_map/ppermute | solution.py:239
  4.6 9.8 %collective-permute-start.1 = (bf16[168,512]{1,0:T(8,128)(2,1)}, bf16[168,512]{1,0:T(8,128)(2,1)S(1)}, u32[]{:S(2)}, u32[]{:S(2)}) collective-permute-start(bf16[168,512]{1,0:T(8,128)(2,1)} %get-tuple-element.14), channel_id=1, source_target_pairs={{0,8},{4,12},{8,16},{12,20},{16,24},{20,28},{24,0},{28,4},{1,9},{5... | collective-permute-start | bytes 516104 | tf_op jit(solution)/shard_map/ppermute | solution.py:239
  7.1 12.8 %collective-permute-start.2 = (bf16[168,512]{1,0:T(8,128)(2,1)}, bf16[168,512]{1,0:T(8,128)(2,1)S(1)}, u32[]{:S(2)}, u32[]{:S(2)}) collective-permute-start(bf16[168,512]{1,0:T(8,128)(2,1)} %get-tuple-element.15), channel_id=1, source_target_pairs={{0,12},{4,16},{8,20},{12,24},{16,28},{20,0},{24,4},{28,8},{1,13},{... | collective-permute-start | bytes 516104 | tf_op jit(solution)/shard_map/ppermute | solution.py:239
  9.5 10.6 %collective-permute-start.3 = (bf16[168,512]{1,0:T(8,128)(2,1)}, bf16[168,512]{1,0:T(8,128)(2,1)S(1)}, u32[]{:S(2)}, u32[]{:S(2)}) collective-permute-start(bf16[168,512]{1,0:T(8,128)(2,1)} %get-tuple-element.16), channel_id=1, source_target_pairs={{0,16},{4,20},{8,24},{12,28},{16,0},{20,4},{24,8},{28,12},{1,17},{... | collective-permute-start | bytes 516104 | tf_op jit(solution)/shard_map/ppermute | solution.py:239
  10.0 13.6 %collective-permute-start.4 = (bf16[168,512]{1,0:T(8,128)(2,1)}, bf16[168,512]{1,0:T(8,128)(2,1)S(1)}, u32[]{:S(2)}, u32[]{:S(2)}) collective-permute-start(bf16[168,512]{1,0:T(8,128)(2,1)} %get-tuple-element.17), channel_id=1, source_target_pairs={{0,20},{4,24},{8,28},{12,0},{16,4},{20,8},{24,12},{28,16},{1,21},{... | collective-permute-start | bytes 516104 | tf_op jit(solution)/shard_map/ppermute | solution.py:239
  11.8 11.7 %copy-start = (bf16[168,512]{1,0:T(8,128)(2,1)}, bf16[168,512]{1,0:T(8,128)(2,1)S(1)}, u32[]{:S(2)}) copy-start(bf16[168,512]{1,0:T(8,128)(2,1)S(1)} %collective-permute-done.refs_3_) | copy-start | bytes 516100
  11.8 11.7 %collective-permute-start.5 = (bf16[168,512]{1,0:T(8,128)(2,1)}, bf16[168,512]{1,0:T(8,128)(2,1)S(1)}, u32[]{:S(2)}, u32[]{:S(2)}) collective-permute-start(bf16[168,512]{1,0:T(8,128)(2,1)} %get-tuple-element.18), channel_id=1, source_target_pairs={{0,24},{4,28},{8,0},{12,4},{16,8},{20,12},{24,16},{28,20},{1,25},{... | collective-permute-start | bytes 516104 | tf_op jit(solution)/shard_map/ppermute | solution.py:239
  14.3 9.2 %copy-start.1 = (bf16[168,512]{1,0:T(8,128)(2,1)}, bf16[168,512]{1,0:T(8,128)(2,1)S(1)}, u32[]{:S(2)}) copy-start(bf16[168,512]{1,0:T(8,128)(2,1)S(1)} %collective-permute-done.1.refs_4_) | copy-start | bytes 516100
  14.3 9.2 %collective-permute-start.6 = (bf16[168,512]{1,0:T(8,128)(2,1)}, bf16[168,512]{1,0:T(8,128)(2,1)S(1)}, u32[]{:S(2)}, u32[]{:S(2)}) collective-permute-start(bf16[168,512]{1,0:T(8,128)(2,1)} %get-tuple-element.19), channel_id=1, source_target_pairs={{0,28},{4,0},{8,4},{12,8},{16,12},{20,16},{24,20},{28,24},{1,29},{... | collective-permute-start | bytes 516104 | tf_op jit(solution)/shard_map/ppermute | solution.py:239
  19.9 3.7 %copy-start.2 = (bf16[168,512]{1,0:T(8,128)(2,1)}, bf16[168,512]{1,0:T(8,128)(2,1)S(1)}, u32[]{:S(2)}) copy-start(bf16[168,512]{1,0:T(8,128)(2,1)S(1)} %collective-permute-done.2.refs_5_) | copy-start | bytes 516100
  20.0 3.5 %copy-start.3 = (bf16[168,512]{1,0:T(8,128)(2,1)}, bf16[168,512]{1,0:T(8,128)(2,1)S(1)}, u32[]{:S(2)}) copy-start(bf16[168,512]{1,0:T(8,128)(2,1)S(1)} %collective-permute-done.3.refs_6_) | copy-start | bytes 516100
  23.5 0.7 %copy-start.4 = (bf16[168,512]{1,0:T(8,128)(2,1)}, bf16[168,512]{1,0:T(8,128)(2,1)S(1)}, u32[]{:S(2)}) copy-start(bf16[168,512]{1,0:T(8,128)(2,1)S(1)} %collective-permute-done.4.refs_7_) | copy-start | bytes 516100
  23.5 0.7 %copy-start.5 = (bf16[168,512]{1,0:T(8,128)(2,1)}, bf16[168,512]{1,0:T(8,128)(2,1)S(1)}, u32[]{:S(2)}) copy-start(bf16[168,512]{1,0:T(8,128)(2,1)S(1)} %collective-permute-done.5.refs_8_) | copy-start | bytes 516100
  23.6 0.8 %copy-start.6 = (bf16[168,512]{1,0:T(8,128)(2,1)}, bf16[168,512]{1,0:T(8,128)(2,1)S(1)}, u32[]{:S(2)}) copy-start(bf16[168,512]{1,0:T(8,128)(2,1)S(1)} %collective-permute-done.6.refs_9_) | copy-start | bytes 516100
  33.7 6.6 %collective-permute-start.9 = (bf16[144,256]{1,0:T(8,128)(2,1)}, bf16[144,256]{1,0:T(8,128)(2,1)S(1)}, u32[]{:S(2)}, u32[]{:S(2)}) collective-permute-start(bf16[144,256]{1,0:T(8,128)(2,1)} %get-tuple-element.21.refs_1_), channel_id=1, source_target_pairs={{0,3},{1,0},{2,1},{3,2},{4,7},{5,4},{6,5},{7,6},{8,11},{9,8},{10,9... | collective-permute-start | bytes 221192 | tf_op jit(solution)/shard_map/ppermute | solution.py:239
  37.3 8.2 %collective-permute-start.8 = (bf16[144,256]{1,0:T(8,128)(2,1)}, bf16[144,256]{1,0:T(8,128)(2,1)S(1)}, u32[]{:S(2)}, u32[]{:S(2)}) collective-permute-start(bf16[144,256]{1,0:T(8,128)(2,1)} %get-tuple-element.21.refs_1_), channel_id=1, source_target_pairs={{0,2},{1,3},{2,0},{3,1},{4,6},{5,7},{6,4},{7,5},{8,10},{9,11},{10,... | collective-permute-start | bytes 221192 | tf_op jit(solution)/shard_map/ppermute | solution.py:239
  37.3 8.2 %collective-permute-start.7 = (bf16[144,256]{1,0:T(8,128)(2,1)}, bf16[144,256]{1,0:T(8,128)(2,1)S(1)}, u32[]{:S(2)}, u32[]{:S(2)}) collective-permute-start(bf16[144,256]{1,0:T(8,128)(2,1)} %get-tuple-element.21.refs_1_), channel_id=1, source_target_pairs={{0,1},{1,2},{2,3},{3,0},{4,5},{5,6},{6,7},{7,4},{8,9},{9,10},{10,1... | collective-permute-start | bytes 221192 | tf_op jit(solution)/shard_map/ppermute | solution.py:239
  40.3 5.2 %copy-start.7 = (bf16[144,256]{1,0:T(8,128)(2,1)}, bf16[144,256]{1,0:T(8,128)(2,1)S(1)}, u32[]{:S(2)}) copy-start(bf16[144,256]{1,0:T(8,128)(2,1)S(1)} %collective-permute-done.9.refs_4_) | copy-start | bytes 221188
  45.5 0.6 %copy-start.8 = (bf16[144,256]{1,0:T(8,128)(2,1)}, bf16[144,256]{1,0:T(8,128)(2,1)S(1)}, u32[]{:S(2)}) copy-start(bf16[144,256]{1,0:T(8,128)(2,1)S(1)} %collective-permute-done.8.refs_3_) | copy-start | bytes 221188
  45.5 0.7 %copy-start.9 = (bf16[144,256]{1,0:T(8,128)(2,1)}, bf16[144,256]{1,0:T(8,128)(2,1)S(1)}, u32[]{:S(2)}) copy-start(bf16[144,256]{1,0:T(8,128)(2,1)S(1)} %collective-permute-done.7.refs_2_) | copy-start | bytes 221188

commit v3 on v2

--- a/solution.py
+++ b/solution.py
@@ -12,6 +12,8 @@
 DATES = 2
 NF = NB - 2
 META = 8
+EARLY = 4
+STEP = 8
 HALF = 256
 
 CORR_LEN = 8.0
@@ -69,46 +71,63 @@
     marks = jnp.where(iota((height, trades), 0).astype(F32) == owner, 1.0, 0.0)
     ahead = jnp.where(iota((trades, trades), 0) < iota((trades, trades), 1), 1.0, 0.0).astype(BF16)
     rank = jnp.sum(dot(marks.astype(BF16), ahead) * marks, axis=0, keepdims=True)
-    target = (owner * cap + rank).astype(jnp.int32) - me_ref[0] * cap
-    target = jnp.where(target < 0, target + owners * cap, target)
+    target = (owner * cap + rank).astype(jnp.int32)
     amounts = amount_ref[...]
     legs = leg_ref[...].astype(F32)
     meta = [p.astype(F32) for p in pieces(amounts[0:1], 3) + pieces(amounts[1:2], 3)]
     meta = pick_rows(meta + [legs[0:1], legs[1:2], local], 16).astype(BF16)
-    loads = load_ref[...]
-    for k in range(owners):
-        place = jnp.where(iota((HALF, trades), 0) + k * cap == target, 1.0, 0.0).astype(BF16)
-        moved = dot(place[:cap], loads)
-        tags = dot_nt(meta, place)
-        out = outs[k] if len(outs) > 1 else outs[0].at[k]
-        out[0:cap, :] = moved.astype(BF16)
-        out[cap : cap + META, 0:HALF] = tags[0:META].astype(BF16)
-        out[cap : cap + META, HALF : 2 * HALF] = tags[META : 2 * META].astype(BF16)
-
-
-def owner_kernel(owners, cap, set_count, weight_ref, state_ref, *refs):
-    blocks = refs[:-8]
-    out_ref, value_ref, level_ref, delta_ref, terms_ref, high_ref, low_ref, place_ref = refs[-8:]
-    if len(blocks) == 1:
-        blocks = [blocks[0].at[k] for k in range(owners)]
-    count = owners * cap
-    cols = state_ref.shape[0]
-    paths = cols // DATES
-    states = state_ref[...]
-    meta = jnp.zeros((2 * META, count), F32)
-    for k in range(owners):
-        tags = jnp.concatenate(
-            [blocks[k][cap : cap + META, 0:HALF], blocks[k][cap : cap + META, HALF : 2 * HALF]], axis=0
-        ).astype(F32)
-        tags = jnp.where(iota(tags.shape, 1) < cap, tags, 0.0)
-        tags = jnp.concatenate([tags, jnp.zeros((2 * META, count - HALF), F32)], axis=1)
-        meta = meta + (pltpu.roll(tags, k * cap, 1) if k else tags)
-    first = meta[0:1] + meta[1:2] + meta[2:3]
-    second = meta[3:4] + meta[4:5] + meta[5:6]
-    columns = pick_rows([first, second], 128).T
+    group = 8 if owners > 8 else owners
+    for base in range(0, owners, group):
+        chosen, places = range(base, base + group), []
+        for k in chosen:
+            spot = target - (me_ref[0] ^ k) * cap
+            spot = jnp.where((spot >= 0) & (spot < cap), spot + (k * cap) % 128, -1)
+            places.append(jnp.where(iota((HALF, trades), 0) == spot, 1.0, 0.0).astype(BF16))
+        aligned = (group * cap) % 128 == 0 and cap % 16 == 0
+        if aligned:
+            rows = [p[(k * cap) % 128 : (k * cap) % 128 + cap] for k, p in zip(chosen, places)]
+            moved = dot(jnp.concatenate(rows, axis=0), load_ref[...])
+        for i, k in enumerate(chosen):
+            tags = dot_nt(meta, places[i]).astype(BF16)
+            out = outs[k] if len(outs) > 1 else outs[0].at[k]
+            if aligned:
+                out[0:cap, :] = moved[i * cap : (i + 1) * cap].astype(BF16)
+            else:
+                whole = dot(places[i], load_ref[...])
+                out[0:cap, :] = whole[(k * cap) % 128 : (k * cap) % 128 + cap].astype(BF16)
+            out[cap : cap + META, 0:HALF] = tags[0:META]
+            out[cap : cap + META, HALF : 2 * HALF] = tags[META : 2 * META]
+
+
+def side_by_side(blocks, at, cap, width):
+    start = at * cap // 128 * 128
+    tiles = [None] * (width // 128 + 2)
+    for i, block in enumerate(blocks):
+        first = ((at + i) * cap - start) // 128
+        for j in range(HALF // 128):
+            low = block[cap : cap + META, j * 128 : (j + 1) * 128]
+            high = block[cap : cap + META, HALF + j * 128 : HALF + (j + 1) * 128]
+            tile = jnp.concatenate([low, high], axis=0).astype(F32)
+            tiles[first + j] = tile if tiles[first + j] is None else tiles[first + j] + tile
+    tiles = [jnp.zeros((2 * META, 128), F32) if t is None else t for t in tiles]
+    shift = at * cap - start
+    if not shift:
+        return jnp.concatenate(tiles[: width // 128], axis=1)
+    meta = jnp.concatenate(tiles, axis=1)
+    return pltpu.roll(meta, meta.shape[1] - shift, 1)[:, :width]
+
+
+def price(blocks, at, cap, set_count, states, scratch):
+    level_ref, terms_ref, high_ref, low_ref, place_ref = scratch
+    count = len(blocks) * cap
+    width = high_ref.shape[0]
     loads = jnp.concatenate([block[0:cap, :] for block in blocks], axis=0)
     level_ref[...] = dot_nt(loads, states)
-    step = 128
+    meta = side_by_side(blocks, at, cap, width)
+    eye = jnp.where(iota((16, 128), 0) % 2 == iota((16, 128), 1), 1.0, 0.0).astype(BF16)
+    turned = pick_rows([meta[i : i + 1] for i in (0, 3, 1, 4, 2, 5)], 16).astype(BF16)
+    columns = lax.dot_general(turned, eye, (((0,), (0,)), ((), ())), preferred_element_type=F32)
+    step = math.gcd(count, 128)
     for r in range(0, count, step):
         x = level_ref[r : r + step, :]
         a = columns[r : r + step, 0:1]
@@ -121,26 +140,63 @@
         up = x >= 0.0
         value = a * (jnp.maximum(x, 0.0) + tail) + c * (jnp.maximum(-x, 0.0) + tail)
         terms_ref[r : r + step, :] = (a * jnp.where(up, near, far)).astype(BF16)
-        terms_ref[count + r : count + r + step, :] = (-c * jnp.where(up, far, near)).astype(BF16)
+        terms_ref[width + r : width + r + step, :] = (-c * jnp.where(up, far, near)).astype(BF16)
         high = value.astype(BF16)
         high_ref[r : r + step, :] = high
         low_ref[r : r + step, :] = (value - high.astype(F32)).astype(BF16)
-    in_set = jnp.where(iota((set_count, count), 0).astype(F32) == meta[8:9], 1.0, 0.0)
-    for leg in range(2):
-        at_leg = meta[6 + leg : 7 + leg]
-        for b in range(B):
-            place_ref[b * set_count : (b + 1) * set_count, leg * count : (leg + 1) * count] = (
-                jnp.where(at_leg == float(b), in_set, 0.0).astype(BF16)
-            )
-    delta_ref[...] = dot(place_ref[...], terms_ref[...])
-    in_set = in_set.astype(BF16)
-    set_value = dot(in_set, high_ref[...]) + dot(in_set, low_ref[...])
+    if width > count:
+        for ref, first in ((terms_ref, 0), (terms_ref, width), (high_ref, 0), (low_ref, 0)):
+            ref[first + count : first + width, :] = jnp.zeros((width - count, ref.shape[1]), BF16)
+    in_set = jnp.where(iota((set_count, width), 0).astype(F32) == meta[8:9], 1.0, 0.0)
+
+    def bucket_deltas(first, last):
+        rows = slice(first * set_count, last * set_count)
+        for leg in range(2):
+            for b in range(first, last):
+                place_ref[b * set_count : (b + 1) * set_count, leg * width : (leg + 1) * width] = (
+                    jnp.where(meta[6 + leg : 7 + leg] == float(b), in_set, 0.0).astype(BF16)
+                )
+        return dot(place_ref[rows, :], terms_ref[...])
+
+    named = in_set.astype(BF16)
+    return bucket_deltas, dot(named, high_ref[...]) + dot(named, low_ref[...])
+
+
+def add_kernel(cap, set_count, state_ref, *refs):
+    scratch, out_ref, blocks = refs[-5:], refs[-6], refs[:-6]
+    deltas, value = price(blocks, 0, cap, set_count, state_ref[...], scratch)
+    for b in range(0, B, STEP):
+        out_ref[b * set_count : (b + STEP) * set_count, :] = deltas(b, b + STEP)
+    out_ref[B * set_count :, :] = value
+
+
+def owner_kernel(owners, at, cap, set_count, weight_ref, state_ref, *refs):
+    out_ref, value_ref = refs[-9:-7] if at else refs[-7:-5]
+    blocks = refs[1:-9] if at else refs[:-7]
+    if at:
+        sofar_ref, arrived = refs[-7:-5]
+        fetch = pltpu.make_async_copy(refs[0], sofar_ref, arrived)
+        fetch.start()
+    if len(blocks) == 1 and owners > 1:
+        blocks = [blocks[0].at[k] for k in range(owners)]
+    cols = state_ref.shape[0]
+    paths = cols // DATES
+    states = state_ref[...]
+    deltas, set_value = price(blocks, at, cap, set_count, states, refs[-5:])
+    if at:
+        fetch.wait()
+        set_value = set_value + sofar_ref[B * set_count :, :]
     rho = math.exp(-1.0 / CORR_LEN)
     carry = jnp.zeros((set_count, cols), F32)
     quad = jnp.zeros((set_count, cols), F32)
-    for b in range(B - 1, -1, -1):
-        carry = rho * carry + weight_ref[b] * delta_ref[b * set_count : (b + 1) * set_count, :]
-        quad = quad + (1.0 if b == 0 else 1.0 - rho * rho) * (carry * carry)
+    for first in range(B - STEP, -1, -STEP):
+        delta = deltas(first, first + STEP)
+        for b in range(first + STEP - 1, first - 1, -1):
+            one = delta[(b - first) * set_count : (b - first + 1) * set_count]
+            if at:
+                one = one + sofar_ref[b * set_count : (b + 1) * set_count, :]
+            carry = rho * carry + weight_ref[b] * one
+            quad = quad + (1.0 if b == 0 else 1.0 - rho * rho) * (carry * carry)
     margin = IM_SCALE * jnp.sqrt(1.0 + quad)
     spread = jnp.tanh(set_value / VALUE_SCALE)
     eye = jnp.where(iota((NB, 128), 0) == iota((NB, 128), 1), 1.0, 0.0).astype(BF16)
@@ -151,16 +207,21 @@
     for d in range(DATES):
         own = slice(d * paths, (d + 1) * paths)
         t, m = spread[:, own], margin[:, own]
-        rows = jnp.concatenate([t, m, t * t, t * m], axis=0)
         some = basis[:, own].astype(BF16)
-        sums.append(sum(dot_nt(some, piece) for piece in pieces(rows, 3)))
+        ones = jnp.where(iota(some.shape, 0) == NB - 1, 1.0, 0.0).astype(BF16)
+        first, second = pieces(jnp.concatenate([t, m], axis=0), 3), pieces(jnp.concatenate([t * t, t * m], axis=0), 3)
+        sums.append(sum(dot_nt(some, piece) for piece in first) + sum(dot_nt(ones, piece) for piece in second))
         value_ref[d] = set_value[:, own]
         out_ref[d * set_count : (d + 1) * set_count, :] = set_value[:, own].astype(BF16)
         base = DATES * set_count
         out_ref[base + d * NB : base + (d + 1) * NB, :] = some
     base = DATES * (set_count + NB)
-    for i, piece in enumerate(pieces(jnp.concatenate(sums, axis=1), 3)):
-        out_ref[base + i * NB : base + (i + 1) * NB, :] = piece
+    sums = pieces(jnp.concatenate(sums, axis=1), 3)
+    width = 2 * DATES * set_count
+    for i, piece in enumerate(sums):
+        row, lane = base + i // 2 * NB, i % 2 * width
+        out_ref[row : row + NB, lane : lane + width] = piece
+    out_ref[base + NB : base + 2 * NB, width : 2 * width] = jnp.zeros((NB, width), BF16)
 
 
 def fit_kernel(groups, set_count, value_ref, *refs):
@@ -168,9 +229,10 @@
     paths = parts[0].shape[1]
     paths_all = groups * paths
     ridge = RIDGE * paths_all
-    width = 4 * set_count
+    width = 2 * DATES * set_count
     base = DATES * (set_count + NB)
-    total = sum(p[base + i * NB : base + (i + 1) * NB, :].astype(F32) for i in range(3) for p in parts)
+    total = sum(p[base : base + 2 * NB, :].astype(F32) for p in parts)
+    total = total[0:NB, 0:width] + total[0:NB, width : 2 * width] + total[NB : 2 * NB, 0:width]
     shape = (NB, width)
     row, lane = iota(shape, 0), iota(shape, 1)
     shift = 2 * set_count
@@ -182,10 +244,10 @@
         placed = jnp.concatenate([blank, basis, blank[: width - shift - NB]], axis=0)
         gram = dot_nt(basis, placed)
         gram = jnp.where(lane - shift == row, gram + ridge, gram)
-        part = total[:, d * width : (d + 1) * width]
+        part = pltpu.roll(total, width - d * shift, 1) if d else total
         bases.append(basis)
         sums.append(part)
-        works.append(jnp.where(lane < shift, part, gram))
+        works.append(jnp.where(lane < shift, jnp.where(row < NB - 1, part, 0.0), gram))
     for j in range(NB - 1):
         for d in range(DATES):
             work = works[d]
@@ -198,9 +260,8 @@
         part, basis = sums[d], bases[d]
         right = jnp.where(row < NB - 1, works[d], 0.0)
         solved = pltpu.roll(right, width - set_count, 1)
-        last = part[NF : NF + 1]
-        square = pltpu.roll(last, width - 2 * set_count, 1) + ridge
-        cross = pltpu.roll(last, width - 3 * set_count, 1)
+        square = part[NB - 1 : NB] + ridge
+        cross = pltpu.roll(part[NB - 1 : NB], width - set_count, 1)
         here = iota((1, width), 1) < set_count
         below = jnp.where(here, square - jnp.sum(part * right, axis=0, keepdims=True), 1.0)
         above = cross - jnp.sum(part * solved, axis=0, keepdims=True)
@@ -237,6 +298,11 @@
 def turn(x, axis, k):
     n = lax.axis_size(axis)
     return lax.ppermute(x, axis, [(i, (i + k) % n) for i in range(n)])
+
+
+def meet(x, axis, k):
+    n = lax.axis_size(axis)
+    return lax.ppermute(x, axis, [(i, i ^ k) for i in range(n)])
 
 
 def on_device(
@@ -274,30 +340,51 @@
         trade_legs,
         trade_loads,
     )
+    states = path_states.reshape(cols, factors)
+    reduced = jax.ShapeDtypeStruct(((B + 1) * set_count, cols), F32)
+
+    def scratch(batch):
+        rows = batch * cap
+        wide = -(-rows // 128) * 128
+        return [
+            pltpu.VMEM((rows, cols), F32),
+            pltpu.VMEM((2 * wide, cols), BF16),
+            pltpu.VMEM((wide, cols), BF16),
+            pltpu.VMEM((wide, cols), BF16),
+            pltpu.VMEM((B * set_count, 2 * wide), BF16),
+        ]
+
+    at, sofar, fetched = 0, [], []
     if few:
-        got = [packed[0]] + [turn(packed[k], "trades", k) for k in range(1, owners)]
+        got = [packed[0]] + [meet(packed[k], "trades", k) for k in range(1, owners)]
+        if owners > EARLY:
+            at = EARLY
+            sofar = pl.pallas_call(
+                lambda *refs: add_kernel(cap, set_count, *refs),
+                out_shape=[reduced],
+                in_specs=vmem(1 + at),
+                out_specs=vmem(1),
+                scratch_shapes=scratch(at),
+                compiler_params=params(),
+                name="add",
+            )(states, *got[:at])
+            fetched = [pltpu.VMEM(reduced.shape, F32), pltpu.SemaphoreType.DMA(())]
+        last, held = got[at:], owners - at
     else:
-        got = [lax.all_to_all(packed[0], "trades", split_axis=0, concat_axis=0, tiled=True)]
-    packet = (DATES * (set_count + NB) + 3 * NB, paths)
+        last, held = [lax.all_to_all(packed[0], "trades", split_axis=0, concat_axis=0, tiled=True)], owners
+    packet = (DATES * (set_count + NB) + 2 * NB, paths)
     mine, value = pl.pallas_call(
-        lambda *refs: owner_kernel(owners, cap, set_count, *refs),
+        lambda *refs: owner_kernel(owners, at, cap, set_count, *refs),
         out_shape=[
             jax.ShapeDtypeStruct(packet, BF16),
             jax.ShapeDtypeStruct((DATES, set_count, paths), F32),
         ],
-        in_specs=[smem()] + vmem(1 + len(got)),
+        in_specs=[smem()] + vmem(1) + [pl.BlockSpec(memory_space=pl.ANY)] * len(sofar) + vmem(len(last)),
         out_specs=vmem(2),
-        scratch_shapes=[
-            pltpu.VMEM((count, cols), F32),
-            pltpu.VMEM((B * set_count, cols), F32),
-            pltpu.VMEM((2 * count, cols), BF16),
-            pltpu.VMEM((count, cols), BF16),
-            pltpu.VMEM((count, cols), BF16),
-            pltpu.VMEM((B * set_count, 2 * count), BF16),
-        ],
+        scratch_shapes=fetched + scratch(held),
         compiler_params=params(),
         name="owner",
-    )(risk_weights, path_states.reshape(cols, factors), *got)
+    )(risk_weights, states, *sofar, *last)
     parts = [mine] + [turn(mine, "paths", k) for k in range(1, groups)]
     fitted_margin, exposure = pl.pallas_call(
         lambda *refs: fit_kernel(groups, set_count, *refs),

time: 50.6 us -> 48.4 us (0.957)
  waiting for transfers between devices: 14.8 us -> 10.6 us
  Pallas kernels: 17 us -> 20.3 us
  starting transfers between devices: 16.5 us -> 13.9 us
  local copies, waits for them, and re-layouts: 1.4 us -> 2.7 us
    ppermute x10 -> x3, starting transfers between devices: 16.5 us -> 4.65 us  [turn(): return lax.ppermute(x, axis, [(i, (i + k) % n) for i in range(n)])]
    ppermute x0 -> x7, starting transfers between devices: none -> 9.22 us  [meet(): return lax.ppermute(x, axis, [(i, i ^ k) for i in range(n)])]
    ppermute x10 -> x3, waiting for transfers between devices: 14.8 us -> 6.52 us  [turn(): return lax.ppermute(x, axis, [(i, (i + k) % n) for i in range(n)])]
    ppermute x0 -> x7, waiting for transfers between devices: none -> 4.07 us  [meet(): return lax.ppermute(x, axis, [(i, i ^ k) for i in range(n)])]
    pallas_call x1 -> x2, Pallas kernels: 9.37 us -> 12.6 us  [the longest x1 6.34 us: on_device(): pl.pallas_call(lambda *refs: add_kernel(cap, set_count, *refs), out_shape...]
    unnamed x20, local copies, waits for them, and re-layouts: 1.4 us -> 2.7 us
  transfers between devices with their start and end apart: 10 -> 10, of which waited for: 6 -> 5; matrix products, arithmetic and copies ran while one was open for 0% -> 0% of each run, Pallas kernels for 0% -> 13%
where the time goes in v3:
time: 48.4 us; the launch traced here: 48.1 us
  Pallas kernels  20.3 us (42%)
  starting transfers between devices  13.9 us (29%)
  waiting for transfers between devices  10.6 us (22%)
  local copies, waits for them, and re-layouts  2.7 us (6%)
  between operations  0.68 us (1%)
    ppermute x7, starting transfers between devices, meet(): return lax.ppermute(x, axis, [(i, i ^ k) for i in range(n)])  9.22 us
    ppermute x3, waiting for transfers between devices, turn(): return lax.ppermute(x, axis, [(i, (i + k) % n) for i in range(n)])  6.52 us
    pallas_call x1, Pallas kernels, on_device(): pl.pallas_call(lambda *refs: add_kernel(cap, set_count, *refs), out_shape...  6.34 us
    pallas_call x1, Pallas kernels, on_device(): pl.pallas_call(lambda *refs: owner_kernel(owners, at, cap, set_count, *re...  6.26 us
    ppermute x3, starting transfers between devices, turn(): return lax.ppermute(x, axis, [(i, (i + k) % n) for i in range(n)])  4.65 us
    pallas_call x1, Pallas kernels, on_device(): pl.pallas_call(lambda *refs: fit_kernel(groups, set_count, *refs), out_sh...  4.17 us
    ppermute x7, waiting for transfers between devices, meet(): return lax.ppermute(x, axis, [(i, i ^ k) for i in range(n)])  4.07 us
    pallas_call x1, Pallas kernels, on_device(): pl.pallas_call(lambda *refs: pack_kernel(owners, cap, set_count, *refs),...  3.49 us
  transfers between devices with their start and end apart: 10, of which 5 were waited for; matrix products, arithmetic and copies ran while one was open for 0% of the time, Pallas kernels for 13%

profile of v3, /device:TPU:0, one launch (start us, length us, event | category | flops | bytes accessed | tf_op | source)
XLA Modules:
  0.0 48.1 jit_solution(5256594179295660923)
XLA Ops:
  0.6 3.5 %pack.1 = (bf16[168,512]{1,0:T(8,128)(2,1)}, bf16[168,512]{1,0:T(8,128)(2,1)}, bf16[168,512]{1,0:T(8,128)(2,1)}, bf16[168,512]{1,0:T(8,128)(2,1)}, bf16[168,512]...) custom-call(s32[1]{0:T(128)} %bitcast.1.refs_0_, ...), custom_call_target="tpu_custom_call" | custom-call | tf_op jit(solution)/shard_map/pack/pallas_call | solution.py:328
  4.1 0.5 collective-permute-start
  4.6 2.5 %collective-permute-start.1 = (bf16[168,512]{1,0:T(8,128)(2,1)}, bf16[168,512]{1,0:T(8,128)(2,1)S(1)}, u32[]{:S(2)}, u32[]{:S(2)}) collective-permute-start(bf16[168,512]{1,0:T(8,128)(2,1)} %get-tuple-element.14), channel_id=1, source_target_pairs={{0,8},{4,12},{8,0},{12,4},{16,24},{20,28},{24,16},{28,20},{1,9},{5... | collective-permute-start | bytes 516104 | tf_op jit(solution)/shard_map/ppermute | solution.py:305
  7.1 0.1 collective-permute-start.2
  7.2 1.7 %collective-permute-start.3 = (bf16[168,512]{1,0:T(8,128)(2,1)}, bf16[168,512]{1,0:T(8,128)(2,1)S(1)}, u32[]{:S(2)}, u32[]{:S(2)}) collective-permute-start(bf16[168,512]{1,0:T(8,128)(2,1)} %get-tuple-element.16), channel_id=1, source_target_pairs={{0,16},{4,20},{8,24},{12,28},{16,0},{20,4},{24,8},{28,12},{1,17},{... | collective-permute-start | bytes 516104 | tf_op jit(solution)/shard_map/ppermute | solution.py:305
  9.0 0.0 collective-permute-start.4
  9.0 0.0 collective-permute-done.refs_2_
  9.0 2.6 %collective-permute-start.5 = (bf16[168,512]{1,0:T(8,128)(2,1)}, bf16[168,512]{1,0:T(8,128)(2,1)S(1)}, u32[]{:S(2)}, u32[]{:S(2)}) collective-permute-start(bf16[168,512]{1,0:T(8,128)(2,1)} %get-tuple-element.18), channel_id=1, source_target_pairs={{0,24},{4,28},{8,16},{12,20},{16,8},{20,12},{24,0},{28,4},{1,25},{... | collective-permute-start | bytes 516104 | tf_op jit(solution)/shard_map/ppermute | solution.py:305
  11.5 1.0 %collective-permute-done.1.refs_3_ = bf16[168,512]{1,0:T(8,128)(2,1)S(1)} collective-permute-done((bf16[168,512]{1,0:T(8,128)(2,1)}, bf16[168,512]{1,0:T(8,128)(2,1)S(1)}, u32[]{:S(2)}, u32[]{:S(2)}) %collective-permute-start.1) | collective-permute-done | bytes 172064 | tf_op jit(solution)/shard_map/ppermute | solution.py:305
  12.5 1.8 %collective-permute-start.6 = (bf16[168,512]{1,0:T(8,128)(2,1)}, bf16[168,512]{1,0:T(8,128)(2,1)S(1)}, u32[]{:S(2)}, u32[]{:S(2)}) collective-permute-start(bf16[168,512]{1,0:T(8,128)(2,1)} %get-tuple-element.19), channel_id=1, source_target_pairs={{0,28},{4,24},{8,20},{12,16},{16,12},{20,8},{24,4},{28,0},{1,29},{... | collective-permute-start | bytes 516104 | tf_op jit(solution)/shard_map/ppermute | solution.py:305
  14.3 1.5 %collective-permute-done.2.refs_4_ = bf16[168,512]{1,0:T(8,128)(2,1)S(1)} collective-permute-done((bf16[168,512]{1,0:T(8,128)(2,1)}, bf16[168,512]{1,0:T(8,128)(2,1)S(1)}, u32[]{:S(2)}, u32[]{:S(2)}) %collective-permute-start.2) | collective-permute-done | bytes 172064 | tf_op jit(solution)/shard_map/ppermute | solution.py:305
  15.8 0.0 copy-done.4
  15.8 0.0 copy-done.5
  15.8 0.7 %copy-done.6 = bf16[168,512]{1,0:T(8,128)(2,1)} copy-done((bf16[168,512]{1,0:T(8,128)(2,1)}, bf16[168,512]{1,0:T(8,128)(2,1)S(1)}, u32[]{:S(2)}) %copy-start.6) | copy-done | bytes 172056
  16.5 6.3 %add.1.refs_2_ = f32[1312,512]{1,0:T(8,128)} custom-call(bf16[512,512]{1,0:T(8,128)(2,1)} %bitcast.4, bf16[168,512]{1,0:T(8,128)(2,1)} %get-tuple-element.12.refs_1_, bf16[168,512]{1,0:T(8,128)(2,1)} %copy-done.4, bf16[168,512]{1,0:T(8,128)(2,1)} %copy-done.5, bf16[168,512]{1,0:T(8,128)(2,1)} %copy-done.6), custom_call_target="tpu_custom_call" | custom-call | tf_op jit(solution)/shard_map/add/pallas_call | solution.py:362
  22.8 0.0 collective-permute-done.3.refs_3_
  22.8 1.6 %collective-permute-done.4.refs_4_ = bf16[168,512]{1,0:T(8,128)(2,1)S(1)} collective-permute-done((bf16[168,512]{1,0:T(8,128)(2,1)}, bf16[168,512]{1,0:T(8,128)(2,1)S(1)}, u32[]{:S(2)}, u32[]{:S(2)}) %collective-permute-start.4) | collective-permute-done | bytes 172064 | tf_op jit(solution)/shard_map/ppermute | solution.py:305
  24.4 0.0 collective-permute-done.5.refs_5_
  24.4 0.0 collective-permute-done.6.refs_6_
  24.5 0.7 %copy-done.1 = bf16[168,512]{1,0:T(8,128)(2,1)} copy-done((bf16[168,512]{1,0:T(8,128)(2,1)}, bf16[168,512]{1,0:T(8,128)(2,1)S(1)}, u32[]{:S(2)}) %copy-start.1) | copy-done | bytes 172056
  25.1 0.1 copy-done.2
  25.2 0.7 %copy-done.3 = bf16[168,512]{1,0:T(8,128)(2,1)} copy-done((bf16[168,512]{1,0:T(8,128)(2,1)}, bf16[168,512]{1,0:T(8,128)(2,1)S(1)}, u32[]{:S(2)}) %copy-start.3) | copy-done | bytes 172056
  25.8 6.3 %owner.1 = (bf16[128,256]{1,0:T(8,128)(2,1)}, f32[2,32,256]{2,1,0:T(8,128)}) custom-call(f32[40]{0:T(128)} %refs_0_.1, bf16[512,512]{1,0:T(8,128)(2,1)} %bitcast.5, f32[1312,512]{1,0:T(8,128)} %add.1.refs_2_, bf16[168,512]{1,0:T(8,128)(2,1)} %copy-done, bf16[168,512]{1,0:T(8,128)(2,1)} %copy-done.1, bf16[168,512]{1,0:T(8,128)(2,1)} %copy-done.2, ...), custom_call_target="tpu_custom_call" | custom-call | tf_op jit(solution)/shard_map/owner/pallas_call | solution.py:376
  32.1 3.6 %collective-permute-start.9 = (bf16[128,256]{1,0:T(8,128)(2,1)}, bf16[128,256]{1,0:T(8,128)(2,1)S(1)}, u32[]{:S(2)}, u32[]{:S(2)}) collective-permute-start(bf16[128,256]{1,0:T(8,128)(2,1)} %get-tuple-element.21.refs_1_), channel_id=1, source_target_pairs={{0,3},{1,0},{2,1},{3,2},{4,7},{5,4},{6,5},{7,6},{8,11},{9,8},{10,9... | collective-permute-start | bytes 196616 | tf_op jit(solution)/shard_map/ppermute | solution.py:300
  35.8 0.0 collective-permute-start.8
  35.8 1.0 %collective-permute-start.7 = (bf16[128,256]{1,0:T(8,128)(2,1)}, bf16[128,256]{1,0:T(8,128)(2,1)S(1)}, u32[]{:S(2)}, u32[]{:S(2)}) collective-permute-start(bf16[128,256]{1,0:T(8,128)(2,1)} %get-tuple-element.21.refs_1_), channel_id=1, source_target_pairs={{0,1},{1,2},{2,3},{3,0},{4,5},{5,6},{6,7},{7,4},{8,9},{9,10},{10,1... | collective-permute-start | bytes 196616 | tf_op jit(solution)/shard_map/ppermute | solution.py:300
  36.8 1.8 %collective-permute-done.9.refs_4_ = bf16[128,256]{1,0:T(8,128)(2,1)S(1)} collective-permute-done((bf16[128,256]{1,0:T(8,128)(2,1)}, bf16[128,256]{1,0:T(8,128)(2,1)S(1)}, u32[]{:S(2)}, u32[]{:S(2)}) %collective-permute-start.9) | collective-permute-done | bytes 65568 | tf_op jit(solution)/shard_map/ppermute | solution.py:300
  38.6 4.7 %collective-permute-done.8.refs_3_ = bf16[128,256]{1,0:T(8,128)(2,1)S(1)} collective-permute-done((bf16[128,256]{1,0:T(8,128)(2,1)}, bf16[128,256]{1,0:T(8,128)(2,1)S(1)}, u32[]{:S(2)}, u32[]{:S(2)}) %collective-permute-start.8) | collective-permute-done | bytes 65568 | tf_op jit(solution)/shard_map/ppermute | solution.py:300
  43.3 0.0 collective-permute-done.7.refs_2_
  43.3 0.6 %copy-done.8 = bf16[128,256]{1,0:T(8,128)(2,1)} copy-done((bf16[128,256]{1,0:T(8,128)(2,1)}, bf16[128,256]{1,0:T(8,128)(2,1)S(1)}, u32[]{:S(2)}) %copy-start.8) | copy-done | bytes 65560
  43.9 0.0 copy-done.9
  43.9 4.2 %fit.1 = (f32[2,32,256]{2,1,0:T(8,128)}, f32[2,32]{1,0:T(2,128)}) custom-call(f32[2,32,256]{2,1,0:T(8,128)} %get-tuple-element.20.refs_0_, bf16[128,256]{1,0:T(8,128)(2,1)} %get-tuple-element.21.refs_1_, bf16[128,256]{1,0:T(8,128)(2,1)} %copy-done.9, bf16[128,256]{1,0:T(8,128)(2,1)} %copy-done.8, bf16[128,256]{1,0:T(8,128)(2,1)} %copy-done.7), custom_call_target="tpu_custom_call" | custom-call | tf_op jit(solution)/shard_map/fit/pallas_call | solution.py:389
  (12 shorter events, 0.0 us)
Async XLA Ops:
  4.1 4.8 %collective-permute-start = (bf16[168,512]{1,0:T(8,128)(2,1)}, bf16[168,512]{1,0:T(8,128)(2,1)S(1)}, u32[]{:S(2)}, u32[]{:S(2)}) collective-permute-start(bf16[168,512]{1,0:T(8,128)(2,1)} %get-tuple-element.13), channel_id=1, source_target_pairs={{0,4},{4,0},{8,12},{12,8},{16,20},{20,16},{24,28},{28,24},{1,5},{5... | collective-permute-start | bytes 516104 | tf_op jit(solution)/shard_map/ppermute | solution.py:305
  4.6 7.9 %collective-permute-start.1 = (bf16[168,512]{1,0:T(8,128)(2,1)}, bf16[168,512]{1,0:T(8,128)(2,1)S(1)}, u32[]{:S(2)}, u32[]{:S(2)}) collective-permute-start(bf16[168,512]{1,0:T(8,128)(2,1)} %get-tuple-element.14), channel_id=1, source_target_pairs={{0,8},{4,12},{8,0},{12,4},{16,24},{20,28},{24,16},{28,20},{1,9},{5... | collective-permute-start | bytes 516104 | tf_op jit(solution)/shard_map/ppermute | solution.py:305
  7.1 8.7 %collective-permute-start.2 = (bf16[168,512]{1,0:T(8,128)(2,1)}, bf16[168,512]{1,0:T(8,128)(2,1)S(1)}, u32[]{:S(2)}, u32[]{:S(2)}) collective-permute-start(bf16[168,512]{1,0:T(8,128)(2,1)} %get-tuple-element.15), channel_id=1, source_target_pairs={{0,12},{4,8},{8,4},{12,0},{16,28},{20,24},{24,20},{28,16},{1,13},{... | collective-permute-start | bytes 516104 | tf_op jit(solution)/shard_map/ppermute | solution.py:305
  7.2 15.6 %collective-permute-start.3 = (bf16[168,512]{1,0:T(8,128)(2,1)}, bf16[168,512]{1,0:T(8,128)(2,1)S(1)}, u32[]{:S(2)}, u32[]{:S(2)}) collective-permute-start(bf16[168,512]{1,0:T(8,128)(2,1)} %get-tuple-element.16), channel_id=1, source_target_pairs={{0,16},{4,20},{8,24},{12,28},{16,0},{20,4},{24,8},{28,12},{1,17},{... | collective-permute-start | bytes 516104 | tf_op jit(solution)/shard_map/ppermute | solution.py:305
  9.0 15.5 %collective-permute-start.4 = (bf16[168,512]{1,0:T(8,128)(2,1)}, bf16[168,512]{1,0:T(8,128)(2,1)S(1)}, u32[]{:S(2)}, u32[]{:S(2)}) collective-permute-start(bf16[168,512]{1,0:T(8,128)(2,1)} %get-tuple-element.17), channel_id=1, source_target_pairs={{0,20},{4,16},{8,28},{12,24},{16,4},{20,0},{24,12},{28,8},{1,21},{... | collective-permute-start | bytes 516104 | tf_op jit(solution)/shard_map/ppermute | solution.py:305
  9.0 6.8 %copy-start.4 = (bf16[168,512]{1,0:T(8,128)(2,1)}, bf16[168,512]{1,0:T(8,128)(2,1)S(1)}, u32[]{:S(2)}) copy-start(bf16[168,512]{1,0:T(8,128)(2,1)S(1)} %collective-permute-done.refs_2_) | copy-start | bytes 516100
  9.0 15.5 %collective-permute-start.5 = (bf16[168,512]{1,0:T(8,128)(2,1)}, bf16[168,512]{1,0:T(8,128)(2,1)S(1)}, u32[]{:S(2)}, u32[]{:S(2)}) collective-permute-start(bf16[168,512]{1,0:T(8,128)(2,1)} %get-tuple-element.18), channel_id=1, source_target_pairs={{0,24},{4,28},{8,16},{12,20},{16,8},{20,12},{24,0},{28,4},{1,25},{... | collective-permute-start | bytes 516104 | tf_op jit(solution)/shard_map/ppermute | solution.py:305
  12.5 3.3 %copy-start.5 = (bf16[168,512]{1,0:T(8,128)(2,1)}, bf16[168,512]{1,0:T(8,128)(2,1)S(1)}, u32[]{:S(2)}) copy-start(bf16[168,512]{1,0:T(8,128)(2,1)S(1)} %collective-permute-done.1.refs_3_) | copy-start | bytes 516100
  12.5 11.9 %collective-permute-start.6 = (bf16[168,512]{1,0:T(8,128)(2,1)}, bf16[168,512]{1,0:T(8,128)(2,1)S(1)}, u32[]{:S(2)}, u32[]{:S(2)}) collective-permute-start(bf16[168,512]{1,0:T(8,128)(2,1)} %get-tuple-element.19), channel_id=1, source_target_pairs={{0,28},{4,24},{8,20},{12,16},{16,12},{20,8},{24,4},{28,0},{1,29},{... | collective-permute-start | bytes 516104 | tf_op jit(solution)/shard_map/ppermute | solution.py:305
  15.8 0.7 %copy-start.6 = (bf16[168,512]{1,0:T(8,128)(2,1)}, bf16[168,512]{1,0:T(8,128)(2,1)S(1)}, u32[]{:S(2)}) copy-start(bf16[168,512]{1,0:T(8,128)(2,1)S(1)} %collective-permute-done.2.refs_4_) | copy-start | bytes 516100
  22.8 1.6 %copy-start = (bf16[168,512]{1,0:T(8,128)(2,1)}, bf16[168,512]{1,0:T(8,128)(2,1)S(1)}, u32[]{:S(2)}) copy-start(bf16[168,512]{1,0:T(8,128)(2,1)S(1)} %collective-permute-done.3.refs_3_) | copy-start | bytes 516100
  24.4 0.7 %copy-start.1 = (bf16[168,512]{1,0:T(8,128)(2,1)}, bf16[168,512]{1,0:T(8,128)(2,1)S(1)}, u32[]{:S(2)}) copy-start(bf16[168,512]{1,0:T(8,128)(2,1)S(1)} %collective-permute-done.4.refs_4_) | copy-start | bytes 516100
  24.4 0.7 %copy-start.2 = (bf16[168,512]{1,0:T(8,128)(2,1)}, bf16[168,512]{1,0:T(8,128)(2,1)S(1)}, u32[]{:S(2)}) copy-start(bf16[168,512]{1,0:T(8,128)(2,1)S(1)} %collective-permute-done.5.refs_5_) | copy-start | bytes 516100
  25.2 0.7 %copy-start.3 = (bf16[168,512]{1,0:T(8,128)(2,1)}, bf16[168,512]{1,0:T(8,128)(2,1)S(1)}, u32[]{:S(2)}) copy-start(bf16[168,512]{1,0:T(8,128)(2,1)S(1)} %collective-permute-done.6.refs_6_) | copy-start | bytes 516100
  32.1 6.5 %collective-permute-start.9 = (bf16[128,256]{1,0:T(8,128)(2,1)}, bf16[128,256]{1,0:T(8,128)(2,1)S(1)}, u32[]{:S(2)}, u32[]{:S(2)}) collective-permute-start(bf16[128,256]{1,0:T(8,128)(2,1)} %get-tuple-element.21.refs_1_), channel_id=1, source_target_pairs={{0,3},{1,0},{2,1},{3,2},{4,7},{5,4},{6,5},{7,6},{8,11},{9,8},{10,9... | collective-permute-start | bytes 196616 | tf_op jit(solution)/shard_map/ppermute | solution.py:300
  35.8 7.5 %collective-permute-start.8 = (bf16[128,256]{1,0:T(8,128)(2,1)}, bf16[128,256]{1,0:T(8,128)(2,1)S(1)}, u32[]{:S(2)}, u32[]{:S(2)}) collective-permute-start(bf16[128,256]{1,0:T(8,128)(2,1)} %get-tuple-element.21.refs_1_), channel_id=1, source_target_pairs={{0,2},{1,3},{2,0},{3,1},{4,6},{5,7},{6,4},{7,5},{8,10},{9,11},{10,... | collective-permute-start | bytes 196616 | tf_op jit(solution)/shard_map/ppermute | solution.py:300
  35.8 7.5 %collective-permute-start.7 = (bf16[128,256]{1,0:T(8,128)(2,1)}, bf16[128,256]{1,0:T(8,128)(2,1)S(1)}, u32[]{:S(2)}, u32[]{:S(2)}) collective-permute-start(bf16[128,256]{1,0:T(8,128)(2,1)} %get-tuple-element.21.refs_1_), channel_id=1, source_target_pairs={{0,1},{1,2},{2,3},{3,0},{4,5},{5,6},{6,7},{7,4},{8,9},{9,10},{10,1... | collective-permute-start | bytes 196616 | tf_op jit(solution)/shard_map/ppermute | solution.py:300
  38.6 4.7 %copy-start.7 = (bf16[128,256]{1,0:T(8,128)(2,1)}, bf16[128,256]{1,0:T(8,128)(2,1)S(1)}, u32[]{:S(2)}) copy-start(bf16[128,256]{1,0:T(8,128)(2,1)S(1)} %collective-permute-done.9.refs_4_) | copy-start | bytes 196612
  43.3 0.6 %copy-start.8 = (bf16[128,256]{1,0:T(8,128)(2,1)}, bf16[128,256]{1,0:T(8,128)(2,1)S(1)}, u32[]{:S(2)}) copy-start(bf16[128,256]{1,0:T(8,128)(2,1)S(1)} %collective-permute-done.8.refs_3_) | copy-start | bytes 196612
  43.3 0.6 %copy-start.9 = (bf16[128,256]{1,0:T(8,128)(2,1)}, bf16[128,256]{1,0:T(8,128)(2,1)S(1)}, u32[]{:S(2)}) copy-start(bf16[128,256]{1,0:T(8,128)(2,1)S(1)} %collective-permute-done.7.refs_2_) | copy-start | bytes 196612

commit v4 on v3

--- a/solution.py
+++ b/solution.py
@@ -12,7 +12,7 @@
 DATES = 2
 NF = NB - 2
 META = 8
-EARLY = 4
+EARLY = 5
 STEP = 8
 HALF = 256
 
@@ -23,7 +23,7 @@
 
 F32 = jnp.float32
 BF16 = jnp.bfloat16
-VMEM_LIMIT = 56 << 20
+VMEM_LIMIT = 40 << 20
 NT = (((1,), (1,)), ((), ()))
 
 
@@ -57,7 +57,14 @@
     return out
 
 
-def pack_kernel(owners, cap, set_count, me_ref, set_ref, slot_ref, amount_ref, leg_ref, load_ref, *outs):
+def pack_kernel(owners, cap, set_count, me_ref, *refs):
+    outs, held, arrived = refs[5:-6], refs[-6:-1], refs[-1]
+    copies = [pltpu.make_async_copy(refs[i], held[i], arrived.at[i]) for i in range(5)]
+    for copy in copies:
+        copy.start()
+    set_ref, slot_ref, amount_ref, leg_ref, load_ref = held
+    for copy in copies[:4]:
+        copy.wait()
     trades = set_ref.shape[1]
     sets = slot_ref.shape[1]
     slot = slot_ref[...].astype(F32)
@@ -76,6 +83,7 @@
     legs = leg_ref[...].astype(F32)
     meta = [p.astype(F32) for p in pieces(amounts[0:1], 3) + pieces(amounts[1:2], 3)]
     meta = pick_rows(meta + [legs[0:1], legs[1:2], local], 16).astype(BF16)
+    copies[4].wait()
     group = 8 if owners > 8 else owners
     for base in range(0, owners, group):
         chosen, places = range(base, base + group), []
@@ -171,12 +179,9 @@
 
 
 def owner_kernel(owners, at, cap, set_count, weight_ref, state_ref, *refs):
-    out_ref, value_ref = refs[-9:-7] if at else refs[-7:-5]
-    blocks = refs[1:-9] if at else refs[:-7]
-    if at:
-        sofar_ref, arrived = refs[-7:-5]
-        fetch = pltpu.make_async_copy(refs[0], sofar_ref, arrived)
-        fetch.start()
+    out_ref, value_ref = refs[-7:-5]
+    blocks = refs[1:-7] if at else refs[:-7]
+    sofar_ref = refs[0]
     if len(blocks) == 1 and owners > 1:
         blocks = [blocks[0].at[k] for k in range(owners)]
     cols = state_ref.shape[0]
@@ -184,7 +189,6 @@
     states = state_ref[...]
     deltas, set_value = price(blocks, at, cap, set_count, states, refs[-5:])
     if at:
-        fetch.wait()
         set_value = set_value + sofar_ref[B * set_count :, :]
     rho = math.exp(-1.0 / CORR_LEN)
     carry = jnp.zeros((set_count, cols), F32)
@@ -295,14 +299,18 @@
     return pltpu.CompilerParams(vmem_limit_bytes=VMEM_LIMIT)
 
 
+def near(x):
+    return pltpu.with_memory_space_constraint(x, pltpu.VMEM)
+
+
 def turn(x, axis, k):
     n = lax.axis_size(axis)
-    return lax.ppermute(x, axis, [(i, (i + k) % n) for i in range(n)])
+    return near(lax.ppermute(x, axis, [(i, (i + k) % n) for i in range(n)]))
 
 
 def meet(x, axis, k):
     n = lax.axis_size(axis)
-    return lax.ppermute(x, axis, [(i, i ^ k) for i in range(n)])
+    return near(lax.ppermute(x, axis, [(i, i ^ k) for i in range(n)]))
 
 
 def on_device(
@@ -321,27 +329,28 @@
     few = owners <= 8
     me = lax.axis_index("trades").astype(jnp.int32)
     if few:
-        shape = [jax.ShapeDtypeStruct(block, BF16)] * owners
+        shape = [pltpu.VMEM(block, BF16)] * owners
     else:
         me = jnp.zeros_like(me)
         shape = [jax.ShapeDtypeStruct((owners,) + block, BF16)]
-    packed = pl.pallas_call(
-        lambda *refs: pack_kernel(owners, cap, set_count, *refs),
-        out_shape=shape,
-        in_specs=[smem()] + vmem(5),
-        out_specs=vmem(len(shape)),
-        compiler_params=params(),
-        name="pack",
-    )(
-        me.reshape(1),
+    inputs = (
         trade_set.reshape(1, trades),
         set_slot.reshape(1, sets),
         trade_amounts,
         trade_legs,
         trade_loads,
     )
+    packed = pl.pallas_call(
+        lambda *refs: pack_kernel(owners, cap, set_count, *refs),
+        out_shape=shape,
+        in_specs=[smem()] + [pl.BlockSpec(memory_space=pltpu.HBM)] * 5,
+        out_specs=vmem(len(shape)),
+        scratch_shapes=[pltpu.VMEM(x.shape, x.dtype) for x in inputs] + [pltpu.SemaphoreType.DMA((5,))],
+        compiler_params=params(),
+        name="pack",
+    )(me.reshape(1), *[pltpu.with_memory_space_constraint(x, pltpu.HBM) for x in inputs])
     states = path_states.reshape(cols, factors)
-    reduced = jax.ShapeDtypeStruct(((B + 1) * set_count, cols), F32)
+    reduced = pltpu.VMEM(((B + 1) * set_count, cols), F32)
 
     def scratch(batch):
         rows = batch * cap
@@ -354,9 +363,9 @@
             pltpu.VMEM((B * set_count, 2 * wide), BF16),
         ]
 
-    at, sofar, fetched = 0, [], []
+    at, sofar = 0, []
     if few:
-        got = [packed[0]] + [meet(packed[k], "trades", k) for k in range(1, owners)]
+        got = [near(packed[0])] + [meet(packed[k], "trades", k) for k in range(1, owners)]
         if owners > EARLY:
             at = EARLY
             sofar = pl.pallas_call(
@@ -368,7 +377,7 @@
                 compiler_params=params(),
                 name="add",
             )(states, *got[:at])
-            fetched = [pltpu.VMEM(reduced.shape, F32), pltpu.SemaphoreType.DMA(())]
+            sofar = [near(sofar[0])]
         last, held = got[at:], owners - at
     else:
         last, held = [lax.all_to_all(packed[0], "trades", split_axis=0, concat_axis=0, tiled=True)], owners
@@ -376,16 +385,16 @@
     mine, value = pl.pallas_call(
         lambda *refs: owner_kernel(owners, at, cap, set_count, *refs),
         out_shape=[
-            jax.ShapeDtypeStruct(packet, BF16),
-            jax.ShapeDtypeStruct((DATES, set_count, paths), F32),
+            pltpu.VMEM(packet, BF16),
+            pltpu.VMEM((DATES, set_count, paths), F32),
         ],
-        in_specs=[smem()] + vmem(1) + [pl.BlockSpec(memory_space=pl.ANY)] * len(sofar) + vmem(len(last)),
+        in_specs=[smem()] + vmem(1 + len(sofar) + len(last)),
         out_specs=vmem(2),
-        scratch_shapes=fetched + scratch(held),
+        scratch_shapes=scratch(held),
         compiler_params=params(),
         name="owner",
     )(risk_weights, states, *sofar, *last)
-    parts = [mine] + [turn(mine, "paths", k) for k in range(1, groups)]
+    parts = [near(mine)] + [turn(mine, "paths", k) for k in range(1, groups)]
     fitted_margin, exposure = pl.pallas_call(
         lambda *refs: fit_kernel(groups, set_count, *refs),
         out_shape=[
@@ -396,7 +405,7 @@
         out_specs=vmem(2),
         compiler_params=params(),
         name="fit",
-    )(value, *parts)
+    )(near(value), *parts)
     return (fitted_margin, exposure)
 
 

time: 48.4 us -> 41.6 us (0.86)
  Pallas kernels: 20.3 us -> 14.2 us
  local copies, waits for them, and re-layouts: 2.7 us -> 1.05 us
  waiting for transfers between devices: 10.6 us -> 11.2 us
    pallas_call x1, Pallas kernels: 6.26 us -> 3.88 us  [on_device(): pl.pallas_call(lambda *refs: owner_kernel(owners, at, cap, set_count, *re...]
    pallas_call x1, Pallas kernels: 6.34 us -> 4.61 us  [on_device(): pl.pallas_call(lambda *refs: add_kernel(cap, set_count, *refs), out_shape...]
    unnamed x20 -> x4, local copies, waits for them, and re-layouts: 2.7 us -> 1.05 us
    pallas_call x1, Pallas kernels: 3.49 us -> 2.47 us  [on_device(): pl.pallas_call(lambda *refs: pack_kernel(owners, cap, set_count, *refs),...]
    pallas_call x1, Pallas kernels: 4.17 us -> 3.21 us  [on_device(): pl.pallas_call(lambda *refs: fit_kernel(groups, set_count, *refs), out_sh...]
    ppermute x10, waiting for transfers between devices: 10.6 us -> 11.2 us  [the longest x3 5.98 us: turn(): return near(lax.ppermute(x, axis, [(i, (i + k) % n) for i in range(n)]))]
  transfers between devices with their start and end apart: 10 -> 10, of which waited for: 5 -> 5; matrix products, arithmetic and copies ran while one was open for 0% -> 0% of each run, Pallas kernels for 13% -> 11%
where the time goes in v4:
time: 41.6 us; the launch traced here: 41.4 us
  starting transfers between devices  14.3 us (34%)
  Pallas kernels  14.2 us (34%)
  waiting for transfers between devices  11.2 us (27%)
  local copies, waits for them, and re-layouts  1.05 us (3%)
  between operations  0.68 us (2%)
    ppermute x7, starting transfers between devices, meet(): return near(lax.ppermute(x, axis, [(i, i ^ k) for i in range(n)]))  9.26 us
    ppermute x3, waiting for transfers between devices, turn(): return near(lax.ppermute(x, axis, [(i, (i + k) % n) for i in range(n)]))  5.98 us
    ppermute x7, waiting for transfers between devices, meet(): return near(lax.ppermute(x, axis, [(i, i ^ k) for i in range(n)]))  5.2 us
    ppermute x3, starting transfers between devices, turn(): return near(lax.ppermute(x, axis, [(i, (i + k) % n) for i in range(n)]))  5.09 us
    pallas_call x1, Pallas kernels, on_device(): pl.pallas_call(lambda *refs: add_kernel(cap, set_count, *refs), out_shape...  4.61 us
    pallas_call x1, Pallas kernels, on_device(): pl.pallas_call(lambda *refs: owner_kernel(owners, at, cap, set_count, *re...  3.88 us
    pallas_call x1, Pallas kernels, on_device(): pl.pallas_call(lambda *refs: fit_kernel(groups, set_count, *refs), out_sh...  3.21 us
    pallas_call x1, Pallas kernels, on_device(): pl.pallas_call(lambda *refs: pack_kernel(owners, cap, set_count, *refs),...  2.47 us
  transfers between devices with their start and end apart: 10, of which 5 were waited for; matrix products, arithmetic and copies ran while one was open for 0% of the time, Pallas kernels for 11%

profile of v4, /device:TPU:0, one launch (start us, length us, event | category | flops | bytes accessed | tf_op | source)
XLA Modules:
  0.0 41.4 jit_solution(17075781538045878636)
XLA Ops:
  0.6 0.0 copy-start.1
  0.6 2.5 %pack.1 = (bf16[168,512]{1,0:T(8,128)(2,1)S(1)}, bf16[168,512]{1,0:T(8,128)(2,1)S(1)}, bf16[168,512]{1,0:T(8,128)(2,1)S(1)}, bf16[168,512]{1,0:T(8,128)(2,1)S(1)...) custom-call(s32[1]{0:T(128)} %bitcast.1.refs_0_, ...), custom_call_target="tpu_custom_call" | custom-call | tf_op jit(solution)/shard_map/pack/pallas_call | solution.py:343
  3.1 0.5 %collective-permute-start = (bf16[168,512]{1,0:T(8,128)(2,1)S(1)}, bf16[168,512]{1,0:T(8,128)(2,1)S(1)}, u32[]{:S(2)}, u32[]{:S(2)}) collective-permute-start(bf16[168,512]{1,0:T(8,128)(2,1)S(1)} %get-tuple-element.13), channel_id=1, source_target_pairs={{0,4},{4,0},{8,12},{12,8},{16,20},{20,16},{24,28},{28,24},{1,5},{5... | collective-permute-start | bytes 516104 | tf_op jit(solution)/shard_map/ppermute | solution.py:313
  3.7 2.6 %collective-permute-start.1 = (bf16[168,512]{1,0:T(8,128)(2,1)S(1)}, bf16[168,512]{1,0:T(8,128)(2,1)S(1)}, u32[]{:S(2)}, u32[]{:S(2)}) collective-permute-start(bf16[168,512]{1,0:T(8,128)(2,1)S(1)} %get-tuple-element.14), channel_id=1, source_target_pairs={{0,8},{4,12},{8,0},{12,4},{16,24},{20,28},{24,16},{28,20},{1,9},{5... | collective-permute-start | bytes 516104 | tf_op jit(solution)/shard_map/ppermute | solution.py:313
  6.2 0.1 collective-permute-start.2
  6.3 1.8 %collective-permute-start.3 = (bf16[168,512]{1,0:T(8,128)(2,1)S(1)}, bf16[168,512]{1,0:T(8,128)(2,1)S(1)}, u32[]{:S(2)}, u32[]{:S(2)}) collective-permute-start(bf16[168,512]{1,0:T(8,128)(2,1)S(1)} %get-tuple-element.16), channel_id=1, source_target_pairs={{0,16},{4,20},{8,24},{12,28},{16,0},{20,4},{24,8},{28,12},{1,17},{... | collective-permute-start | bytes 516104 | tf_op jit(solution)/shard_map/ppermute | solution.py:313
  8.1 0.0 collective-permute-start.4
  8.1 0.0 collective-permute-done.refs_2_
  8.1 2.6 %collective-permute-start.5 = (bf16[168,512]{1,0:T(8,128)(2,1)S(1)}, bf16[168,512]{1,0:T(8,128)(2,1)S(1)}, u32[]{:S(2)}, u32[]{:S(2)}) collective-permute-start(bf16[168,512]{1,0:T(8,128)(2,1)S(1)} %get-tuple-element.18), channel_id=1, source_target_pairs={{0,24},{4,28},{8,16},{12,20},{16,8},{20,12},{24,0},{28,4},{1,25},{... | collective-permute-start | bytes 516104 | tf_op jit(solution)/shard_map/ppermute | solution.py:313
  10.7 0.8 %collective-permute-done.1.refs_3_ = bf16[168,512]{1,0:T(8,128)(2,1)S(1)} collective-permute-done((bf16[168,512]{1,0:T(8,128)(2,1)S(1)}, bf16[168,512]{1,0:T(8,128)(2,1)S(1)}, u32[]{:S(2)}, u32[]{:S(2)}) %collective-permute-start.1) | collective-permute-done | bytes 172064 | tf_op jit(solution)/shard_map/ppermute | solution.py:313
  11.4 1.7 %collective-permute-start.6 = (bf16[168,512]{1,0:T(8,128)(2,1)S(1)}, bf16[168,512]{1,0:T(8,128)(2,1)S(1)}, u32[]{:S(2)}, u32[]{:S(2)}) collective-permute-start(bf16[168,512]{1,0:T(8,128)(2,1)S(1)} %get-tuple-element.19), channel_id=1, source_target_pairs={{0,28},{4,24},{8,20},{12,16},{16,12},{20,8},{24,4},{28,0},{1,29},{... | collective-permute-start | bytes 516104 | tf_op jit(solution)/shard_map/ppermute | solution.py:313
  13.2 1.4 %collective-permute-done.2.refs_4_ = bf16[168,512]{1,0:T(8,128)(2,1)S(1)} collective-permute-done((bf16[168,512]{1,0:T(8,128)(2,1)S(1)}, bf16[168,512]{1,0:T(8,128)(2,1)S(1)}, u32[]{:S(2)}, u32[]{:S(2)}) %collective-permute-start.2) | collective-permute-done | bytes 172064 | tf_op jit(solution)/shard_map/ppermute | solution.py:313
  14.6 0.0 collective-permute-done.3.refs_5_
  14.6 0.0 copy-start
  14.6 1.0 %copy-done = bf16[2,256,512]{2,1,0:T(8,128)(2,1)S(1)} copy-done((bf16[2,256,512]{2,1,0:T(8,128)(2,1)S(1)}, bf16[2,256,512]{2,1,0:T(8,128)(2,1)}, u32[]{:S(2)}) %copy-start) | copy-done | bytes 524312
  15.7 4.6 %add.1.refs_2_ = f32[1312,512]{1,0:T(8,128)S(1)} custom-call(bf16[512,512]{1,0:T(8,128)(2,1)S(1)} %bitcast.4, bf16[168,512]{1,0:T(8,128)(2,1)S(1)} %get-tuple-element.12.refs_1_, bf16[168,512]{1,0:T(8,128)(2,1)S(1)} %collective-permute-done.refs_2_, bf16[168,512]{1,0:T(8,128)(2,1)S(1)} %collective-permute-done.1.refs_3_, ...), custom_call_target="tpu_custom_call" | custom-call | tf_op jit(solution)/shard_map/add/pallas_call | solution.py:371
  20.3 3.0 %collective-permute-done.4.refs_3_ = bf16[168,512]{1,0:T(8,128)(2,1)S(1)} collective-permute-done((bf16[168,512]{1,0:T(8,128)(2,1)S(1)}, bf16[168,512]{1,0:T(8,128)(2,1)S(1)}, u32[]{:S(2)}, u32[]{:S(2)}) %collective-permute-start.4) | collective-permute-done | bytes 172064 | tf_op jit(solution)/shard_map/ppermute | solution.py:313
  23.2 0.0 collective-permute-done.5.refs_4_
  23.2 0.0 collective-permute-done.6.refs_5_
  23.2 0.0 copy-done.1
  23.3 3.9 %owner.1 = (bf16[128,256]{1,0:T(8,128)(2,1)S(1)}, f32[2,32,256]{2,1,0:T(8,128)S(1)}) custom-call(f32[40]{0:T(128)S(1)} %copy-done.1, bf16[512,512]{1,0:T(8,128)(2,1)S(1)} %bitcast.5, f32[1312,512]{1,0:T(8,128)S(1)} %add.1.refs_2_, bf16[168,512]{1,0:T(8,128)(2,1)S(1)} %collective-permute-done.4.refs_3_, bf16[168,512]{1,0:T(8,128)(2,1)S(1)} %collective-permute-done.5.refs_4_, ...), custom_call_target="tpu_custom_call" | custom-call | tf_op jit(solution)/shard_map/owner/pallas_call | solution.py:385
  27.1 4.1 %collective-permute-start.9 = (bf16[128,256]{1,0:T(8,128)(2,1)S(1)}, bf16[128,256]{1,0:T(8,128)(2,1)S(1)}, u32[]{:S(2)}, u32[]{:S(2)}) collective-permute-start(bf16[128,256]{1,0:T(8,128)(2,1)S(1)} %get-tuple-element.21.refs_1_), channel_id=1, source_target_pairs={{0,3},{1,0},{2,1},{3,2},{4,7},{5,4},{6,5},{7,6},{8,11},{9,8},{10,9... | collective-permute-start | bytes 196616 | tf_op jit(solution)/shard_map/ppermute | solution.py:308
  31.2 0.0 collective-permute-start.8
  31.2 1.0 %collective-permute-start.7 = (bf16[128,256]{1,0:T(8,128)(2,1)S(1)}, bf16[128,256]{1,0:T(8,128)(2,1)S(1)}, u32[]{:S(2)}, u32[]{:S(2)}) collective-permute-start(bf16[128,256]{1,0:T(8,128)(2,1)S(1)} %get-tuple-element.21.refs_1_), channel_id=1, source_target_pairs={{0,1},{1,2},{2,3},{3,0},{4,5},{5,6},{6,7},{7,4},{8,9},{9,10},{10,1... | collective-permute-start | bytes 196616 | tf_op jit(solution)/shard_map/ppermute | solution.py:308
  32.2 1.4 %collective-permute-done.9.refs_4_ = bf16[128,256]{1,0:T(8,128)(2,1)S(1)} collective-permute-done((bf16[128,256]{1,0:T(8,128)(2,1)S(1)}, bf16[128,256]{1,0:T(8,128)(2,1)S(1)}, u32[]{:S(2)}, u32[]{:S(2)}) %collective-permute-start.9) | collective-permute-done | bytes 65568 | tf_op jit(solution)/shard_map/ppermute | solution.py:308
  33.6 4.6 %collective-permute-done.8.refs_3_ = bf16[128,256]{1,0:T(8,128)(2,1)S(1)} collective-permute-done((bf16[128,256]{1,0:T(8,128)(2,1)S(1)}, bf16[128,256]{1,0:T(8,128)(2,1)S(1)}, u32[]{:S(2)}, u32[]{:S(2)}) %collective-permute-start.8) | collective-permute-done | bytes 65568 | tf_op jit(solution)/shard_map/ppermute | solution.py:308
  38.2 0.0 collective-permute-done.7.refs_2_
  38.2 3.2 %fit.1 = (f32[2,32,256]{2,1,0:T(8,128)}, f32[2,32]{1,0:T(2,128)}) custom-call(f32[2,32,256]{2,1,0:T(8,128)S(1)} %get-tuple-element.20.refs_0_, bf16[128,256]{1,0:T(8,128)(2,1)S(1)} %get-tuple-element.21.refs_1_, bf16[128,256]{1,0:T(8,128)(2,1)S(1)} %collective-permute-done.7.refs_2_, bf16[128,256]{1,0:T(8,128)(2,1)S(1)} %collective-permute-done.8.refs_3_, ...), custom_call_target="tpu_custom_call" | custom-call | tf_op jit(solution)/shard_map/fit/pallas_call | solution.py:398
Async XLA Ops:
  0.6 22.6 %copy-start.1 = (f32[40]{0:T(128)S(1)}, f32[40]{0:T(128)}, u32[]{:S(2)}) copy-start(f32[40]{0:T(128)} %refs_0_.1) | copy-start | bytes 484
  3.1 4.9 %collective-permute-start = (bf16[168,512]{1,0:T(8,128)(2,1)S(1)}, bf16[168,512]{1,0:T(8,128)(2,1)S(1)}, u32[]{:S(2)}, u32[]{:S(2)}) collective-permute-start(bf16[168,512]{1,0:T(8,128)(2,1)S(1)} %get-tuple-element.13), channel_id=1, source_target_pairs={{0,4},{4,0},{8,12},{12,8},{16,20},{20,16},{24,28},{28,24},{1,5},{5... | collective-permute-start | bytes 516104 | tf_op jit(solution)/shard_map/ppermute | solution.py:313
  3.7 7.8 %collective-permute-start.1 = (bf16[168,512]{1,0:T(8,128)(2,1)S(1)}, bf16[168,512]{1,0:T(8,128)(2,1)S(1)}, u32[]{:S(2)}, u32[]{:S(2)}) collective-permute-start(bf16[168,512]{1,0:T(8,128)(2,1)S(1)} %get-tuple-element.14), channel_id=1, source_target_pairs={{0,8},{4,12},{8,0},{12,4},{16,24},{20,28},{24,16},{28,20},{1,9},{5... | collective-permute-start | bytes 516104 | tf_op jit(solution)/shard_map/ppermute | solution.py:313
  6.2 8.4 %collective-permute-start.2 = (bf16[168,512]{1,0:T(8,128)(2,1)S(1)}, bf16[168,512]{1,0:T(8,128)(2,1)S(1)}, u32[]{:S(2)}, u32[]{:S(2)}) collective-permute-start(bf16[168,512]{1,0:T(8,128)(2,1)S(1)} %get-tuple-element.15), channel_id=1, source_target_pairs={{0,12},{4,8},{8,4},{12,0},{16,28},{20,24},{24,20},{28,16},{1,13},{... | collective-permute-start | bytes 516104 | tf_op jit(solution)/shard_map/ppermute | solution.py:313
  6.3 8.3 %collective-permute-start.3 = (bf16[168,512]{1,0:T(8,128)(2,1)S(1)}, bf16[168,512]{1,0:T(8,128)(2,1)S(1)}, u32[]{:S(2)}, u32[]{:S(2)}) collective-permute-start(bf16[168,512]{1,0:T(8,128)(2,1)S(1)} %get-tuple-element.16), channel_id=1, source_target_pairs={{0,16},{4,20},{8,24},{12,28},{16,0},{20,4},{24,8},{28,12},{1,17},{... | collective-permute-start | bytes 516104 | tf_op jit(solution)/shard_map/ppermute | solution.py:313
  8.1 15.2 %collective-permute-start.4 = (bf16[168,512]{1,0:T(8,128)(2,1)S(1)}, bf16[168,512]{1,0:T(8,128)(2,1)S(1)}, u32[]{:S(2)}, u32[]{:S(2)}) collective-permute-start(bf16[168,512]{1,0:T(8,128)(2,1)S(1)} %get-tuple-element.17), channel_id=1, source_target_pairs={{0,20},{4,16},{8,28},{12,24},{16,4},{20,0},{24,12},{28,8},{1,21},{... | collective-permute-start | bytes 516104 | tf_op jit(solution)/shard_map/ppermute | solution.py:313
  8.1 15.2 %collective-permute-start.5 = (bf16[168,512]{1,0:T(8,128)(2,1)S(1)}, bf16[168,512]{1,0:T(8,128)(2,1)S(1)}, u32[]{:S(2)}, u32[]{:S(2)}) collective-permute-start(bf16[168,512]{1,0:T(8,128)(2,1)S(1)} %get-tuple-element.18), channel_id=1, source_target_pairs={{0,24},{4,28},{8,16},{12,20},{16,8},{20,12},{24,0},{28,4},{1,25},{... | collective-permute-start | bytes 516104 | tf_op jit(solution)/shard_map/ppermute | solution.py:313
  11.4 11.8 %collective-permute-start.6 = (bf16[168,512]{1,0:T(8,128)(2,1)S(1)}, bf16[168,512]{1,0:T(8,128)(2,1)S(1)}, u32[]{:S(2)}, u32[]{:S(2)}) collective-permute-start(bf16[168,512]{1,0:T(8,128)(2,1)S(1)} %get-tuple-element.19), channel_id=1, source_target_pairs={{0,28},{4,24},{8,20},{12,16},{16,12},{20,8},{24,4},{28,0},{1,29},{... | collective-permute-start | bytes 516104 | tf_op jit(solution)/shard_map/ppermute | solution.py:313
  14.6 1.0 %copy-start = (bf16[2,256,512]{2,1,0:T(8,128)(2,1)S(1)}, bf16[2,256,512]{2,1,0:T(8,128)(2,1)}, u32[]{:S(2)}) copy-start(bf16[2,256,512]{2,1,0:T(8,128)(2,1)} %param.7) | copy-start | bytes 1572868
  27.1 6.5 %collective-permute-start.9 = (bf16[128,256]{1,0:T(8,128)(2,1)S(1)}, bf16[128,256]{1,0:T(8,128)(2,1)S(1)}, u32[]{:S(2)}, u32[]{:S(2)}) collective-permute-start(bf16[128,256]{1,0:T(8,128)(2,1)S(1)} %get-tuple-element.21.refs_1_), channel_id=1, source_target_pairs={{0,3},{1,0},{2,1},{3,2},{4,7},{5,4},{6,5},{7,6},{8,11},{9,8},{10,9... | collective-permute-start | bytes 196616 | tf_op jit(solution)/shard_map/ppermute | solution.py:308
  31.2 7.0 %collective-permute-start.8 = (bf16[128,256]{1,0:T(8,128)(2,1)S(1)}, bf16[128,256]{1,0:T(8,128)(2,1)S(1)}, u32[]{:S(2)}, u32[]{:S(2)}) collective-permute-start(bf16[128,256]{1,0:T(8,128)(2,1)S(1)} %get-tuple-element.21.refs_1_), channel_id=1, source_target_pairs={{0,2},{1,3},{2,0},{3,1},{4,6},{5,7},{6,4},{7,5},{8,10},{9,11},{10,... | collective-permute-start | bytes 196616 | tf_op jit(solution)/shard_map/ppermute | solution.py:308
  31.2 7.0 %collective-permute-start.7 = (bf16[128,256]{1,0:T(8,128)(2,1)S(1)}, bf16[128,256]{1,0:T(8,128)(2,1)S(1)}, u32[]{:S(2)}, u32[]{:S(2)}) collective-permute-start(bf16[128,256]{1,0:T(8,128)(2,1)S(1)} %get-tuple-element.21.refs_1_), channel_id=1, source_target_pairs={{0,1},{1,2},{2,3},{3,0},{4,5},{5,6},{6,7},{7,4},{8,9},{9,10},{10,1... | collective-permute-start | bytes 196616 | tf_op jit(solution)/shard_map/ppermute | solution.py:308

commit v5 on v4

--- a/solution.py
+++ b/solution.py
@@ -13,6 +13,7 @@
 NF = NB - 2
 META = 8
 EARLY = 5
+ORDER = (0, 2, 4, 3, 1, 5, 6, 7)
 STEP = 8
 HALF = 256
 
@@ -57,7 +58,7 @@
     return out
 
 
-def pack_kernel(owners, cap, set_count, me_ref, *refs):
+def pack_kernel(owners, order, cap, set_count, me_ref, *refs):
     outs, held, arrived = refs[5:-6], refs[-6:-1], refs[-1]
     copies = [pltpu.make_async_copy(refs[i], held[i], arrived.at[i]) for i in range(5)]
     for copy in copies:
@@ -88,7 +89,7 @@
     for base in range(0, owners, group):
         chosen, places = range(base, base + group), []
         for k in chosen:
-            spot = target - (me_ref[0] ^ k) * cap
+            spot = target - (me_ref[0] ^ order[k]) * cap
             spot = jnp.where((spot >= 0) & (spot < cap), spot + (k * cap) % 128, -1)
             places.append(jnp.where(iota((HALF, trades), 0) == spot, 1.0, 0.0).astype(BF16))
         aligned = (group * cap) % 128 == 0 and cap % 16 == 0
@@ -327,6 +328,7 @@
     count = owners * cap
     block = (cap + META, factors)
     few = owners <= 8
+    order = ORDER if owners == len(ORDER) else tuple(range(owners))
     me = lax.axis_index("trades").astype(jnp.int32)
     if few:
         shape = [pltpu.VMEM(block, BF16)] * owners
@@ -341,7 +343,7 @@
         trade_loads,
     )
     packed = pl.pallas_call(
-        lambda *refs: pack_kernel(owners, cap, set_count, *refs),
+        lambda *refs: pack_kernel(owners, order, cap, set_count, *refs),
         out_shape=shape,
         in_specs=[smem()] + [pl.BlockSpec(memory_space=pltpu.HBM)] * 5,
         out_specs=vmem(len(shape)),
@@ -365,7 +367,7 @@
 
     at, sofar = 0, []
     if few:
-        got = [near(packed[0])] + [meet(packed[k], "trades", k) for k in range(1, owners)]
+        got = [near(packed[0])] + [meet(packed[k], "trades", order[k]) for k in range(1, owners)]
         if owners > EARLY:
             at = EARLY
             sofar = pl.pallas_call(
@@ -394,7 +396,7 @@
         compiler_params=params(),
         name="owner",
     )(risk_weights, states, *sofar, *last)
-    parts = [near(mine)] + [turn(mine, "paths", k) for k in range(1, groups)]
+    parts = [near(mine)] + [meet(mine, "paths", k) for k in range(1, groups)]
     fitted_margin, exposure = pl.pallas_call(
         lambda *refs: fit_kernel(groups, set_count, *refs),
         out_shape=[

time: 41.6 us -> 39.4 us (0.947)
  starting transfers between devices: 14.3 us -> 13.2 us
  waiting for transfers between devices: 11.2 us -> 10.1 us
    ppermute x3 -> x0, waiting for transfers between devices: 5.98 us -> none  [turn(): return near(lax.ppermute(x, axis, [(i, (i + k) % n) for i in range(n)]))]
    ppermute x3 -> x0, starting transfers between devices: 5.09 us -> none  [turn(): return near(lax.ppermute(x, axis, [(i, (i + k) % n) for i in range(n)]))]
    ppermute x7 -> x10, waiting for transfers between devices: 5.2 us -> 10.1 us  [meet(): return near(lax.ppermute(x, axis, [(i, i ^ k) for i in range(n)]))]
    ppermute x7 -> x10, starting transfers between devices: 9.26 us -> 13.2 us  [meet(): return near(lax.ppermute(x, axis, [(i, i ^ k) for i in range(n)]))]
  transfers between devices with their start and end apart: 10 -> 10, of which waited for: 5 -> 5; matrix products, arithmetic and copies ran while one was open for 0% -> 0% of each run, Pallas kernels for 11% -> 12%
where the time goes in v5:
time: 39.4 us; the launch traced here: 39.2 us
  Pallas kernels  14.2 us (36%)
  starting transfers between devices  13.2 us (34%)
  waiting for transfers between devices  10.1 us (26%)
  local copies, waits for them, and re-layouts  1.05 us (3%)
  between operations  0.68 us (2%)
    ppermute x10, starting transfers between devices, meet(): return near(lax.ppermute(x, axis, [(i, i ^ k) for i in range(n)]))  13.2 us
    ppermute x10, waiting for transfers between devices, meet(): return near(lax.ppermute(x, axis, [(i, i ^ k) for i in range(n)]))  10.1 us
    pallas_call x1, Pallas kernels, on_device(): pl.pallas_call(lambda *refs: add_kernel(cap, set_count, *refs), out_shape...  4.61 us
    pallas_call x1, Pallas kernels, on_device(): pl.pallas_call(lambda *refs: owner_kernel(owners, at, cap, set_count, *re...  3.87 us
    pallas_call x1, Pallas kernels, on_device(): pl.pallas_call(lambda *refs: fit_kernel(groups, set_count, *refs), out_sh...  3.2 us
    pallas_call x1, Pallas kernels, on_device(): pl.pallas_call(lambda *refs: pack_kernel(owners, order, cap, set_count, *...  2.47 us
    unnamed x4, local copies, waits for them, and re-layouts  1.05 us
  transfers between devices with their start and end apart: 10, of which 5 were waited for; matrix products, arithmetic and copies ran while one was open for 0% of the time, Pallas kernels for 12%

profile of v5, /device:TPU:0, one launch (start us, length us, event | category | flops | bytes accessed | tf_op | source)
XLA Modules:
  0.0 39.2 jit_solution(16538827631084472422)
XLA Ops:
  0.6 0.0 copy-start.1
  0.6 2.5 %pack.1 = (bf16[168,512]{1,0:T(8,128)(2,1)S(1)}, bf16[168,512]{1,0:T(8,128)(2,1)S(1)}, bf16[168,512]{1,0:T(8,128)(2,1)S(1)}, bf16[168,512]{1,0:T(8,128)(2,1)S(1)...) custom-call(s32[1]{0:T(128)} %bitcast.1.refs_0_, ...), custom_call_target="tpu_custom_call" | custom-call | tf_op jit(solution)/shard_map/pack/pallas_call | solution.py:345
  3.1 3.0 %collective-permute-start = (bf16[168,512]{1,0:T(8,128)(2,1)S(1)}, bf16[168,512]{1,0:T(8,128)(2,1)S(1)}, u32[]{:S(2)}, u32[]{:S(2)}) collective-permute-start(bf16[168,512]{1,0:T(8,128)(2,1)S(1)} %get-tuple-element.13), channel_id=1, source_target_pairs={{0,8},{4,12},{8,0},{12,4},{16,24},{20,28},{24,16},{28,20},{1,9},{5... | collective-permute-start | bytes 516104 | tf_op jit(solution)/shard_map/ppermute | solution.py:314
  6.1 1.5 %collective-permute-start.1 = (bf16[168,512]{1,0:T(8,128)(2,1)S(1)}, bf16[168,512]{1,0:T(8,128)(2,1)S(1)}, u32[]{:S(2)}, u32[]{:S(2)}) collective-permute-start(bf16[168,512]{1,0:T(8,128)(2,1)S(1)} %get-tuple-element.14), channel_id=1, source_target_pairs={{0,16},{4,20},{8,24},{12,28},{16,0},{20,4},{24,8},{28,12},{1,17},{... | collective-permute-start | bytes 516104 | tf_op jit(solution)/shard_map/ppermute | solution.py:314
  7.7 0.0 collective-permute-start.2
  7.7 0.6 %collective-permute-start.3 = (bf16[168,512]{1,0:T(8,128)(2,1)S(1)}, bf16[168,512]{1,0:T(8,128)(2,1)S(1)}, u32[]{:S(2)}, u32[]{:S(2)}) collective-permute-start(bf16[168,512]{1,0:T(8,128)(2,1)S(1)} %get-tuple-element.16), channel_id=1, source_target_pairs={{0,4},{4,0},{8,12},{12,8},{16,20},{20,16},{24,28},{28,24},{1,5},{5... | collective-permute-start | bytes 516104 | tf_op jit(solution)/shard_map/ppermute | solution.py:314
  8.3 0.0 collective-permute-start.4
  8.3 2.5 %collective-permute-done.refs_2_ = bf16[168,512]{1,0:T(8,128)(2,1)S(1)} collective-permute-done((bf16[168,512]{1,0:T(8,128)(2,1)S(1)}, bf16[168,512]{1,0:T(8,128)(2,1)S(1)}, u32[]{:S(2)}, u32[]{:S(2)}) %collective-permute-start) | collective-permute-done | bytes 172064 | tf_op jit(solution)/shard_map/ppermute | solution.py:314
  10.8 3.6 %collective-permute-start.5 = (bf16[168,512]{1,0:T(8,128)(2,1)S(1)}, bf16[168,512]{1,0:T(8,128)(2,1)S(1)}, u32[]{:S(2)}, u32[]{:S(2)}) collective-permute-start(bf16[168,512]{1,0:T(8,128)(2,1)S(1)} %get-tuple-element.18), channel_id=1, source_target_pairs={{0,24},{4,28},{8,16},{12,20},{16,8},{20,12},{24,0},{28,4},{1,25},{... | collective-permute-start | bytes 516104 | tf_op jit(solution)/shard_map/ppermute | solution.py:314
  14.4 0.0 collective-permute-done.1.refs_3_
  14.4 0.0 collective-permute-start.6
  14.4 0.1 collective-permute-done.2.refs_4_
  14.4 0.0 collective-permute-done.3.refs_5_
  14.5 0.0 copy-start
  14.5 1.0 %copy-done = bf16[2,256,512]{2,1,0:T(8,128)(2,1)S(1)} copy-done((bf16[2,256,512]{2,1,0:T(8,128)(2,1)S(1)}, bf16[2,256,512]{2,1,0:T(8,128)(2,1)}, u32[]{:S(2)}) %copy-start) | copy-done | bytes 524312
  15.5 4.6 %add.1.refs_2_ = f32[1312,512]{1,0:T(8,128)S(1)} custom-call(bf16[512,512]{1,0:T(8,128)(2,1)S(1)} %bitcast.4, bf16[168,512]{1,0:T(8,128)(2,1)S(1)} %get-tuple-element.12.refs_1_, bf16[168,512]{1,0:T(8,128)(2,1)S(1)} %collective-permute-done.refs_2_, bf16[168,512]{1,0:T(8,128)(2,1)S(1)} %collective-permute-done.1.refs_3_, ...), custom_call_target="tpu_custom_call" | custom-call | tf_op jit(solution)/shard_map/add/pallas_call | solution.py:373
  20.1 2.0 %collective-permute-done.4.refs_3_ = bf16[168,512]{1,0:T(8,128)(2,1)S(1)} collective-permute-done((bf16[168,512]{1,0:T(8,128)(2,1)S(1)}, bf16[168,512]{1,0:T(8,128)(2,1)S(1)}, u32[]{:S(2)}, u32[]{:S(2)}) %collective-permute-start.4) | collective-permute-done | bytes 172064 | tf_op jit(solution)/shard_map/ppermute | solution.py:314
  22.1 0.0 collective-permute-done.5.refs_4_
  22.1 0.0 collective-permute-done.6.refs_5_
  22.1 0.0 copy-done.1
  22.1 3.9 %owner.1 = (bf16[128,256]{1,0:T(8,128)(2,1)S(1)}, f32[2,32,256]{2,1,0:T(8,128)S(1)}) custom-call(f32[40]{0:T(128)S(1)} %copy-done.1, bf16[512,512]{1,0:T(8,128)(2,1)S(1)} %bitcast.5, f32[1312,512]{1,0:T(8,128)S(1)} %add.1.refs_2_, bf16[168,512]{1,0:T(8,128)(2,1)S(1)} %collective-permute-done.4.refs_3_, bf16[168,512]{1,0:T(8,128)(2,1)S(1)} %collective-permute-done.5.refs_4_, ...), custom_call_target="tpu_custom_call" | custom-call | tf_op jit(solution)/shard_map/owner/pallas_call | solution.py:387
  26.0 3.7 %collective-permute-start.9 = (bf16[128,256]{1,0:T(8,128)(2,1)S(1)}, bf16[128,256]{1,0:T(8,128)(2,1)S(1)}, u32[]{:S(2)}, u32[]{:S(2)}) collective-permute-start(bf16[128,256]{1,0:T(8,128)(2,1)S(1)} %get-tuple-element.21.refs_1_), channel_id=1, source_target_pairs={{0,3},{1,2},{2,1},{3,0},{4,7},{5,6},{6,5},{7,4},{8,11},{9,10},{10,... | collective-permute-start | bytes 196616 | tf_op jit(solution)/shard_map/ppermute | solution.py:314
  29.6 0.0 collective-permute-start.8
  29.6 0.8 %collective-permute-start.7 = (bf16[128,256]{1,0:T(8,128)(2,1)S(1)}, bf16[128,256]{1,0:T(8,128)(2,1)S(1)}, u32[]{:S(2)}, u32[]{:S(2)}) collective-permute-start(bf16[128,256]{1,0:T(8,128)(2,1)S(1)} %get-tuple-element.21.refs_1_), channel_id=1, source_target_pairs={{0,1},{1,0},{2,3},{3,2},{4,5},{5,4},{6,7},{7,6},{8,9},{9,8},{10,11... | collective-permute-start | bytes 196616 | tf_op jit(solution)/shard_map/ppermute | solution.py:314
  30.4 2.4 %collective-permute-done.9.refs_4_ = bf16[128,256]{1,0:T(8,128)(2,1)S(1)} collective-permute-done((bf16[128,256]{1,0:T(8,128)(2,1)S(1)}, bf16[128,256]{1,0:T(8,128)(2,1)S(1)}, u32[]{:S(2)}, u32[]{:S(2)}) %collective-permute-start.9) | collective-permute-done | bytes 65568 | tf_op jit(solution)/shard_map/ppermute | solution.py:314
  32.9 3.2 %collective-permute-done.8.refs_3_ = bf16[128,256]{1,0:T(8,128)(2,1)S(1)} collective-permute-done((bf16[128,256]{1,0:T(8,128)(2,1)S(1)}, bf16[128,256]{1,0:T(8,128)(2,1)S(1)}, u32[]{:S(2)}, u32[]{:S(2)}) %collective-permute-start.8) | collective-permute-done | bytes 65568 | tf_op jit(solution)/shard_map/ppermute | solution.py:314
  36.0 0.0 collective-permute-done.7.refs_2_
  36.0 3.2 %fit.1 = (f32[2,32,256]{2,1,0:T(8,128)}, f32[2,32]{1,0:T(2,128)}) custom-call(f32[2,32,256]{2,1,0:T(8,128)S(1)} %get-tuple-element.20.refs_0_, bf16[128,256]{1,0:T(8,128)(2,1)S(1)} %get-tuple-element.21.refs_1_, bf16[128,256]{1,0:T(8,128)(2,1)S(1)} %collective-permute-done.7.refs_2_, bf16[128,256]{1,0:T(8,128)(2,1)S(1)} %collective-permute-done.8.refs_3_, ...), custom_call_target="tpu_custom_call" | custom-call | tf_op jit(solution)/shard_map/fit/pallas_call | solution.py:400
Async XLA Ops:
  0.6 21.4 %copy-start.1 = (f32[40]{0:T(128)S(1)}, f32[40]{0:T(128)}, u32[]{:S(2)}) copy-start(f32[40]{0:T(128)} %refs_0_.1) | copy-start | bytes 484
  3.1 7.6 %collective-permute-start = (bf16[168,512]{1,0:T(8,128)(2,1)S(1)}, bf16[168,512]{1,0:T(8,128)(2,1)S(1)}, u32[]{:S(2)}, u32[]{:S(2)}) collective-permute-start(bf16[168,512]{1,0:T(8,128)(2,1)S(1)} %get-tuple-element.13), channel_id=1, source_target_pairs={{0,8},{4,12},{8,0},{12,4},{16,24},{20,28},{24,16},{28,20},{1,9},{5... | collective-permute-start | bytes 516104 | tf_op jit(solution)/shard_map/ppermute | solution.py:314
  6.1 8.2 %collective-permute-start.1 = (bf16[168,512]{1,0:T(8,128)(2,1)S(1)}, bf16[168,512]{1,0:T(8,128)(2,1)S(1)}, u32[]{:S(2)}, u32[]{:S(2)}) collective-permute-start(bf16[168,512]{1,0:T(8,128)(2,1)S(1)} %get-tuple-element.14), channel_id=1, source_target_pairs={{0,16},{4,20},{8,24},{12,28},{16,0},{20,4},{24,8},{28,12},{1,17},{... | collective-permute-start | bytes 516104 | tf_op jit(solution)/shard_map/ppermute | solution.py:314
  7.7 6.8 %collective-permute-start.2 = (bf16[168,512]{1,0:T(8,128)(2,1)S(1)}, bf16[168,512]{1,0:T(8,128)(2,1)S(1)}, u32[]{:S(2)}, u32[]{:S(2)}) collective-permute-start(bf16[168,512]{1,0:T(8,128)(2,1)S(1)} %get-tuple-element.15), channel_id=1, source_target_pairs={{0,12},{4,8},{8,4},{12,0},{16,28},{20,24},{24,20},{28,16},{1,13},{... | collective-permute-start | bytes 516104 | tf_op jit(solution)/shard_map/ppermute | solution.py:314
  7.7 6.8 %collective-permute-start.3 = (bf16[168,512]{1,0:T(8,128)(2,1)S(1)}, bf16[168,512]{1,0:T(8,128)(2,1)S(1)}, u32[]{:S(2)}, u32[]{:S(2)}) collective-permute-start(bf16[168,512]{1,0:T(8,128)(2,1)S(1)} %get-tuple-element.16), channel_id=1, source_target_pairs={{0,4},{4,0},{8,12},{12,8},{16,20},{20,16},{24,28},{28,24},{1,5},{5... | collective-permute-start | bytes 516104 | tf_op jit(solution)/shard_map/ppermute | solution.py:314
  8.3 13.8 %collective-permute-start.4 = (bf16[168,512]{1,0:T(8,128)(2,1)S(1)}, bf16[168,512]{1,0:T(8,128)(2,1)S(1)}, u32[]{:S(2)}, u32[]{:S(2)}) collective-permute-start(bf16[168,512]{1,0:T(8,128)(2,1)S(1)} %get-tuple-element.17), channel_id=1, source_target_pairs={{0,20},{4,16},{8,28},{12,24},{16,4},{20,0},{24,12},{28,8},{1,21},{... | collective-permute-start | bytes 516104 | tf_op jit(solution)/shard_map/ppermute | solution.py:314
  10.8 11.3 %collective-permute-start.5 = (bf16[168,512]{1,0:T(8,128)(2,1)S(1)}, bf16[168,512]{1,0:T(8,128)(2,1)S(1)}, u32[]{:S(2)}, u32[]{:S(2)}) collective-permute-start(bf16[168,512]{1,0:T(8,128)(2,1)S(1)} %get-tuple-element.18), channel_id=1, source_target_pairs={{0,24},{4,28},{8,16},{12,20},{16,8},{20,12},{24,0},{28,4},{1,25},{... | collective-permute-start | bytes 516104 | tf_op jit(solution)/shard_map/ppermute | solution.py:314
  14.4 7.7 %collective-permute-start.6 = (bf16[168,512]{1,0:T(8,128)(2,1)S(1)}, bf16[168,512]{1,0:T(8,128)(2,1)S(1)}, u32[]{:S(2)}, u32[]{:S(2)}) collective-permute-start(bf16[168,512]{1,0:T(8,128)(2,1)S(1)} %get-tuple-element.19), channel_id=1, source_target_pairs={{0,28},{4,24},{8,20},{12,16},{16,12},{20,8},{24,4},{28,0},{1,29},{... | collective-permute-start | bytes 516104 | tf_op jit(solution)/shard_map/ppermute | solution.py:314
  14.5 1.0 %copy-start = (bf16[2,256,512]{2,1,0:T(8,128)(2,1)S(1)}, bf16[2,256,512]{2,1,0:T(8,128)(2,1)}, u32[]{:S(2)}) copy-start(bf16[2,256,512]{2,1,0:T(8,128)(2,1)} %param.7) | copy-start | bytes 1572868
  26.0 6.9 %collective-permute-start.9 = (bf16[128,256]{1,0:T(8,128)(2,1)S(1)}, bf16[128,256]{1,0:T(8,128)(2,1)S(1)}, u32[]{:S(2)}, u32[]{:S(2)}) collective-permute-start(bf16[128,256]{1,0:T(8,128)(2,1)S(1)} %get-tuple-element.21.refs_1_), channel_id=1, source_target_pairs={{0,3},{1,2},{2,1},{3,0},{4,7},{5,6},{6,5},{7,4},{8,11},{9,10},{10,... | collective-permute-start | bytes 196616 | tf_op jit(solution)/shard_map/ppermute | solution.py:314
  29.6 6.4 %collective-permute-start.8 = (bf16[128,256]{1,0:T(8,128)(2,1)S(1)}, bf16[128,256]{1,0:T(8,128)(2,1)S(1)}, u32[]{:S(2)}, u32[]{:S(2)}) collective-permute-start(bf16[128,256]{1,0:T(8,128)(2,1)S(1)} %get-tuple-element.21.refs_1_), channel_id=1, source_target_pairs={{0,2},{1,3},{2,0},{3,1},{4,6},{5,7},{6,4},{7,5},{8,10},{9,11},{10,... | collective-permute-start | bytes 196616 | tf_op jit(solution)/shard_map/ppermute | solution.py:314
  29.6 6.4 %collective-permute-start.7 = (bf16[128,256]{1,0:T(8,128)(2,1)S(1)}, bf16[128,256]{1,0:T(8,128)(2,1)S(1)}, u32[]{:S(2)}, u32[]{:S(2)}) collective-permute-start(bf16[128,256]{1,0:T(8,128)(2,1)S(1)} %get-tuple-element.21.refs_1_), channel_id=1, source_target_pairs={{0,1},{1,0},{2,3},{3,2},{4,5},{5,4},{6,7},{7,6},{8,9},{9,8},{10,11... | collective-permute-start | bytes 196616 | tf_op jit(solution)/shard_map/ppermute | solution.py:314

commit v6 on v5

--- a/solution.py
+++ b/solution.py
@@ -14,7 +14,7 @@
 META = 8
 EARLY = 5
 ORDER = (0, 2, 4, 3, 1, 5, 6, 7)
-STEP = 8
+STEP = 4
 HALF = 256
 
 CORR_LEN = 8.0
@@ -239,31 +239,33 @@
     total = sum(p[base : base + 2 * NB, :].astype(F32) for p in parts)
     total = total[0:NB, 0:width] + total[0:NB, width : 2 * width] + total[NB : 2 * NB, 0:width]
     shape = (NB, width)
-    row, lane = iota(shape, 0), iota(shape, 1)
+    row = iota(shape, 0)
     shift = 2 * set_count
-    bases, sums, works = [], [], []
+    bases, sums, works, columns, scales = [], [], [], [], []
     for d in range(DATES):
         first = DATES * set_count + d * NB
         basis = jnp.concatenate([p[first : first + NB, :] for p in parts], axis=1)
-        blank = jnp.zeros((shift, basis.shape[1]), BF16)
-        placed = jnp.concatenate([blank, basis, blank[: width - shift - NB]], axis=0)
-        gram = dot_nt(basis, placed)
-        gram = jnp.where(lane - shift == row, gram + ridge, gram)
+        gram = dot_nt(basis, basis)
+        gram = jnp.where(iota((NB, NB), 0) == iota((NB, NB), 1), gram + ridge, gram)
         part = pltpu.roll(total, width - d * shift, 1) if d else total
         bases.append(basis)
         sums.append(part)
-        works.append(jnp.where(lane < shift, jnp.where(row < NB - 1, part, 0.0), gram))
+        works.append(jnp.where(row < NB - 1, part, 0.0))
+        columns.append([jnp.broadcast_to(gram[:, j : j + 1], shape) for j in range(NB - 1)])
+        scales.append(jnp.zeros(shape, F32))
     for j in range(NB - 1):
         for d in range(DATES):
-            work = works[d]
-            col = jnp.broadcast_to(work[:, shift + j : shift + j + 1], shape)
-            inv = 1.0 / jnp.broadcast_to(col[j : j + 1, :], shape)
-            pivot = jnp.broadcast_to(work[j : j + 1, :], shape) * inv
-            works[d] = jnp.where(row == j, pivot, work - col * pivot)
+            column = columns[d]
+            inv = 1.0 / jnp.broadcast_to(column[j][j : j + 1, :], shape)
+            factor = jnp.where(row == j, 0.0, column[j] * inv)
+            scales[d] = jnp.where(row == j, inv, scales[d])
+            for k in range(j + 1, NB - 1):
+                column[k] = column[k] - factor * jnp.broadcast_to(column[k][j : j + 1, :], shape)
+            works[d] = works[d] - factor * jnp.broadcast_to(works[d][j : j + 1, :], shape)
     flats = []
     for d in range(DATES):
         part, basis = sums[d], bases[d]
-        right = jnp.where(row < NB - 1, works[d], 0.0)
+        right = works[d] * scales[d]
         solved = pltpu.roll(right, width - set_count, 1)
         square = part[NB - 1 : NB] + ridge
         cross = pltpu.roll(part[NB - 1 : NB], width - set_count, 1)

time: 39.4 us -> 37.8 us (0.959)
  Pallas kernels: 14.2 us -> 12.6 us
    pallas_call x1, Pallas kernels: 3.2 us -> 1.67 us  [on_device(): pl.pallas_call(lambda *refs: fit_kernel(groups, set_count, *refs), out_sh...]
where the time goes in v6:
time: 37.8 us; the launch traced here: 37.7 us
  starting transfers between devices  13.2 us (35%)
  Pallas kernels  12.6 us (33%)
  waiting for transfers between devices  10.1 us (27%)
  local copies, waits for them, and re-layouts  1.05 us (3%)
  between operations  0.68 us (2%)
    ppermute x10, starting transfers between devices, meet(): return near(lax.ppermute(x, axis, [(i, i ^ k) for i in range(n)]))  13.2 us
    ppermute x10, waiting for transfers between devices, meet(): return near(lax.ppermute(x, axis, [(i, i ^ k) for i in range(n)]))  10.1 us
    pallas_call x1, Pallas kernels, on_device(): pl.pallas_call(lambda *refs: add_kernel(cap, set_count, *refs), out_shape...  4.62 us
    pallas_call x1, Pallas kernels, on_device(): pl.pallas_call(lambda *refs: owner_kernel(owners, at, cap, set_count, *re...  3.83 us
    pallas_call x1, Pallas kernels, on_device(): pl.pallas_call(lambda *refs: pack_kernel(owners, order, cap, set_count, *...  2.47 us
    pallas_call x1, Pallas kernels, on_device(): pl.pallas_call(lambda *refs: fit_kernel(groups, set_count, *refs), out_sh...  1.67 us
    unnamed x4, local copies, waits for them, and re-layouts  1.05 us
  transfers between devices with their start and end apart: 10, of which 5 were waited for; matrix products, arithmetic and copies ran while one was open for 0% of the time, Pallas kernels for 12%

profile of v6, /device:TPU:0, one launch (start us, length us, event | category | flops | bytes accessed | tf_op | source)
XLA Modules:
  0.0 37.7 jit_solution(10813594747312147580)
XLA Ops:
  0.6 0.0 copy-start.1
  0.6 2.5 %pack.1 = (bf16[168,512]{1,0:T(8,128)(2,1)S(1)}, bf16[168,512]{1,0:T(8,128)(2,1)S(1)}, bf16[168,512]{1,0:T(8,128)(2,1)S(1)}, bf16[168,512]{1,0:T(8,128)(2,1)S(1)...) custom-call(s32[1]{0:T(128)} %bitcast.1.refs_0_, ...), custom_call_target="tpu_custom_call" | custom-call | tf_op jit(solution)/shard_map/pack/pallas_call | solution.py:347
  3.1 3.0 %collective-permute-start = (bf16[168,512]{1,0:T(8,128)(2,1)S(1)}, bf16[168,512]{1,0:T(8,128)(2,1)S(1)}, u32[]{:S(2)}, u32[]{:S(2)}) collective-permute-start(bf16[168,512]{1,0:T(8,128)(2,1)S(1)} %get-tuple-element.13), channel_id=1, source_target_pairs={{0,8},{4,12},{8,0},{12,4},{16,24},{20,28},{24,16},{28,20},{1,9},{5... | collective-permute-start | bytes 516104 | tf_op jit(solution)/shard_map/ppermute | solution.py:316
  6.1 1.5 %collective-permute-start.1 = (bf16[168,512]{1,0:T(8,128)(2,1)S(1)}, bf16[168,512]{1,0:T(8,128)(2,1)S(1)}, u32[]{:S(2)}, u32[]{:S(2)}) collective-permute-start(bf16[168,512]{1,0:T(8,128)(2,1)S(1)} %get-tuple-element.14), channel_id=1, source_target_pairs={{0,16},{4,20},{8,24},{12,28},{16,0},{20,4},{24,8},{28,12},{1,17},{... | collective-permute-start | bytes 516104 | tf_op jit(solution)/shard_map/ppermute | solution.py:316
  7.7 0.0 collective-permute-start.2
  7.7 0.6 %collective-permute-start.3 = (bf16[168,512]{1,0:T(8,128)(2,1)S(1)}, bf16[168,512]{1,0:T(8,128)(2,1)S(1)}, u32[]{:S(2)}, u32[]{:S(2)}) collective-permute-start(bf16[168,512]{1,0:T(8,128)(2,1)S(1)} %get-tuple-element.16), channel_id=1, source_target_pairs={{0,4},{4,0},{8,12},{12,8},{16,20},{20,16},{24,28},{28,24},{1,5},{5... | collective-permute-start | bytes 516104 | tf_op jit(solution)/shard_map/ppermute | solution.py:316
  8.3 0.0 collective-permute-start.4
  8.3 2.5 %collective-permute-done.refs_2_ = bf16[168,512]{1,0:T(8,128)(2,1)S(1)} collective-permute-done((bf16[168,512]{1,0:T(8,128)(2,1)S(1)}, bf16[168,512]{1,0:T(8,128)(2,1)S(1)}, u32[]{:S(2)}, u32[]{:S(2)}) %collective-permute-start) | collective-permute-done | bytes 172064 | tf_op jit(solution)/shard_map/ppermute | solution.py:316
  10.8 3.6 %collective-permute-start.5 = (bf16[168,512]{1,0:T(8,128)(2,1)S(1)}, bf16[168,512]{1,0:T(8,128)(2,1)S(1)}, u32[]{:S(2)}, u32[]{:S(2)}) collective-permute-start(bf16[168,512]{1,0:T(8,128)(2,1)S(1)} %get-tuple-element.18), channel_id=1, source_target_pairs={{0,24},{4,28},{8,16},{12,20},{16,8},{20,12},{24,0},{28,4},{1,25},{... | collective-permute-start | bytes 516104 | tf_op jit(solution)/shard_map/ppermute | solution.py:316
  14.4 0.0 collective-permute-done.1.refs_3_
  14.4 0.0 collective-permute-start.6
  14.4 0.1 collective-permute-done.2.refs_4_
  14.4 0.0 collective-permute-done.3.refs_5_
  14.5 0.0 copy-start
  14.5 1.0 %copy-done = bf16[2,256,512]{2,1,0:T(8,128)(2,1)S(1)} copy-done((bf16[2,256,512]{2,1,0:T(8,128)(2,1)S(1)}, bf16[2,256,512]{2,1,0:T(8,128)(2,1)}, u32[]{:S(2)}) %copy-start) | copy-done | bytes 524312
  15.5 4.6 %add.1.refs_2_ = f32[1312,512]{1,0:T(8,128)S(1)} custom-call(bf16[512,512]{1,0:T(8,128)(2,1)S(1)} %bitcast.4, bf16[168,512]{1,0:T(8,128)(2,1)S(1)} %get-tuple-element.12.refs_1_, bf16[168,512]{1,0:T(8,128)(2,1)S(1)} %collective-permute-done.refs_2_, bf16[168,512]{1,0:T(8,128)(2,1)S(1)} %collective-permute-done.1.refs_3_, ...), custom_call_target="tpu_custom_call" | custom-call | tf_op jit(solution)/shard_map/add/pallas_call | solution.py:375
  20.1 1.9 %collective-permute-done.4.refs_3_ = bf16[168,512]{1,0:T(8,128)(2,1)S(1)} collective-permute-done((bf16[168,512]{1,0:T(8,128)(2,1)S(1)}, bf16[168,512]{1,0:T(8,128)(2,1)S(1)}, u32[]{:S(2)}, u32[]{:S(2)}) %collective-permute-start.4) | collective-permute-done | bytes 172064 | tf_op jit(solution)/shard_map/ppermute | solution.py:316
  22.1 0.0 collective-permute-done.5.refs_4_
  22.1 0.0 collective-permute-done.6.refs_5_
  22.1 0.0 copy-done.1
  22.1 3.8 %owner.1 = (bf16[128,256]{1,0:T(8,128)(2,1)S(1)}, f32[2,32,256]{2,1,0:T(8,128)S(1)}) custom-call(f32[40]{0:T(128)S(1)} %copy-done.1, bf16[512,512]{1,0:T(8,128)(2,1)S(1)} %bitcast.5, f32[1312,512]{1,0:T(8,128)S(1)} %add.1.refs_2_, bf16[168,512]{1,0:T(8,128)(2,1)S(1)} %collective-permute-done.4.refs_3_, bf16[168,512]{1,0:T(8,128)(2,1)S(1)} %collective-permute-done.5.refs_4_, ...), custom_call_target="tpu_custom_call" | custom-call | tf_op jit(solution)/shard_map/owner/pallas_call | solution.py:389
  25.9 3.7 %collective-permute-start.9 = (bf16[128,256]{1,0:T(8,128)(2,1)S(1)}, bf16[128,256]{1,0:T(8,128)(2,1)S(1)}, u32[]{:S(2)}, u32[]{:S(2)}) collective-permute-start(bf16[128,256]{1,0:T(8,128)(2,1)S(1)} %get-tuple-element.21.refs_1_), channel_id=1, source_target_pairs={{0,3},{1,2},{2,1},{3,0},{4,7},{5,6},{6,5},{7,4},{8,11},{9,10},{10,... | collective-permute-start | bytes 196616 | tf_op jit(solution)/shard_map/ppermute | solution.py:316
  29.6 0.0 collective-permute-start.8
  29.6 0.8 %collective-permute-start.7 = (bf16[128,256]{1,0:T(8,128)(2,1)S(1)}, bf16[128,256]{1,0:T(8,128)(2,1)S(1)}, u32[]{:S(2)}, u32[]{:S(2)}) collective-permute-start(bf16[128,256]{1,0:T(8,128)(2,1)S(1)} %get-tuple-element.21.refs_1_), channel_id=1, source_target_pairs={{0,1},{1,0},{2,3},{3,2},{4,5},{5,4},{6,7},{7,6},{8,9},{9,8},{10,11... | collective-permute-start | bytes 196616 | tf_op jit(solution)/shard_map/ppermute | solution.py:316
  30.4 2.4 %collective-permute-done.9.refs_4_ = bf16[128,256]{1,0:T(8,128)(2,1)S(1)} collective-permute-done((bf16[128,256]{1,0:T(8,128)(2,1)S(1)}, bf16[128,256]{1,0:T(8,128)(2,1)S(1)}, u32[]{:S(2)}, u32[]{:S(2)}) %collective-permute-start.9) | collective-permute-done | bytes 65568 | tf_op jit(solution)/shard_map/ppermute | solution.py:316
  32.8 3.2 %collective-permute-done.8.refs_3_ = bf16[128,256]{1,0:T(8,128)(2,1)S(1)} collective-permute-done((bf16[128,256]{1,0:T(8,128)(2,1)S(1)}, bf16[128,256]{1,0:T(8,128)(2,1)S(1)}, u32[]{:S(2)}, u32[]{:S(2)}) %collective-permute-start.8) | collective-permute-done | bytes 65568 | tf_op jit(solution)/shard_map/ppermute | solution.py:316
  36.0 0.0 collective-permute-done.7.refs_2_
  36.0 1.7 %fit.1 = (f32[2,32,256]{2,1,0:T(8,128)}, f32[2,32]{1,0:T(2,128)}) custom-call(f32[2,32,256]{2,1,0:T(8,128)S(1)} %get-tuple-element.20.refs_0_, bf16[128,256]{1,0:T(8,128)(2,1)S(1)} %get-tuple-element.21.refs_1_, bf16[128,256]{1,0:T(8,128)(2,1)S(1)} %collective-permute-done.7.refs_2_, bf16[128,256]{1,0:T(8,128)(2,1)S(1)} %collective-permute-done.8.refs_3_, ...), custom_call_target="tpu_custom_call" | custom-call | tf_op jit(solution)/shard_map/fit/pallas_call | solution.py:402
Async XLA Ops:
  0.6 21.4 %copy-start.1 = (f32[40]{0:T(128)S(1)}, f32[40]{0:T(128)}, u32[]{:S(2)}) copy-start(f32[40]{0:T(128)} %refs_0_.1) | copy-start | bytes 484
  3.1 7.6 %collective-permute-start = (bf16[168,512]{1,0:T(8,128)(2,1)S(1)}, bf16[168,512]{1,0:T(8,128)(2,1)S(1)}, u32[]{:S(2)}, u32[]{:S(2)}) collective-permute-start(bf16[168,512]{1,0:T(8,128)(2,1)S(1)} %get-tuple-element.13), channel_id=1, source_target_pairs={{0,8},{4,12},{8,0},{12,4},{16,24},{20,28},{24,16},{28,20},{1,9},{5... | collective-permute-start | bytes 516104 | tf_op jit(solution)/shard_map/ppermute | solution.py:316
  6.1 8.2 %collective-permute-start.1 = (bf16[168,512]{1,0:T(8,128)(2,1)S(1)}, bf16[168,512]{1,0:T(8,128)(2,1)S(1)}, u32[]{:S(2)}, u32[]{:S(2)}) collective-permute-start(bf16[168,512]{1,0:T(8,128)(2,1)S(1)} %get-tuple-element.14), channel_id=1, source_target_pairs={{0,16},{4,20},{8,24},{12,28},{16,0},{20,4},{24,8},{28,12},{1,17},{... | collective-permute-start | bytes 516104 | tf_op jit(solution)/shard_map/ppermute | solution.py:316
  7.7 6.8 %collective-permute-start.2 = (bf16[168,512]{1,0:T(8,128)(2,1)S(1)}, bf16[168,512]{1,0:T(8,128)(2,1)S(1)}, u32[]{:S(2)}, u32[]{:S(2)}) collective-permute-start(bf16[168,512]{1,0:T(8,128)(2,1)S(1)} %get-tuple-element.15), channel_id=1, source_target_pairs={{0,12},{4,8},{8,4},{12,0},{16,28},{20,24},{24,20},{28,16},{1,13},{... | collective-permute-start | bytes 516104 | tf_op jit(solution)/shard_map/ppermute | solution.py:316
  7.7 6.8 %collective-permute-start.3 = (bf16[168,512]{1,0:T(8,128)(2,1)S(1)}, bf16[168,512]{1,0:T(8,128)(2,1)S(1)}, u32[]{:S(2)}, u32[]{:S(2)}) collective-permute-start(bf16[168,512]{1,0:T(8,128)(2,1)S(1)} %get-tuple-element.16), channel_id=1, source_target_pairs={{0,4},{4,0},{8,12},{12,8},{16,20},{20,16},{24,28},{28,24},{1,5},{5... | collective-permute-start | bytes 516104 | tf_op jit(solution)/shard_map/ppermute | solution.py:316
  8.3 13.8 %collective-permute-start.4 = (bf16[168,512]{1,0:T(8,128)(2,1)S(1)}, bf16[168,512]{1,0:T(8,128)(2,1)S(1)}, u32[]{:S(2)}, u32[]{:S(2)}) collective-permute-start(bf16[168,512]{1,0:T(8,128)(2,1)S(1)} %get-tuple-element.17), channel_id=1, source_target_pairs={{0,20},{4,16},{8,28},{12,24},{16,4},{20,0},{24,12},{28,8},{1,21},{... | collective-permute-start | bytes 516104 | tf_op jit(solution)/shard_map/ppermute | solution.py:316
  10.8 11.3 %collective-permute-start.5 = (bf16[168,512]{1,0:T(8,128)(2,1)S(1)}, bf16[168,512]{1,0:T(8,128)(2,1)S(1)}, u32[]{:S(2)}, u32[]{:S(2)}) collective-permute-start(bf16[168,512]{1,0:T(8,128)(2,1)S(1)} %get-tuple-element.18), channel_id=1, source_target_pairs={{0,24},{4,28},{8,16},{12,20},{16,8},{20,12},{24,0},{28,4},{1,25},{... | collective-permute-start | bytes 516104 | tf_op jit(solution)/shard_map/ppermute | solution.py:316
  14.4 7.7 %collective-permute-start.6 = (bf16[168,512]{1,0:T(8,128)(2,1)S(1)}, bf16[168,512]{1,0:T(8,128)(2,1)S(1)}, u32[]{:S(2)}, u32[]{:S(2)}) collective-permute-start(bf16[168,512]{1,0:T(8,128)(2,1)S(1)} %get-tuple-element.19), channel_id=1, source_target_pairs={{0,28},{4,24},{8,20},{12,16},{16,12},{20,8},{24,4},{28,0},{1,29},{... | collective-permute-start | bytes 516104 | tf_op jit(solution)/shard_map/ppermute | solution.py:316
  14.5 1.0 %copy-start = (bf16[2,256,512]{2,1,0:T(8,128)(2,1)S(1)}, bf16[2,256,512]{2,1,0:T(8,128)(2,1)}, u32[]{:S(2)}) copy-start(bf16[2,256,512]{2,1,0:T(8,128)(2,1)} %param.7) | copy-start | bytes 1572868
  25.9 6.9 %collective-permute-start.9 = (bf16[128,256]{1,0:T(8,128)(2,1)S(1)}, bf16[128,256]{1,0:T(8,128)(2,1)S(1)}, u32[]{:S(2)}, u32[]{:S(2)}) collective-permute-start(bf16[128,256]{1,0:T(8,128)(2,1)S(1)} %get-tuple-element.21.refs_1_), channel_id=1, source_target_pairs={{0,3},{1,2},{2,1},{3,0},{4,7},{5,6},{6,5},{7,4},{8,11},{9,10},{10,... | collective-permute-start | bytes 196616 | tf_op jit(solution)/shard_map/ppermute | solution.py:316
  29.6 6.4 %collective-permute-start.8 = (bf16[128,256]{1,0:T(8,128)(2,1)S(1)}, bf16[128,256]{1,0:T(8,128)(2,1)S(1)}, u32[]{:S(2)}, u32[]{:S(2)}) collective-permute-start(bf16[128,256]{1,0:T(8,128)(2,1)S(1)} %get-tuple-element.21.refs_1_), channel_id=1, source_target_pairs={{0,2},{1,3},{2,0},{3,1},{4,6},{5,7},{6,4},{7,5},{8,10},{9,11},{10,... | collective-permute-start | bytes 196616 | tf_op jit(solution)/shard_map/ppermute | solution.py:316
  29.6 6.4 %collective-permute-start.7 = (bf16[128,256]{1,0:T(8,128)(2,1)S(1)}, bf16[128,256]{1,0:T(8,128)(2,1)S(1)}, u32[]{:S(2)}, u32[]{:S(2)}) collective-permute-start(bf16[128,256]{1,0:T(8,128)(2,1)S(1)} %get-tuple-element.21.refs_1_), channel_id=1, source_target_pairs={{0,1},{1,0},{2,3},{3,2},{4,5},{5,4},{6,7},{7,6},{8,9},{9,8},{10,11... | collective-permute-start | bytes 196616 | tf_op jit(solution)/shard_map/ppermute | solution.py:316

commit v7 on v6

--- a/solution.py
+++ b/solution.py
@@ -200,7 +200,7 @@
             one = delta[(b - first) * set_count : (b - first + 1) * set_count]
             if at:
                 one = one + sofar_ref[b * set_count : (b + 1) * set_count, :]
-            carry = rho * carry + weight_ref[b] * one
+            carry = rho * carry + jnp.broadcast_to(weight_ref[0:1, b : b + 1], one.shape) * one
             quad = quad + (1.0 if b == 0 else 1.0 - rho * rho) * (carry * carry)
     margin = IM_SCALE * jnp.sqrt(1.0 + quad)
     spread = jnp.tanh(set_value / VALUE_SCALE)
@@ -223,10 +223,11 @@
     base = DATES * (set_count + NB)
     sums = pieces(jnp.concatenate(sums, axis=1), 3)
     width = 2 * DATES * set_count
-    for i, piece in enumerate(sums):
-        row, lane = base + i // 2 * NB, i % 2 * width
-        out_ref[row : row + NB, lane : lane + width] = piece
-    out_ref[base + NB : base + 2 * NB, width : 2 * width] = jnp.zeros((NB, width), BF16)
+    out_ref[base : base + NB, 0:width] = sums[0]
+    out_ref[base : base + NB, width : 2 * width] = sums[1]
+    half = NB // 2
+    out_ref[base + NB : base + NB + half, 0:width] = sums[2][0:half]
+    out_ref[base + NB : base + NB + half, width : 2 * width] = sums[2][half:NB]
 
 
 def fit_kernel(groups, set_count, value_ref, *refs):
@@ -236,8 +237,10 @@
     ridge = RIDGE * paths_all
     width = 2 * DATES * set_count
     base = DATES * (set_count + NB)
-    total = sum(p[base : base + 2 * NB, :].astype(F32) for p in parts)
-    total = total[0:NB, 0:width] + total[0:NB, width : 2 * width] + total[NB : 2 * NB, 0:width]
+    rest = sum(p[base + NB : base + NB + NB // 2, :].astype(F32) for p in parts)
+    total = sum(p[base : base + NB, :].astype(F32) for p in parts)
+    total = total[:, 0:width] + total[:, width : 2 * width]
+    total = total + jnp.concatenate([rest[:, 0:width], rest[:, width : 2 * width]], axis=0)
     shape = (NB, width)
     row = iota(shape, 0)
     shift = 2 * set_count
@@ -385,19 +388,19 @@
         last, held = got[at:], owners - at
     else:
         last, held = [lax.all_to_all(packed[0], "trades", split_axis=0, concat_axis=0, tiled=True)], owners
-    packet = (DATES * (set_count + NB) + 2 * NB, paths)
+    packet = (DATES * (set_count + NB) + NB + NB // 2, paths)
     mine, value = pl.pallas_call(
         lambda *refs: owner_kernel(owners, at, cap, set_count, *refs),
         out_shape=[
             pltpu.VMEM(packet, BF16),
             pltpu.VMEM((DATES, set_count, paths), F32),
         ],
-        in_specs=[smem()] + vmem(1 + len(sofar) + len(last)),
+        in_specs=vmem(2 + len(sofar) + len(last)),
         out_specs=vmem(2),
         scratch_shapes=scratch(held),
         compiler_params=params(),
         name="owner",
-    )(risk_weights, states, *sofar, *last)
+    )(near(risk_weights.reshape(1, B)), states, *sofar, *last)
     parts = [near(mine)] + [meet(mine, "paths", k) for k in range(1, groups)]
     fitted_margin, exposure = pl.pallas_call(
         lambda *refs: fit_kernel(groups, set_count, *refs),

time: 37.8 us -> 36.9 us (0.976)
  Pallas kernels: 12.6 us -> 12 us
    pallas_call x1, Pallas kernels: 3.83 us -> 3.29 us  [on_device(): pl.pallas_call(lambda *refs: owner_kernel(owners, at, cap, set_count, *re...]
  transfers between devices with their start and end apart: 10 -> 10, of which waited for: 5 -> 5; matrix products, arithmetic and copies ran while one was open for 0% -> 0% of each run, Pallas kernels for 12% -> 13%
where the time goes in v7:
time: 36.9 us; the launch traced here: 36.8 us
  starting transfers between devices  13.2 us (36%)
  Pallas kernels  12 us (33%)
  waiting for transfers between devices  9.76 us (26%)
  local copies, waits for them, and re-layouts  1.05 us (3%)
  between operations  0.68 us (2%)
    ppermute x10, starting transfers between devices, meet(): return near(lax.ppermute(x, axis, [(i, i ^ k) for i in range(n)]))  13.2 us
    ppermute x10, waiting for transfers between devices, meet(): return near(lax.ppermute(x, axis, [(i, i ^ k) for i in range(n)]))  9.76 us
    pallas_call x1, Pallas kernels, on_device(): pl.pallas_call(lambda *refs: add_kernel(cap, set_count, *refs), out_shape...  4.62 us
    pallas_call x1, Pallas kernels, on_device(): pl.pallas_call(lambda *refs: owner_kernel(owners, at, cap, set_count, *re...  3.29 us
    pallas_call x1, Pallas kernels, on_device(): pl.pallas_call(lambda *refs: pack_kernel(owners, order, cap, set_count, *...  2.47 us
    pallas_call x1, Pallas kernels, on_device(): pl.pallas_call(lambda *refs: fit_kernel(groups, set_count, *refs), out_sh...  1.67 us
    unnamed x4, local copies, waits for them, and re-layouts  1.05 us
  transfers between devices with their start and end apart: 10, of which 5 were waited for; matrix products, arithmetic and copies ran while one was open for 0% of the time, Pallas kernels for 13%

profile of v7, /device:TPU:0, one launch (start us, length us, event | category | flops | bytes accessed | tf_op | source)
XLA Modules:
  0.0 36.8 jit_solution(11859995067317828525)
XLA Ops:
  0.6 0.0 copy-start.1
  0.6 2.5 %pack.1 = (bf16[168,512]{1,0:T(8,128)(2,1)S(1)}, bf16[168,512]{1,0:T(8,128)(2,1)S(1)}, bf16[168,512]{1,0:T(8,128)(2,1)S(1)}, bf16[168,512]{1,0:T(8,128)(2,1)S(1)...) custom-call(s32[1]{0:T(128)} %bitcast.2.refs_0_, ...), custom_call_target="tpu_custom_call" | custom-call | tf_op jit(solution)/shard_map/pack/pallas_call | solution.py:350
  3.1 3.0 %collective-permute-start = (bf16[168,512]{1,0:T(8,128)(2,1)S(1)}, bf16[168,512]{1,0:T(8,128)(2,1)S(1)}, u32[]{:S(2)}, u32[]{:S(2)}) collective-permute-start(bf16[168,512]{1,0:T(8,128)(2,1)S(1)} %get-tuple-element.13), channel_id=1, source_target_pairs={{0,8},{4,12},{8,0},{12,4},{16,24},{20,28},{24,16},{28,20},{1,9},{5... | collective-permute-start | bytes 516104 | tf_op jit(solution)/shard_map/ppermute | solution.py:319
  6.1 1.5 %collective-permute-start.1 = (bf16[168,512]{1,0:T(8,128)(2,1)S(1)}, bf16[168,512]{1,0:T(8,128)(2,1)S(1)}, u32[]{:S(2)}, u32[]{:S(2)}) collective-permute-start(bf16[168,512]{1,0:T(8,128)(2,1)S(1)} %get-tuple-element.14), channel_id=1, source_target_pairs={{0,16},{4,20},{8,24},{12,28},{16,0},{20,4},{24,8},{28,12},{1,17},{... | collective-permute-start | bytes 516104 | tf_op jit(solution)/shard_map/ppermute | solution.py:319
  7.7 0.0 collective-permute-start.2
  7.7 0.6 %collective-permute-start.3 = (bf16[168,512]{1,0:T(8,128)(2,1)S(1)}, bf16[168,512]{1,0:T(8,128)(2,1)S(1)}, u32[]{:S(2)}, u32[]{:S(2)}) collective-permute-start(bf16[168,512]{1,0:T(8,128)(2,1)S(1)} %get-tuple-element.16), channel_id=1, source_target_pairs={{0,4},{4,0},{8,12},{12,8},{16,20},{20,16},{24,28},{28,24},{1,5},{5... | collective-permute-start | bytes 516104 | tf_op jit(solution)/shard_map/ppermute | solution.py:319
  8.3 0.0 collective-permute-start.4
  8.3 2.5 %collective-permute-done.refs_2_ = bf16[168,512]{1,0:T(8,128)(2,1)S(1)} collective-permute-done((bf16[168,512]{1,0:T(8,128)(2,1)S(1)}, bf16[168,512]{1,0:T(8,128)(2,1)S(1)}, u32[]{:S(2)}, u32[]{:S(2)}) %collective-permute-start) | collective-permute-done | bytes 172064 | tf_op jit(solution)/shard_map/ppermute | solution.py:319
  10.8 3.6 %collective-permute-start.5 = (bf16[168,512]{1,0:T(8,128)(2,1)S(1)}, bf16[168,512]{1,0:T(8,128)(2,1)S(1)}, u32[]{:S(2)}, u32[]{:S(2)}) collective-permute-start(bf16[168,512]{1,0:T(8,128)(2,1)S(1)} %get-tuple-element.18), channel_id=1, source_target_pairs={{0,24},{4,28},{8,16},{12,20},{16,8},{20,12},{24,0},{28,4},{1,25},{... | collective-permute-start | bytes 516104 | tf_op jit(solution)/shard_map/ppermute | solution.py:319
  14.4 0.0 collective-permute-done.1.refs_3_
  14.4 0.0 collective-permute-start.6
  14.4 0.1 collective-permute-done.2.refs_4_
  14.4 0.0 collective-permute-done.3.refs_5_
  14.5 0.0 copy-start
  14.5 1.0 %copy-done = bf16[2,256,512]{2,1,0:T(8,128)(2,1)S(1)} copy-done((bf16[2,256,512]{2,1,0:T(8,128)(2,1)S(1)}, bf16[2,256,512]{2,1,0:T(8,128)(2,1)}, u32[]{:S(2)}) %copy-start) | copy-done | bytes 524312
  15.5 4.6 %add.1.refs_2_ = f32[1312,512]{1,0:T(8,128)S(1)} custom-call(bf16[512,512]{1,0:T(8,128)(2,1)S(1)} %bitcast.5, bf16[168,512]{1,0:T(8,128)(2,1)S(1)} %get-tuple-element.12.refs_1_, bf16[168,512]{1,0:T(8,128)(2,1)S(1)} %collective-permute-done.refs_2_, bf16[168,512]{1,0:T(8,128)(2,1)S(1)} %collective-permute-done.1.refs_3_, ...), custom_call_target="tpu_custom_call" | custom-call | tf_op jit(solution)/shard_map/add/pallas_call | solution.py:378
  20.1 1.9 %collective-permute-done.4.refs_3_ = bf16[168,512]{1,0:T(8,128)(2,1)S(1)} collective-permute-done((bf16[168,512]{1,0:T(8,128)(2,1)S(1)}, bf16[168,512]{1,0:T(8,128)(2,1)S(1)}, u32[]{:S(2)}, u32[]{:S(2)}) %collective-permute-start.4) | collective-permute-done | bytes 172064 | tf_op jit(solution)/shard_map/ppermute | solution.py:319
  22.1 0.0 collective-permute-done.5.refs_4_
  22.1 0.0 collective-permute-done.6.refs_5_
  22.1 0.0 copy-done.1
  22.1 3.3 %owner.1 = (bf16[120,256]{1,0:T(8,128)(2,1)S(1)}, f32[2,32,256]{2,1,0:T(8,128)S(1)}) custom-call(f32[1,40]{1,0:T(1,128)S(1)} %bitcast.7, bf16[512,512]{1,0:T(8,128)(2,1)S(1)} %bitcast.6, f32[1312,512]{1,0:T(8,128)S(1)} %add.1.refs_2_, bf16[168,512]{1,0:T(8,128)(2,1)S(1)} %collective-permute-done.4.refs_3_, ...), custom_call_target="tpu_custom_call" | custom-call | tf_op jit(solution)/shard_map/owner/pallas_call | solution.py:392
  25.4 3.7 %collective-permute-start.9 = (bf16[120,256]{1,0:T(8,128)(2,1)S(1)}, bf16[120,256]{1,0:T(8,128)(2,1)S(1)}, u32[]{:S(2)}, u32[]{:S(2)}) collective-permute-start(bf16[120,256]{1,0:T(8,128)(2,1)S(1)} %get-tuple-element.21.refs_1_), channel_id=1, source_target_pairs={{0,3},{1,2},{2,1},{3,0},{4,7},{5,6},{6,5},{7,4},{8,11},{9,10},{10,... | collective-permute-start | bytes 184328 | tf_op jit(solution)/shard_map/ppermute | solution.py:319
  29.0 0.0 collective-permute-start.8
  29.0 0.8 %collective-permute-start.7 = (bf16[120,256]{1,0:T(8,128)(2,1)S(1)}, bf16[120,256]{1,0:T(8,128)(2,1)S(1)}, u32[]{:S(2)}, u32[]{:S(2)}) collective-permute-start(bf16[120,256]{1,0:T(8,128)(2,1)S(1)} %get-tuple-element.21.refs_1_), channel_id=1, source_target_pairs={{0,1},{1,0},{2,3},{3,2},{4,5},{5,4},{6,7},{7,6},{8,9},{9,8},{10,11... | collective-permute-start | bytes 184328 | tf_op jit(solution)/shard_map/ppermute | solution.py:319
  29.8 2.3 %collective-permute-done.9.refs_4_ = bf16[120,256]{1,0:T(8,128)(2,1)S(1)} collective-permute-done((bf16[120,256]{1,0:T(8,128)(2,1)S(1)}, bf16[120,256]{1,0:T(8,128)(2,1)S(1)}, u32[]{:S(2)}, u32[]{:S(2)}) %collective-permute-start.9) | collective-permute-done | bytes 61472 | tf_op jit(solution)/shard_map/ppermute | solution.py:319
  32.1 3.0 %collective-permute-done.8.refs_3_ = bf16[120,256]{1,0:T(8,128)(2,1)S(1)} collective-permute-done((bf16[120,256]{1,0:T(8,128)(2,1)S(1)}, bf16[120,256]{1,0:T(8,128)(2,1)S(1)}, u32[]{:S(2)}, u32[]{:S(2)}) %collective-permute-start.8) | collective-permute-done | bytes 61472 | tf_op jit(solution)/shard_map/ppermute | solution.py:319
  35.1 0.0 collective-permute-done.7.refs_2_
  35.1 1.7 %fit.1 = (f32[2,32,256]{2,1,0:T(8,128)}, f32[2,32]{1,0:T(2,128)}) custom-call(f32[2,32,256]{2,1,0:T(8,128)S(1)} %get-tuple-element.20.refs_0_, bf16[120,256]{1,0:T(8,128)(2,1)S(1)} %get-tuple-element.21.refs_1_, bf16[120,256]{1,0:T(8,128)(2,1)S(1)} %collective-permute-done.7.refs_2_, bf16[120,256]{1,0:T(8,128)(2,1)S(1)} %collective-permute-done.8.refs_3_, ...), custom_call_target="tpu_custom_call" | custom-call | tf_op jit(solution)/shard_map/fit/pallas_call | solution.py:405
Async XLA Ops:
  0.6 21.4 %copy-start.1 = (f32[40]{0:T(128)S(1)}, f32[40]{0:T(128)}, u32[]{:S(2)}) copy-start(f32[40]{0:T(128)} %param.13) | copy-start | bytes 484
  3.1 7.6 %collective-permute-start = (bf16[168,512]{1,0:T(8,128)(2,1)S(1)}, bf16[168,512]{1,0:T(8,128)(2,1)S(1)}, u32[]{:S(2)}, u32[]{:S(2)}) collective-permute-start(bf16[168,512]{1,0:T(8,128)(2,1)S(1)} %get-tuple-element.13), channel_id=1, source_target_pairs={{0,8},{4,12},{8,0},{12,4},{16,24},{20,28},{24,16},{28,20},{1,9},{5... | collective-permute-start | bytes 516104 | tf_op jit(solution)/shard_map/ppermute | solution.py:319
  6.1 8.2 %collective-permute-start.1 = (bf16[168,512]{1,0:T(8,128)(2,1)S(1)}, bf16[168,512]{1,0:T(8,128)(2,1)S(1)}, u32[]{:S(2)}, u32[]{:S(2)}) collective-permute-start(bf16[168,512]{1,0:T(8,128)(2,1)S(1)} %get-tuple-element.14), channel_id=1, source_target_pairs={{0,16},{4,20},{8,24},{12,28},{16,0},{20,4},{24,8},{28,12},{1,17},{... | collective-permute-start | bytes 516104 | tf_op jit(solution)/shard_map/ppermute | solution.py:319
  7.7 6.8 %collective-permute-start.2 = (bf16[168,512]{1,0:T(8,128)(2,1)S(1)}, bf16[168,512]{1,0:T(8,128)(2,1)S(1)}, u32[]{:S(2)}, u32[]{:S(2)}) collective-permute-start(bf16[168,512]{1,0:T(8,128)(2,1)S(1)} %get-tuple-element.15), channel_id=1, source_target_pairs={{0,12},{4,8},{8,4},{12,0},{16,28},{20,24},{24,20},{28,16},{1,13},{... | collective-permute-start | bytes 516104 | tf_op jit(solution)/shard_map/ppermute | solution.py:319
  7.7 6.8 %collective-permute-start.3 = (bf16[168,512]{1,0:T(8,128)(2,1)S(1)}, bf16[168,512]{1,0:T(8,128)(2,1)S(1)}, u32[]{:S(2)}, u32[]{:S(2)}) collective-permute-start(bf16[168,512]{1,0:T(8,128)(2,1)S(1)} %get-tuple-element.16), channel_id=1, source_target_pairs={{0,4},{4,0},{8,12},{12,8},{16,20},{20,16},{24,28},{28,24},{1,5},{5... | collective-permute-start | bytes 516104 | tf_op jit(solution)/shard_map/ppermute | solution.py:319
  8.3 13.8 %collective-permute-start.4 = (bf16[168,512]{1,0:T(8,128)(2,1)S(1)}, bf16[168,512]{1,0:T(8,128)(2,1)S(1)}, u32[]{:S(2)}, u32[]{:S(2)}) collective-permute-start(bf16[168,512]{1,0:T(8,128)(2,1)S(1)} %get-tuple-element.17), channel_id=1, source_target_pairs={{0,20},{4,16},{8,28},{12,24},{16,4},{20,0},{24,12},{28,8},{1,21},{... | collective-permute-start | bytes 516104 | tf_op jit(solution)/shard_map/ppermute | solution.py:319
  10.8 11.3 %collective-permute-start.5 = (bf16[168,512]{1,0:T(8,128)(2,1)S(1)}, bf16[168,512]{1,0:T(8,128)(2,1)S(1)}, u32[]{:S(2)}, u32[]{:S(2)}) collective-permute-start(bf16[168,512]{1,0:T(8,128)(2,1)S(1)} %get-tuple-element.18), channel_id=1, source_target_pairs={{0,24},{4,28},{8,16},{12,20},{16,8},{20,12},{24,0},{28,4},{1,25},{... | collective-permute-start | bytes 516104 | tf_op jit(solution)/shard_map/ppermute | solution.py:319
  14.4 7.7 %collective-permute-start.6 = (bf16[168,512]{1,0:T(8,128)(2,1)S(1)}, bf16[168,512]{1,0:T(8,128)(2,1)S(1)}, u32[]{:S(2)}, u32[]{:S(2)}) collective-permute-start(bf16[168,512]{1,0:T(8,128)(2,1)S(1)} %get-tuple-element.19), channel_id=1, source_target_pairs={{0,28},{4,24},{8,20},{12,16},{16,12},{20,8},{24,4},{28,0},{1,29},{... | collective-permute-start | bytes 516104 | tf_op jit(solution)/shard_map/ppermute | solution.py:319
  14.5 1.0 %copy-start = (bf16[2,256,512]{2,1,0:T(8,128)(2,1)S(1)}, bf16[2,256,512]{2,1,0:T(8,128)(2,1)}, u32[]{:S(2)}) copy-start(bf16[2,256,512]{2,1,0:T(8,128)(2,1)} %param.7) | copy-start | bytes 1572868
  25.4 6.7 %collective-permute-start.9 = (bf16[120,256]{1,0:T(8,128)(2,1)S(1)}, bf16[120,256]{1,0:T(8,128)(2,1)S(1)}, u32[]{:S(2)}, u32[]{:S(2)}) collective-permute-start(bf16[120,256]{1,0:T(8,128)(2,1)S(1)} %get-tuple-element.21.refs_1_), channel_id=1, source_target_pairs={{0,3},{1,2},{2,1},{3,0},{4,7},{5,6},{6,5},{7,4},{8,11},{9,10},{10,... | collective-permute-start | bytes 184328 | tf_op jit(solution)/shard_map/ppermute | solution.py:319
  29.0 6.1 %collective-permute-start.8 = (bf16[120,256]{1,0:T(8,128)(2,1)S(1)}, bf16[120,256]{1,0:T(8,128)(2,1)S(1)}, u32[]{:S(2)}, u32[]{:S(2)}) collective-permute-start(bf16[120,256]{1,0:T(8,128)(2,1)S(1)} %get-tuple-element.21.refs_1_), channel_id=1, source_target_pairs={{0,2},{1,3},{2,0},{3,1},{4,6},{5,7},{6,4},{7,5},{8,10},{9,11},{10,... | collective-permute-start | bytes 184328 | tf_op jit(solution)/shard_map/ppermute | solution.py:319
  29.0 6.1 %collective-permute-start.7 = (bf16[120,256]{1,0:T(8,128)(2,1)S(1)}, bf16[120,256]{1,0:T(8,128)(2,1)S(1)}, u32[]{:S(2)}, u32[]{:S(2)}) collective-permute-start(bf16[120,256]{1,0:T(8,128)(2,1)S(1)} %get-tuple-element.21.refs_1_), channel_id=1, source_target_pairs={{0,1},{1,0},{2,3},{3,2},{4,5},{5,4},{6,7},{7,6},{8,9},{9,8},{10,11... | collective-permute-start | bytes 184328 | tf_op jit(solution)/shard_map/ppermute | solution.py:319

commit v8 on v7

--- a/solution.py
+++ b/solution.py
@@ -14,7 +14,7 @@
 META = 8
 EARLY = 5
 ORDER = (0, 2, 4, 3, 1, 5, 6, 7)
-STEP = 4
+STEP = 5
 HALF = 256
 
 CORR_LEN = 8.0

time: 36.9 us -> 36.9 us (level)
  no operation moved by 1% of the time
where the time goes in v8:
time: 36.9 us; the launch traced here: 36.7 us
  starting transfers between devices  13.2 us (36%)
  Pallas kernels  12 us (33%)
  waiting for transfers between devices  9.78 us (27%)
  local copies, waits for them, and re-layouts  1.05 us (3%)
  between operations  0.68 us (2%)
    ppermute x10, starting transfers between devices, meet(): return near(lax.ppermute(x, axis, [(i, i ^ k) for i in range(n)]))  13.2 us
    ppermute x10, waiting for transfers between devices, meet(): return near(lax.ppermute(x, axis, [(i, i ^ k) for i in range(n)]))  9.78 us
    pallas_call x1, Pallas kernels, on_device(): pl.pallas_call(lambda *refs: add_kernel(cap, set_count, *refs), out_shape...  4.61 us
    pallas_call x1, Pallas kernels, on_device(): pl.pallas_call(lambda *refs: owner_kernel(owners, at, cap, set_count, *re...  3.25 us
    pallas_call x1, Pallas kernels, on_device(): pl.pallas_call(lambda *refs: pack_kernel(owners, order, cap, set_count, *...  2.47 us
    pallas_call x1, Pallas kernels, on_device(): pl.pallas_call(lambda *refs: fit_kernel(groups, set_count, *refs), out_sh...  1.67 us
    unnamed x4, local copies, waits for them, and re-layouts  1.05 us
  transfers between devices with their start and end apart: 10, of which 5 were waited for; matrix products, arithmetic and copies ran while one was open for 0% of the time, Pallas kernels for 13%

profile of v8, /device:TPU:0, one launch (start us, length us, event | category | flops | bytes accessed | tf_op | source)
XLA Modules:
  0.0 36.7 jit_solution(17036198821122143450)
XLA Ops:
  0.6 0.0 copy-start.1
  0.6 2.5 %pack.1 = (bf16[168,512]{1,0:T(8,128)(2,1)S(1)}, bf16[168,512]{1,0:T(8,128)(2,1)S(1)}, bf16[168,512]{1,0:T(8,128)(2,1)S(1)}, bf16[168,512]{1,0:T(8,128)(2,1)S(1)...) custom-call(s32[1]{0:T(128)} %bitcast.2.refs_0_, ...), custom_call_target="tpu_custom_call" | custom-call | tf_op jit(solution)/shard_map/pack/pallas_call | solution.py:350
  3.1 3.0 %collective-permute-start = (bf16[168,512]{1,0:T(8,128)(2,1)S(1)}, bf16[168,512]{1,0:T(8,128)(2,1)S(1)}, u32[]{:S(2)}, u32[]{:S(2)}) collective-permute-start(bf16[168,512]{1,0:T(8,128)(2,1)S(1)} %get-tuple-element.13), channel_id=1, source_target_pairs={{0,8},{4,12},{8,0},{12,4},{16,24},{20,28},{24,16},{28,20},{1,9},{5... | collective-permute-start | bytes 516104 | tf_op jit(solution)/shard_map/ppermute | solution.py:319
  6.1 1.5 %collective-permute-start.1 = (bf16[168,512]{1,0:T(8,128)(2,1)S(1)}, bf16[168,512]{1,0:T(8,128)(2,1)S(1)}, u32[]{:S(2)}, u32[]{:S(2)}) collective-permute-start(bf16[168,512]{1,0:T(8,128)(2,1)S(1)} %get-tuple-element.14), channel_id=1, source_target_pairs={{0,16},{4,20},{8,24},{12,28},{16,0},{20,4},{24,8},{28,12},{1,17},{... | collective-permute-start | bytes 516104 | tf_op jit(solution)/shard_map/ppermute | solution.py:319
  7.7 0.0 collective-permute-start.2
  7.7 0.6 %collective-permute-start.3 = (bf16[168,512]{1,0:T(8,128)(2,1)S(1)}, bf16[168,512]{1,0:T(8,128)(2,1)S(1)}, u32[]{:S(2)}, u32[]{:S(2)}) collective-permute-start(bf16[168,512]{1,0:T(8,128)(2,1)S(1)} %get-tuple-element.16), channel_id=1, source_target_pairs={{0,4},{4,0},{8,12},{12,8},{16,20},{20,16},{24,28},{28,24},{1,5},{5... | collective-permute-start | bytes 516104 | tf_op jit(solution)/shard_map/ppermute | solution.py:319
  8.3 0.0 collective-permute-start.4
  8.3 2.5 %collective-permute-done.refs_2_ = bf16[168,512]{1,0:T(8,128)(2,1)S(1)} collective-permute-done((bf16[168,512]{1,0:T(8,128)(2,1)S(1)}, bf16[168,512]{1,0:T(8,128)(2,1)S(1)}, u32[]{:S(2)}, u32[]{:S(2)}) %collective-permute-start) | collective-permute-done | bytes 172064 | tf_op jit(solution)/shard_map/ppermute | solution.py:319
  10.8 3.6 %collective-permute-start.5 = (bf16[168,512]{1,0:T(8,128)(2,1)S(1)}, bf16[168,512]{1,0:T(8,128)(2,1)S(1)}, u32[]{:S(2)}, u32[]{:S(2)}) collective-permute-start(bf16[168,512]{1,0:T(8,128)(2,1)S(1)} %get-tuple-element.18), channel_id=1, source_target_pairs={{0,24},{4,28},{8,16},{12,20},{16,8},{20,12},{24,0},{28,4},{1,25},{... | collective-permute-start | bytes 516104 | tf_op jit(solution)/shard_map/ppermute | solution.py:319
  14.4 0.0 collective-permute-done.1.refs_3_
  14.4 0.0 collective-permute-start.6
  14.4 0.1 collective-permute-done.2.refs_4_
  14.4 0.0 collective-permute-done.3.refs_5_
  14.5 0.0 copy-start
  14.5 1.0 %copy-done = bf16[2,256,512]{2,1,0:T(8,128)(2,1)S(1)} copy-done((bf16[2,256,512]{2,1,0:T(8,128)(2,1)S(1)}, bf16[2,256,512]{2,1,0:T(8,128)(2,1)}, u32[]{:S(2)}) %copy-start) | copy-done | bytes 524312
  15.5 4.6 %add.1.refs_2_ = f32[1312,512]{1,0:T(8,128)S(1)} custom-call(bf16[512,512]{1,0:T(8,128)(2,1)S(1)} %bitcast.5, bf16[168,512]{1,0:T(8,128)(2,1)S(1)} %get-tuple-element.12.refs_1_, bf16[168,512]{1,0:T(8,128)(2,1)S(1)} %collective-permute-done.refs_2_, bf16[168,512]{1,0:T(8,128)(2,1)S(1)} %collective-permute-done.1.refs_3_, ...), custom_call_target="tpu_custom_call" | custom-call | tf_op jit(solution)/shard_map/add/pallas_call | solution.py:378
  20.1 2.0 %collective-permute-done.4.refs_3_ = bf16[168,512]{1,0:T(8,128)(2,1)S(1)} collective-permute-done((bf16[168,512]{1,0:T(8,128)(2,1)S(1)}, bf16[168,512]{1,0:T(8,128)(2,1)S(1)}, u32[]{:S(2)}, u32[]{:S(2)}) %collective-permute-start.4) | collective-permute-done | bytes 172064 | tf_op jit(solution)/shard_map/ppermute | solution.py:319
  22.1 0.0 collective-permute-done.5.refs_4_
  22.1 0.0 collective-permute-done.6.refs_5_
  22.1 0.0 copy-done.1
  22.1 3.2 %owner.1 = (bf16[120,256]{1,0:T(8,128)(2,1)S(1)}, f32[2,32,256]{2,1,0:T(8,128)S(1)}) custom-call(f32[1,40]{1,0:T(1,128)S(1)} %bitcast.7, bf16[512,512]{1,0:T(8,128)(2,1)S(1)} %bitcast.6, f32[1312,512]{1,0:T(8,128)S(1)} %add.1.refs_2_, bf16[168,512]{1,0:T(8,128)(2,1)S(1)} %collective-permute-done.4.refs_3_, ...), custom_call_target="tpu_custom_call" | custom-call | tf_op jit(solution)/shard_map/owner/pallas_call | solution.py:392
  25.3 3.7 %collective-permute-start.9 = (bf16[120,256]{1,0:T(8,128)(2,1)S(1)}, bf16[120,256]{1,0:T(8,128)(2,1)S(1)}, u32[]{:S(2)}, u32[]{:S(2)}) collective-permute-start(bf16[120,256]{1,0:T(8,128)(2,1)S(1)} %get-tuple-element.21.refs_1_), channel_id=1, source_target_pairs={{0,3},{1,2},{2,1},{3,0},{4,7},{5,6},{6,5},{7,4},{8,11},{9,10},{10,... | collective-permute-start | bytes 184328 | tf_op jit(solution)/shard_map/ppermute | solution.py:319
  29.0 0.0 collective-permute-start.8
  29.0 0.8 %collective-permute-start.7 = (bf16[120,256]{1,0:T(8,128)(2,1)S(1)}, bf16[120,256]{1,0:T(8,128)(2,1)S(1)}, u32[]{:S(2)}, u32[]{:S(2)}) collective-permute-start(bf16[120,256]{1,0:T(8,128)(2,1)S(1)} %get-tuple-element.21.refs_1_), channel_id=1, source_target_pairs={{0,1},{1,0},{2,3},{3,2},{4,5},{5,4},{6,7},{7,6},{8,9},{9,8},{10,11... | collective-permute-start | bytes 184328 | tf_op jit(solution)/shard_map/ppermute | solution.py:319
  29.8 2.3 %collective-permute-done.9.refs_4_ = bf16[120,256]{1,0:T(8,128)(2,1)S(1)} collective-permute-done((bf16[120,256]{1,0:T(8,128)(2,1)S(1)}, bf16[120,256]{1,0:T(8,128)(2,1)S(1)}, u32[]{:S(2)}, u32[]{:S(2)}) %collective-permute-start.9) | collective-permute-done | bytes 61472 | tf_op jit(solution)/shard_map/ppermute | solution.py:319
  32.1 3.0 %collective-permute-done.8.refs_3_ = bf16[120,256]{1,0:T(8,128)(2,1)S(1)} collective-permute-done((bf16[120,256]{1,0:T(8,128)(2,1)S(1)}, bf16[120,256]{1,0:T(8,128)(2,1)S(1)}, u32[]{:S(2)}, u32[]{:S(2)}) %collective-permute-start.8) | collective-permute-done | bytes 61472 | tf_op jit(solution)/shard_map/ppermute | solution.py:319
  35.1 0.0 collective-permute-done.7.refs_2_
  35.1 1.7 %fit.1 = (f32[2,32,256]{2,1,0:T(8,128)}, f32[2,32]{1,0:T(2,128)}) custom-call(f32[2,32,256]{2,1,0:T(8,128)S(1)} %get-tuple-element.20.refs_0_, bf16[120,256]{1,0:T(8,128)(2,1)S(1)} %get-tuple-element.21.refs_1_, bf16[120,256]{1,0:T(8,128)(2,1)S(1)} %collective-permute-done.7.refs_2_, bf16[120,256]{1,0:T(8,128)(2,1)S(1)} %collective-permute-done.8.refs_3_, ...), custom_call_target="tpu_custom_call" | custom-call | tf_op jit(solution)/shard_map/fit/pallas_call | solution.py:405
Async XLA Ops:
  0.6 21.4 %copy-start.1 = (f32[40]{0:T(128)S(1)}, f32[40]{0:T(128)}, u32[]{:S(2)}) copy-start(f32[40]{0:T(128)} %param.13) | copy-start | bytes 484
  3.1 7.6 %collective-permute-start = (bf16[168,512]{1,0:T(8,128)(2,1)S(1)}, bf16[168,512]{1,0:T(8,128)(2,1)S(1)}, u32[]{:S(2)}, u32[]{:S(2)}) collective-permute-start(bf16[168,512]{1,0:T(8,128)(2,1)S(1)} %get-tuple-element.13), channel_id=1, source_target_pairs={{0,8},{4,12},{8,0},{12,4},{16,24},{20,28},{24,16},{28,20},{1,9},{5... | collective-permute-start | bytes 516104 | tf_op jit(solution)/shard_map/ppermute | solution.py:319
  6.1 8.2 %collective-permute-start.1 = (bf16[168,512]{1,0:T(8,128)(2,1)S(1)}, bf16[168,512]{1,0:T(8,128)(2,1)S(1)}, u32[]{:S(2)}, u32[]{:S(2)}) collective-permute-start(bf16[168,512]{1,0:T(8,128)(2,1)S(1)} %get-tuple-element.14), channel_id=1, source_target_pairs={{0,16},{4,20},{8,24},{12,28},{16,0},{20,4},{24,8},{28,12},{1,17},{... | collective-permute-start | bytes 516104 | tf_op jit(solution)/shard_map/ppermute | solution.py:319
  7.7 6.8 %collective-permute-start.2 = (bf16[168,512]{1,0:T(8,128)(2,1)S(1)}, bf16[168,512]{1,0:T(8,128)(2,1)S(1)}, u32[]{:S(2)}, u32[]{:S(2)}) collective-permute-start(bf16[168,512]{1,0:T(8,128)(2,1)S(1)} %get-tuple-element.15), channel_id=1, source_target_pairs={{0,12},{4,8},{8,4},{12,0},{16,28},{20,24},{24,20},{28,16},{1,13},{... | collective-permute-start | bytes 516104 | tf_op jit(solution)/shard_map/ppermute | solution.py:319
  7.7 6.8 %collective-permute-start.3 = (bf16[168,512]{1,0:T(8,128)(2,1)S(1)}, bf16[168,512]{1,0:T(8,128)(2,1)S(1)}, u32[]{:S(2)}, u32[]{:S(2)}) collective-permute-start(bf16[168,512]{1,0:T(8,128)(2,1)S(1)} %get-tuple-element.16), channel_id=1, source_target_pairs={{0,4},{4,0},{8,12},{12,8},{16,20},{20,16},{24,28},{28,24},{1,5},{5... | collective-permute-start | bytes 516104 | tf_op jit(solution)/shard_map/ppermute | solution.py:319
  8.3 13.8 %collective-permute-start.4 = (bf16[168,512]{1,0:T(8,128)(2,1)S(1)}, bf16[168,512]{1,0:T(8,128)(2,1)S(1)}, u32[]{:S(2)}, u32[]{:S(2)}) collective-permute-start(bf16[168,512]{1,0:T(8,128)(2,1)S(1)} %get-tuple-element.17), channel_id=1, source_target_pairs={{0,20},{4,16},{8,28},{12,24},{16,4},{20,0},{24,12},{28,8},{1,21},{... | collective-permute-start | bytes 516104 | tf_op jit(solution)/shard_map/ppermute | solution.py:319
  10.8 11.3 %collective-permute-start.5 = (bf16[168,512]{1,0:T(8,128)(2,1)S(1)}, bf16[168,512]{1,0:T(8,128)(2,1)S(1)}, u32[]{:S(2)}, u32[]{:S(2)}) collective-permute-start(bf16[168,512]{1,0:T(8,128)(2,1)S(1)} %get-tuple-element.18), channel_id=1, source_target_pairs={{0,24},{4,28},{8,16},{12,20},{16,8},{20,12},{24,0},{28,4},{1,25},{... | collective-permute-start | bytes 516104 | tf_op jit(solution)/shard_map/ppermute | solution.py:319
  14.4 7.7 %collective-permute-start.6 = (bf16[168,512]{1,0:T(8,128)(2,1)S(1)}, bf16[168,512]{1,0:T(8,128)(2,1)S(1)}, u32[]{:S(2)}, u32[]{:S(2)}) collective-permute-start(bf16[168,512]{1,0:T(8,128)(2,1)S(1)} %get-tuple-element.19), channel_id=1, source_target_pairs={{0,28},{4,24},{8,20},{12,16},{16,12},{20,8},{24,4},{28,0},{1,29},{... | collective-permute-start | bytes 516104 | tf_op jit(solution)/shard_map/ppermute | solution.py:319
  14.5 1.0 %copy-start = (bf16[2,256,512]{2,1,0:T(8,128)(2,1)S(1)}, bf16[2,256,512]{2,1,0:T(8,128)(2,1)}, u32[]{:S(2)}) copy-start(bf16[2,256,512]{2,1,0:T(8,128)(2,1)} %param.7) | copy-start | bytes 1572868
  25.3 6.7 %collective-permute-start.9 = (bf16[120,256]{1,0:T(8,128)(2,1)S(1)}, bf16[120,256]{1,0:T(8,128)(2,1)S(1)}, u32[]{:S(2)}, u32[]{:S(2)}) collective-permute-start(bf16[120,256]{1,0:T(8,128)(2,1)S(1)} %get-tuple-element.21.refs_1_), channel_id=1, source_target_pairs={{0,3},{1,2},{2,1},{3,0},{4,7},{5,6},{6,5},{7,4},{8,11},{9,10},{10,... | collective-permute-start | bytes 184328 | tf_op jit(solution)/shard_map/ppermute | solution.py:319
  29.0 6.1 %collective-permute-start.8 = (bf16[120,256]{1,0:T(8,128)(2,1)S(1)}, bf16[120,256]{1,0:T(8,128)(2,1)S(1)}, u32[]{:S(2)}, u32[]{:S(2)}) collective-permute-start(bf16[120,256]{1,0:T(8,128)(2,1)S(1)} %get-tuple-element.21.refs_1_), channel_id=1, source_target_pairs={{0,2},{1,3},{2,0},{3,1},{4,6},{5,7},{6,4},{7,5},{8,10},{9,11},{10,... | collective-permute-start | bytes 184328 | tf_op jit(solution)/shard_map/ppermute | solution.py:319
  29.0 6.1 %collective-permute-start.7 = (bf16[120,256]{1,0:T(8,128)(2,1)S(1)}, bf16[120,256]{1,0:T(8,128)(2,1)S(1)}, u32[]{:S(2)}, u32[]{:S(2)}) collective-permute-start(bf16[120,256]{1,0:T(8,128)(2,1)S(1)} %get-tuple-element.21.refs_1_), channel_id=1, source_target_pairs={{0,1},{1,0},{2,3},{3,2},{4,5},{5,4},{6,7},{7,6},{8,9},{9,8},{10,11... | collective-permute-start | bytes 184328 | tf_op jit(solution)/shard_map/ppermute | solution.py:319
